TPU v7x, 32 devices: a whole 2x2x4 slice. The times are simulated.
32 devices in a mesh: groups: 2 (over y), ctx: 4 (over z), dp: 2 (over x), hp: 2 (over core).
Axes of the slice: x: 2, y: 2, z: 4, core: 2. Of those that a mesh axis runs over, the one named last changes fastest.
Arguments:
- residual: bfloat16 [8, 7168], P(('groups', 'dp'), 'ctx'), parts along dimension 0
- expert_out: bfloat16 [4, 2, 16, 7168], P(('groups', 'dp'), None, None, 'ctx'), parts along dimension 0, may hold values from -6 to 6
- combine_slot: int32 [8, 8], P(('groups', 'dp')), parts along dimension 0, may hold values from 0 to 31, as said below
- combine_gate: float32 [8, 8], P(('groups', 'dp')), parts along dimension 0, may hold values from 0.05 to 0.6
- attn_gain: float32 [7168], P('ctx'), may hold values from 0.1 to 1.9
- query_down: bfloat16 [7168, 1536], P('ctx'), may hold values from -0.0625 to 0.0625
- index_gate: bfloat16 [7168, 64], P('ctx'), may hold values from -0.0625 to 0.0625
- latent_gain: float32 [1536], replicated, may hold values from 0.1 to 1.9
- query_up: bfloat16 [1536, 128, 192], P(None, ('ctx', 'hp')), may hold values from -0.15625 to 0.15625
- key_absorb: bfloat16 [128, 128, 512], P(('ctx', 'hp')), may hold values from -0.5 to 0.5
- index_query: bfloat16 [1536, 64, 128], P(None, ('ctx', 'hp')), may hold values from -0.15625 to 0.15625
- value_up: bfloat16 [128, 512, 128], P(('ctx', 'hp')), may hold values from -0.25 to 0.25
- latent_cache: bfloat16 [8, 2048, 576], P(('groups', 'dp'), 'ctx'), parts along dimension 0
- index_keys: bfloat16 [8, 2048, 128], P(('groups', 'dp'), ('ctx', 'hp')), parts along dimension 0, may hold values from -6 to 6
- lengths: int32 [8], P(('groups', 'dp')), parts along dimension 0, may hold values from 512 to 2048, as said below
- block_list: int32 [8, 4], P(('groups', 'dp')), parts along dimension 0, may hold values from 0 to 31, as said below
Outputs:
- hidden: bfloat16 [8, 7168], P(('groups', 'dp'), 'ctx'), parts along dimension 0
- index_scores: float32 [8, 2048], P(('groups', 'dp'), ('ctx', 'hp')), parts along dimension 0
- attn_out: bfloat16 [8, 128, 128], P(('groups', 'dp'), ('ctx', 'hp')), parts along dimension 0
There are 2 independent parts, one for each index of `groups`. A program takes and returns all parts, laid end to end along the dimension named above; an argument that names none is the same for every part. Nothing has to cross between parts.
Inputs may be any that keep to these rules, and one draw needn't show every extreme that they name: `combine_slot`: within one group of 2 rows the slots are distinct; at most 16 of them fall in the range of one source s (s * 16 to s * 16 + 15), and in every group some source has exactly 16. `lengths`: each group of 2 rows holds a row of length exactly 2048. `block_list`: A row's entries are distinct blocks that hold some position below its length, and include block 0 and the block of position lengths - 1.
All inputs are finite; a program needn't handle non-finite values.
Results may differ from a plain program's by a relative error of at most 0.02.
Values may be sent and summed in bfloat16 or wider, within the bound.
No kernel may reach another device: no remote copies, remote signals or barrier semaphores. Data moves between devices by JAX's collectives and lax.ppermute only.
A program may use at most 64 MiB of HBM per device.

v0:
```python
import jax
import jax.numpy as jnp
from jax import lax
from jax.sharding import PartitionSpec as P

D = 7168
KVLORA = 512
ROPE = 64
NOPE = 128
IHEADS = 64
IDIM = 128
BLK = 64


epsilon = 1e-06
very_low = -1e30


def combined_all(array, axis, combine):
    everything = jax.tree.map(lambda part: lax.all_gather(part, axis), array)
    leading = jax.tree.map(lambda part: part[0], everything)

    def lap(k, so_far):
        return combine(so_far, jax.tree.map(lambda part: part[k], everything))

    return lax.fori_loop(1, lax.axis_size(axis), lap, leading)


def combine_rows(received, resid_part, combine_slot, combine_gate):
    flat = received.reshape(-1, received.shape[-1])
    picked = flat[combine_slot].astype(jnp.float32)
    routed = jnp.sum(combine_gate[:, :, None] * picked, axis=1)
    return (resid_part.astype(jnp.float32) + routed).astype(jnp.bfloat16)


def merge_pair(first, second):
    first_peak, first_total, first_out = first
    second_peak, second_total, second_out = second
    highest = jnp.maximum(first_peak, second_peak)
    first_factor = jnp.exp(first_peak - highest)
    second_factor = jnp.exp(second_peak - highest)
    total = first_total * first_factor + second_total * second_factor
    output = first_out * first_factor[..., None] + second_out * second_factor[..., None]
    return (highest, total, output)


def local(
    residual,
    expert_out,
    combine_slot,
    combine_gate,
    attn_gain,
    query_down,
    index_gate,
    latent_gain,
    query_up,
    key_absorb,
    index_query,
    value_up,
    latent_cache,
    index_keys,
    lengths,
    block_list,
):
    head_count = lax.axis_size("hp")
    ctx_index = lax.axis_index("ctx")
    head_index = lax.axis_index("hp")
    owned = value_up.shape[0]
    received = lax.all_to_all(expert_out, "dp", split_axis=1, concat_axis=0, tiled=True)
    hidden = combine_rows(received, residual, combine_slot, combine_gate)
    widened = hidden.astype(jnp.float32)
    squares = lax.psum(jnp.sum(widened * widened, axis=1), "ctx")
    normed = (widened * lax.rsqrt(squares / D + epsilon)[:, None] * attn_gain).astype(jnp.bfloat16)
    latent_part = jnp.dot(normed, query_down, preferred_element_type=jnp.float32)
    gate_part = jnp.dot(normed, index_gate, preferred_element_type=jnp.float32)
    latent_sum, gate_sum = lax.psum((latent_part, gate_part), "ctx")
    latent_scale = lax.rsqrt(jnp.mean(latent_sum * latent_sum, axis=-1, keepdims=True) + epsilon)
    latent = (latent_sum * latent_scale * latent_gain).astype(jnp.bfloat16)
    head_gate = gate_sum * IHEADS ** (-0.5)
    projected = jnp.einsum(
        "rq,qnd->rnd", latent, query_up, preferred_element_type=jnp.float32
    ).astype(jnp.bfloat16)
    absorbed = jnp.einsum(
        "rnk,nkc->rnc", projected[:, :, :NOPE], key_absorb, preferred_element_type=jnp.float32
    ).astype(jnp.bfloat16)
    queries = jnp.concatenate([absorbed, projected[:, :, NOPE:]], axis=-1)
    index_local = jnp.einsum(
        "rq,qnd->rnd", latent, index_query, preferred_element_type=jnp.float32
    ).astype(jnp.bfloat16)
    group_queries = lax.all_gather(queries, "ctx", axis=1, tiled=True)
    all_index = lax.all_gather(index_local, ("ctx", "hp"), axis=1, tiled=True)
    index_span = index_keys.shape[1]
    index_pos = (ctx_index * head_count + head_index) * index_span + jnp.arange(
        index_span, dtype=jnp.int32
    )
    index_logits = jnp.einsum(
        "rhd,rtd->rht", all_index, index_keys, preferred_element_type=jnp.float32
    )
    index_raw = jnp.sum(head_gate[:, :, None] * jnp.maximum(index_logits, 0.0), axis=1) * IDIM ** (
        -0.5
    )
    index_scores = jnp.where(index_pos[None, :] < lengths[:, None], index_raw, 0.0)
    span = latent_cache.shape[1]
    local_pos = ctx_index * span + jnp.arange(span, dtype=jnp.int32)
    chosen = jnp.any(block_list[:, :, None] == (local_pos // BLK)[None, None, :], axis=1)
    live = chosen & (local_pos[None, :] < lengths[:, None])
    logits = jnp.einsum(
        "rnc,rtc->rnt", group_queries, latent_cache, preferred_element_type=jnp.float32
    ) * (NOPE + ROPE) ** (-0.5)
    masked = jnp.where(live[:, None, :], logits, very_low)
    local_peak = jnp.max(masked, axis=-1)
    weights = jnp.where(live[:, None, :], jnp.exp(masked - local_peak[..., None]), 0.0)
    local_total = jnp.sum(weights, axis=-1)
    local_out = jnp.einsum(
        "rnt,rtc->rnc",
        weights.astype(jnp.bfloat16),
        latent_cache[:, :, :KVLORA],
        preferred_element_type=jnp.float32,
    )
    peak_all, total_all, out_all = combined_all(
        (local_peak, local_total, local_out), "ctx", merge_pair
    )
    first_head = ctx_index * owned
    total = lax.dynamic_slice_in_dim(total_all, first_head, owned, 1)
    merged = lax.dynamic_slice_in_dim(out_all, first_head, owned, 1)
    attended = (merged / total[..., None]).astype(jnp.bfloat16)
    attn_out = jnp.einsum(
        "rnc,ncv->rnv", attended, value_up, preferred_element_type=jnp.float32
    ).astype(jnp.bfloat16)
    return (hidden, index_scores, attn_out)


def solution(mesh):
    placed = (
        P(("groups", "dp"), "ctx"),
        P(("groups", "dp"), None, None, "ctx"),
        P(("groups", "dp"), None),
        P(("groups", "dp"), None),
        P("ctx"),
        P("ctx", None),
        P("ctx", None),
        P(),
        P(None, ("ctx", "hp"), None),
        P(("ctx", "hp"), None, None),
        P(None, ("ctx", "hp"), None),
        P(("ctx", "hp"), None, None),
        P(("groups", "dp"), "ctx", None),
        P(("groups", "dp"), ("ctx", "hp"), None),
        P(("groups", "dp")),
        P(("groups", "dp"), None),
    )
    return jax.shard_map(
        local,
        mesh=mesh,
        in_specs=placed,
        out_specs=(
            P(("groups", "dp"), "ctx"),
            P(("groups", "dp"), ("ctx", "hp")),
            P(("groups", "dp"), ("ctx", "hp"), None),
        ),
        check_vma=False,
    )
```

profile of v0, /device:TPU:1, one launch (start us, length us, event | category | flops | bytes accessed | tf_op | source)
XLA Modules:
  0.0 119.9 jit_solution(5031923924929819054)
XLA Ops:
  7.2 3.6 %all-to-all-start = ((bf16[1,2,16,1792]{3,2,0,1:T(8,128)(2,1)}), bf16[1,2,16,1792]{3,2,0,1:T(8,128)(2,1)S(1)}, u32[]{:S(2)}, u32[]{:S(2)}) async-start(bf16[1,2,16,1792]{3,2,0,1:T(8,128)(2,1)} %bitcast.49), calls=%async_computation | async-start | bytes 229376 | tf_op jit(solution)/shard_map/all_to_all | solution.py:69
  10.9 0.7 compare_select_fusion.1
  11.7 0.8 compare_reduce_fusion
  12.4 0.7 compare_and_fusion
  13.2 1.4 %all-to-all-done = bf16[1,2,16,1792]{3,2,0,1:T(8,128)(2,1)S(1)} async-done(((bf16[1,2,16,1792]{3,2,0,1:T(8,128)(2,1)}), bf16[1,2,16,1792]{3,2,0,1:T(8,128)(2,1)S(1)}, u32[]{:S(2)}, u32[]{:S(2)}) %all-to-all-start) | async-done | bytes 114720 | tf_op jit(solution)/shard_map/all_to_all | solution.py:69
  15.2 0.8 fusion.22
  16.0 0.8 fusion.25
  16.8 10.2 %psum.21 = f32[2]{0:T(128)S(1)} all-reduce(f32[2]{0:T(128)S(1)} %get-tuple-element.214), channel_id=1, replica_groups=mesh['groups'=2,'ctx'=4,'dp'=2,'hp'=2] {'ctx'}, use_global_device_ids=true, to_apply=%region_2.0 | all-reduce | flops 2 | bytes 16 | tf_op jit(solution)/shard_map/psum | solution.py:72
  27.1 1.2 fusion.37
  28.2 3.5 %fusion.35 = f32[2,1536]{1,0:T(2,128)S(1)} fusion(bf16[1792,1536]{1,0:T(8,128)(2,1)} %param.23, bf16[2,1792]{1,0:T(2,128)(2,1)S(1)} %get-tuple-element.215, f32[2]{0:T(128)S(1)} %add_rsqrt_fusion.1, f32[1792]{0:T(1024)} %param.22), kind=kOutput, calls=%fused_computation.71 | convolution fusion | flops 11024384 | bytes 5531656 | tf_op jit(solution)/shard_map/dot_general | solution.py:74
  31.7 12.1 %all-reduce = (f32[2,64]{1,0:T(2,128)S(1)}, f32[2,1536]{1,0:T(2,128)S(1)}) all-reduce(f32[2,64]{1,0:T(2,128)S(1)} %fusion.37, f32[2,1536]{1,0:T(2,128)S(1)} %fusion.35), channel_id=1, replica_groups=mesh['groups'=2,'ctx'=4,'dp'=2,'hp'=2] {'ctx'}, use_global_device_ids=true, to_apply=%region_3.0 | all-reduce | flops 3200 | bytes 25600 | tf_op jit(solution)/shard_map/psum | solution.py:76
  43.9 6.4 %convolution_convert_fusion.1 = bf16[2,16,192]{2,0,1:T(2,128)(2,1)S(1)} fusion(bf16[1536,16,192]{0,2,1:T(8,128)(2,1)} %param.26, f32[2,1536]{1,0:T(2,128)S(1)} %get-tuple-element.209, f32[2]{0:T(128)S(1)} %add_rsqrt_fusion, f32[1536]{0:T(1024)S(1)} %copy-done.3), kind=kOutput, calls=%fused_computation.19 | convolution fusion | flops 18889728 | bytes 9467912 | tf_op jit(solution)/shard_map/rq,qnd->rnd/dot_general | solution.py:80
  50.8 10.6 %all_gather.25 = bf16[2,64,576]{2,0,1:T(2,128)(2,1)S(1)} all-gather(bf16[2,16,576]{2,0,1:T(2,128)(2,1)S(1)} %pad_maximum_fusion), channel_id=1, replica_groups=mesh['groups'=2,'ctx'=4,'dp'=2,'hp'=2] {'ctx'}, dimensions={1}, use_global_device_ids=true | all-gather | bytes 184320 | tf_op jit(solution)/shard_map/all_gather | solution.py:90
  61.8 1.2 fusion.13
  63.3 6.8 %all-gather.4 = f32[4,2,64]{2,1,0:T(2,128)S(1)} all-gather(f32[1,2,64]{2,1,0:T(2,128)S(1)} %bitcast.51), channel_id=3, replica_groups=mesh['groups'=2,'ctx'=4,'dp'=2,'hp'=2] {'ctx'}, dimensions={0}, use_global_device_ids=true | all-gather | bytes 2560 | tf_op jit(solution)/shard_map/all_gather | solution.py:20
  70.0 6.6 %all-gather.3 = f32[4,2,64]{2,1,0:T(2,128)S(1)} all-gather(f32[1,2,64]{2,1,0:T(2,128)S(1)} %bitcast.50), channel_id=2, replica_groups=mesh['groups'=2,'ctx'=4,'dp'=2,'hp'=2] {'ctx'}, dimensions={0}, use_global_device_ids=true | all-gather | bytes 2560 | tf_op jit(solution)/shard_map/all_gather | solution.py:20
  77.2 27.9 %all_gather.24 = bf16[2,64,128]{2,0,1:T(2,128)(2,1)S(1)} all-gather(bf16[2,8,128]{2,0,1:T(2,128)(2,1)S(1)} %fusion.10), channel_id=1, replica_groups=mesh['groups'=2,'ctx'=4,'dp'=2,'hp'=2] {'ctx','hp'}, dimensions={1}, use_global_device_ids=true | all-gather | bytes 36864 | tf_op jit(solution)/shard_map/all_gather | solution.py:91
  105.3 0.6 compare_select_fusion
  105.9 1.0 slice.35
  106.9 3.4 %while.19 = (s32[]{:T(128)}, f32[2,64]{1,0:T(2,128)S(1)}, f32[2,64]{1,0:T(2,128)S(1)}, f32[2,64,512]{2,1,0:T(8,128)S(1)}, f32[4,2,64]{2,1,0:T(2,128)S(1)}, /*ind...) while((s32[]{:T(128)}, f32[2,64]{1,0:T(2,128)S(1)}, ...), condition=%wide.region_11.12_spmd, body=%wide.region_10.11_spmd.sunk | while | flops 197381 | bytes 791695 | solution.py:26
  107.0 1.1 fusion.51
  108.1 1.1 fusion.51
  109.2 1.1 fusion.51
  110.5 2.0 %fusion.9 = bf16[2,16,128]{2,0,1:T(2,128)(2,1)S(1)} fusion(bf16[16,512,128]{2,1,0:T(8,128)(2,1)} %param.29, bf16[2,16,512]{2,1,0:T(8,128)(2,1)S(1)} %divide_convert_fusion), kind=kOutput, calls=%fused_computation.21 | convolution fusion | flops 4198400 | bytes 2138112 | tf_op jit(solution)/shard_map/rnc,ncv->rnv/dot_general | solution.py:127
  (42 shorter events, 3.6 us)
Async XLA Ops:
  7.2 69.5 %copy-start = (bf16[1536,8,128]{2,1,0:T(8,128)(2,1)S(1)}, bf16[1536,8,128]{2,1,0:T(8,128)(2,1)}, u32[]{:S(2)}) copy-start(bf16[1536,8,128]{2,1,0:T(8,128)(2,1)} %param.28) | copy-start | bytes 9437188
  7.2 7.4 %all-to-all-start = ((bf16[1,2,16,1792]{3,2,0,1:T(8,128)(2,1)}), bf16[1,2,16,1792]{3,2,0,1:T(8,128)(2,1)S(1)}, u32[]{:S(2)}, u32[]{:S(2)}) async-start(bf16[1,2,16,1792]{3,2,0,1:T(8,128)(2,1)} %bitcast.49), calls=%async_computation | async-start | bytes 229376 | tf_op jit(solution)/shard_map/all_to_all | solution.py:69
  10.8 95.1 %all-gather.7.cloned.1.call-start = ((), (), s32[]{:S(2)}) async-start(), calls=%async_computation.1 | async-start | bytes 1310720 | tf_op jit(solution)/shard_map/all_gather | solution.py:20
  16.8 14.9 %copy-start.4 = (bf16[2,1792]{1,0:T(2,128)(2,1)}, bf16[2,1792]{1,0:T(2,128)(2,1)S(1)}, u32[]{:S(2)}) copy-start(bf16[2,1792]{1,0:T(2,128)(2,1)S(1)} %get-tuple-element.215) | copy-start | bytes 21508
  28.2 15.7 %copy-start.3 = (f32[1536]{0:T(1024)S(1)}, f32[1536]{0:T(1024)}, u32[]{:S(2)}) copy-start(f32[1536]{0:T(1024)} %param.25) | copy-start | bytes 18436
  43.9 6.4 %copy-start.2 = (bf16[16,128,512]{2,1,0:T(8,128)(2,1)S(1)}, bf16[16,128,512]{2,1,0:T(8,128)(2,1)}, u32[]{:S(2)}) copy-start(bf16[16,128,512]{2,1,0:T(8,128)(2,1)} %param.27) | copy-start | bytes 6291460
  50.3 11.1 %copy-start.1 = (bf16[2,512,576]{1,2,0:T(8,128)(2,1)S(1)}, bf16[2,512,576]{1,2,0:T(8,128)(2,1)}, u32[]{:S(2)}) copy-start(bf16[2,512,576]{1,2,0:T(8,128)(2,1)} %param.30) | copy-start | bytes 3538948
  63.0 42.3 %copy-start.5 = (s32[2]{0:T(128)S(1)}, s32[2]{0:T(128)}, u32[]{:S(2)}) copy-start(s32[2]{0:T(128)} %param.32) | copy-start | bytes 28
  63.0 42.0 %copy-start.6 = (bf16[2,256,128]{2,1,0:T(8,128)(2,1)S(1)}, bf16[2,256,128]{2,1,0:T(8,128)(2,1)}, u32[]{:S(2)}) copy-start(bf16[2,256,128]{2,1,0:T(8,128)(2,1)} %param.31) | copy-start | bytes 393220
Sparse Core Ops, SparseCore 0:
  63.2 35.1 all-gather.6
where the time goes:
time: 121 us; the launch traced here: 120 us
  blocking collectives  74.1 us (61%)
  matrix products  15.7 us (13%)
  between operations  14.2 us (12%)
  other arithmetic  8.23 us (7%)
  starting transfers between devices  3.67 us (3%)
  local copies, waits for them, and re-layouts  2.41 us (2%)
  waiting for transfers between devices  1.46 us (1%)
    all_gather x1, blocking collectives, local(): all_index = lax.all_gather(index_local, ('ctx', 'hp'), axis=1, tiled=True)  27.9 us
    all_gather x2, blocking collectives, combined_all(): everything = jax.tree.map(lambda part: lax.all_gather(part, axis), array)  13.4 us
    psum x1, blocking collectives, local(): latent_sum, gate_sum = lax.psum((latent_part, gate_part), 'ctx')  12.1 us
    all_gather x1, blocking collectives, local(): group_queries = lax.all_gather(queries, 'ctx', axis=1, tiled=True)  10.6 us
    psum x1, blocking collectives, local(): squares = lax.psum(jnp.sum(widened * widened, axis=1), 'ctx')  10.2 us
    dot_general x1, matrix products, local(): jnp.einsum('rq,qnd->rnd', latent, query_up, preferred_element_type=jnp.fl...  6.38 us
    all_to_all x1, starting transfers between devices, local(): lax.all_to_all(expert_out, 'dp', split_axis=1, concat_axis=0, tiled=True)  3.63 us
    dot_general x1, matrix products, local(): jnp.dot(normed, query_down, preferred_element_type=jnp.float32)  3.48 us
  transfers between devices with their start and end apart: 2, of which 1 were waited for; matrix products, arithmetic and copies ran while one was open for 3% of the time, Pallas kernels for 0%

commit v1 on v0

v1 whole, which is shorter than its diff:
```python
import functools

import jax
import jax.numpy as jnp
from jax import lax
from jax.experimental import pallas as pl
from jax.experimental.pallas import tpu as pltpu
from jax.sharding import PartitionSpec as P

D = 7168
KVLORA = 512
ROPE = 64
NOPE = 128
IHEADS = 64
IDIM = 128
BLK = 64


epsilon = 1e-06
very_low = -1e30


def shifted(size, step):
    return [(i, (i + step) % size) for i in range(size)]


def swapped(size, bit):
    return [(i, i ^ bit) for i in range(size)]


def pick_blocks(half, first_ref, row_ref, blocks_ref, cache_ref, keep_ref, send_ref):
    row = row_ref[0]
    width = cache_ref.shape[1]
    lane = lax.broadcasted_iota(jnp.int32, (width, 2 * BLK), 1)
    for j, out_ref in enumerate((keep_ref, send_ref)):
        begin = first_ref[1 + j]
        for pair in range(half // 2):
            total = jnp.zeros((width, 2 * BLK), jnp.float32)
            for side in range(2):
                local = blocks_ref[row, begin + 2 * pair + side] - first_ref[0]
                owned = (local >= 0) & (local < cache_ref.shape[2] // BLK)
                local = jnp.where(owned, local, 0)
                tile = cache_ref[row, :, pl.ds(pl.multiple_of(local // 2 * (2 * BLK), 2 * BLK), 2 * BLK)]
                tile = tile.astype(jnp.float32)
                swap = (local % 2) != side
                tile = jnp.where(swap, pltpu.roll(tile, BLK, 1), tile)
                mask = (lane // BLK == side) & owned
                total = jnp.where(mask, tile, total)
            out_ref[:, pair * 2 * BLK : (pair + 1) * 2 * BLK] = total.astype(out_ref.dtype)


def local(
    residual,
    expert_out,
    combine_slot,
    combine_gate,
    attn_gain,
    query_down,
    index_gate,
    latent_gain,
    query_up,
    key_absorb,
    index_query,
    value_up,
    latent_cache,
    index_keys,
    lengths,
    block_list,
):
    n_ctx, n_dp, n_hp = (lax.axis_size(name) for name in ("ctx", "dp", "hp"))
    c, d, h = (lax.axis_index(name) for name in ("ctx", "dp", "hp"))
    capacity = expert_out.shape[2]
    selected = block_list.shape[1]
    half = selected // 2
    span = latent_cache.shape[1]

    pieces = [(d, lax.dynamic_index_in_dim(expert_out[0], d, 0, False))]
    for step in range(1, n_dp):
        piece = lax.dynamic_index_in_dim(expert_out[0], (d + step) % n_dp, 0, False)
        pieces.append(((d + n_dp - step) % n_dp, lax.ppermute(piece, "dp", shifted(n_dp, step))))

    parity = c % 2
    first = jnp.stack([c * (span // BLK), parity * half, (1 - parity) * half]).astype(jnp.int32)
    width = latent_cache.shape[2]
    buffer = jax.ShapeDtypeStruct((width, half * BLK), jnp.bfloat16)
    smem = pl.BlockSpec(memory_space=pltpu.SMEM)
    vmem = pl.BlockSpec(memory_space=pltpu.VMEM)
    keep, send = pl.pallas_call(
        functools.partial(pick_blocks, half),
        out_shape=(buffer, buffer),
        in_specs=[smem, smem, smem, vmem],
        out_specs=(vmem, vmem),
        name="pick_blocks",
    )(first, h.reshape(1), block_list, jnp.swapaxes(latent_cache, 1, 2))
    held = keep + lax.ppermute(send, "ctx", swapped(n_ctx, 1))
    bit = 2
    while bit < n_ctx:
        held = held + lax.ppermute(held, "ctx", swapped(n_ctx, bit))
        bit *= 2
    other = lax.ppermute(held, "ctx", swapped(n_ctx, 1))
    mine = jnp.concatenate([held, other], axis=1)
    theirs = lax.ppermute(mine, "hp", swapped(n_hp, 1))

    routed = 0.0
    for source, piece in pieces:
        slot = source * capacity + jnp.arange(capacity, dtype=jnp.int32)
        weight = jnp.sum(
            jnp.where(combine_slot[:, :, None] == slot[None, None, :], combine_gate[:, :, None], 0.0), axis=1
        )
        routed = routed + jnp.sum(weight[:, :, None] * piece.astype(jnp.float32)[None], axis=1)
    hidden = (residual.astype(jnp.float32) + routed).astype(jnp.bfloat16)
    widened = hidden.astype(jnp.float32)
    scaled = (widened * attn_gain).astype(jnp.bfloat16)
    squares = jnp.sum(widened * widened, axis=1, keepdims=True)
    latent_part = jnp.dot(scaled, query_down, preferred_element_type=jnp.float32)
    gate_part = jnp.dot(scaled, index_gate, preferred_element_type=jnp.float32)
    part = jnp.concatenate([latent_part, gate_part, jnp.broadcast_to(squares, gate_part.shape)], axis=1)

    total = part
    for step in range(1, n_ctx):
        total = total + lax.ppermute(part, "ctx", shifted(n_ctx, step))
    qlora = latent_part.shape[1]
    scale = lax.rsqrt(total[:, qlora + IHEADS : qlora + IHEADS + 1] / D + epsilon)
    latent_sum = total[:, :qlora] * scale
    head_gate = total[:, qlora : qlora + IHEADS] * (scale * IHEADS**-0.5 * IDIM**-0.5)
    latent_scale = lax.rsqrt(jnp.mean(latent_sum * latent_sum, axis=-1, keepdims=True) + epsilon)
    latent = (latent_sum * latent_scale * latent_gain).astype(jnp.bfloat16)

    index_local = jnp.einsum("rq,qnd->nrd", latent, index_query, preferred_element_type=jnp.float32).astype(
        jnp.bfloat16
    )
    index_pair = lax.ppermute(index_local, "hp", swapped(n_hp, 1))
    index_pair = jnp.where(h == 0, jnp.stack([index_local, index_pair]), jnp.stack([index_pair, index_local]))
    gathered = [(c, index_pair)]
    for step in range(1, n_ctx):
        gathered.append(((c + n_ctx - step) % n_ctx, lax.ppermute(index_pair, "ctx", shifted(n_ctx, step))))
    gate_heads = head_gate.reshape(head_gate.shape[0], n_ctx, n_hp, -1)
    raw = 0.0
    for source, pair in gathered:
        gates = lax.dynamic_index_in_dim(gate_heads, source, 1, False)
        logits = jnp.einsum("hnrd,rtd->rhnt", pair, index_keys, preferred_element_type=jnp.float32)
        raw = raw + jnp.sum(gates[..., None] * jnp.maximum(logits, 0.0), axis=(1, 2))
    index_span = index_keys.shape[1]
    index_pos = (c * n_hp + h) * index_span + jnp.arange(index_span, dtype=jnp.int32)
    index_scores = jnp.where(index_pos[None, :] < lengths[:, None], raw, 0.0)

    projected = jnp.einsum("rq,qnd->rnd", latent, query_up, preferred_element_type=jnp.float32).astype(jnp.bfloat16)
    absorbed = jnp.einsum(
        "rnk,nkc->rnc", projected[:, :, :NOPE], key_absorb, preferred_element_type=jnp.float32
    ).astype(jnp.bfloat16)
    queries = jnp.concatenate([absorbed, projected[:, :, NOPE:]], axis=-1)
    cache = jnp.where(h == 0, jnp.stack([mine, theirs]), jnp.stack([theirs, mine]))
    order = jnp.where(parity == 0, block_list, jnp.concatenate([block_list[:, half:], block_list[:, :half]], axis=1))
    position = (order[:, :, None] * BLK + jnp.arange(BLK, dtype=jnp.int32)).reshape(order.shape[0], -1)
    live = (position < lengths[:, None])[:, None, :]
    logits = jnp.einsum("rnc,rct->rnt", queries, cache, preferred_element_type=jnp.float32) * (NOPE + ROPE) ** -0.5
    masked = jnp.where(live, logits, very_low)
    weights = jnp.where(live, jnp.exp(masked - jnp.max(masked, axis=-1, keepdims=True)), 0.0)
    merged = jnp.einsum(
        "rnt,rct->rnc", weights.astype(jnp.bfloat16), cache[:, :KVLORA], preferred_element_type=jnp.float32
    )
    attended = (merged / jnp.sum(weights, axis=-1, keepdims=True)).astype(jnp.bfloat16)
    attn_out = jnp.einsum("rnc,ncv->rnv", attended, value_up, preferred_element_type=jnp.float32).astype(jnp.bfloat16)
    return (hidden, index_scores, attn_out)


def solution(mesh):
    placed = (
        P(("groups", "dp"), "ctx"),
        P(("groups", "dp"), None, None, "ctx"),
        P(("groups", "dp"), None),
        P(("groups", "dp"), None),
        P("ctx"),
        P("ctx", None),
        P("ctx", None),
        P(),
        P(None, ("ctx", "hp"), None),
        P(("ctx", "hp"), None, None),
        P(None, ("ctx", "hp"), None),
        P(("ctx", "hp"), None, None),
        P(("groups", "dp"), "ctx", None),
        P(("groups", "dp"), ("ctx", "hp"), None),
        P(("groups", "dp")),
        P(("groups", "dp"), None),
    )
    return jax.shard_map(
        local,
        mesh=mesh,
        in_specs=placed,
        out_specs=(
            P(("groups", "dp"), "ctx"),
            P(("groups", "dp"), ("ctx", "hp")),
            P(("groups", "dp"), ("ctx", "hp"), None),
        ),
        check_vma=False,
    )
```

time: 121 us -> 57.2 us (0.47)
  blocking collectives: 74.1 us -> 0 us
  between operations: 14.2 us -> 0.91 us
  starting transfers between devices: 3.67 us -> 15.3 us
  waiting for transfers between devices: 1.46 us -> 10.6 us
  matrix products: 15.7 us -> 18.5 us
  Pallas kernels: 0 us -> 2.22 us
  other arithmetic: 8.23 us -> 6.51 us
    all_gather x4 -> x0, blocking collectives: 51.9 us -> none  [the longest x1 27.9 us: local(): all_index = lax.all_gather(index_local, ('ctx', 'hp'), axis=1, tiled=True)]
    psum x2 -> x0, blocking collectives: 22.3 us -> none  [the longest x1 12.1 us: local(): latent_sum, gate_sum = lax.psum((latent_part, gate_part), 'ctx')]
    ppermute x0 -> x12, starting transfers between devices: none -> 15.3 us  [the longest x3 3.86 us: local(): lax.ppermute(index_pair, 'ctx', shifted(n_ctx, step))]
    ppermute x0 -> x12, waiting for transfers between devices: none -> 10.6 us  [the longest x1 4.84 us: local(): held = held + lax.ppermute(held, 'ctx', swapped(n_ctx, bit))]
    all_to_all x1 -> x0, starting transfers between devices: 3.63 us -> none  [local(): lax.all_to_all(expert_out, 'dp', split_axis=1, concat_axis=0, tiled=True)]
    add x8 -> x5, other arithmetic: 3.3 us -> 0.11 us  [the longest x1 0.04 us: local(): held = keep + lax.ppermute(send, 'ctx', swapped(n_ctx, 1))]
    dot_general x6 -> x9, matrix products: 6.99 us -> 9.86 us  [the longest x4 4.28 us: local(): jnp.einsum('hnrd,rtd->rhnt', pair, index_keys, preferred_element_type=jnp...]
    pallas_call x0 -> x1, Pallas kernels: none -> 2.22 us  [local(): pl.pallas_call(functools.partial(pick_blocks, half), out_shape=(buffer, b...]
  transfers between devices with their start and end apart: 2 -> 12, of which waited for: 1 -> 4; matrix products, arithmetic and copies ran while one was open for 3% -> 38% of each run, Pallas kernels for 0% -> 4%
where the time goes in v1:
time: 57.2 us; the launch traced here: 56.8 us
  matrix products  18.5 us (32%)
  starting transfers between devices  15.3 us (27%)
  waiting for transfers between devices  10.6 us (19%)
  other arithmetic  6.51 us (11%)
  local copies, waits for them, and re-layouts  2.85 us (5%)
  Pallas kernels  2.22 us (4%)
  between operations  0.91 us (2%)
    dot_general x1, matrix products, local(): jnp.einsum('rq,qnd->rnd', latent, query_up, preferred_element_type=jnp.fl...  6.23 us
    ppermute x1, waiting for transfers between devices, local(): held = held + lax.ppermute(held, 'ctx', swapped(n_ctx, bit))  4.84 us
    dot_general x4, matrix products, local(): jnp.einsum('hnrd,rtd->rhnt', pair, index_keys, preferred_element_type=jnp...  4.28 us
    ppermute x3, starting transfers between devices, local(): lax.ppermute(index_pair, 'ctx', shifted(n_ctx, step))  3.86 us
    ppermute x3, starting transfers between devices, local(): total = total + lax.ppermute(part, 'ctx', shifted(n_ctx, step))  3.78 us
    dot_general x1, matrix products, local(): jnp.dot(scaled, query_down, preferred_element_type=jnp.float32)  3.39 us
    ppermute x3, waiting for transfers between devices, local(): total = total + lax.ppermute(part, 'ctx', shifted(n_ctx, step))  2.98 us
    ppermute x1, waiting for transfers between devices, local(): other = lax.ppermute(held, 'ctx', swapped(n_ctx, 1))  2.72 us
  transfers between devices with their start and end apart: 12, of which 4 were waited for; matrix products, arithmetic and copies ran while one was open for 38% of the time, Pallas kernels for 4%

profile of v1, /device:TPU:1, one launch (start us, length us, event | category | flops | bytes accessed | tf_op | source)
XLA Modules:
  0.0 56.8 jit_solution(8166146459317110534)
XLA Ops:
  0.7 1.0 %dynamic-slice_bitcast_fusion = (bf16[16,1792]{1,0:T(8,128)(2,1)S(1)}, f32[16,1792]{1,0:T(8,128)S(1)}) fusion(bf16[1,2,16,1792]{3,2,1,0:T(8,128)(2,1)} %param.17, s32[]{:T(128)S(6)} %select_n.91, s32[]{:T(128)S(6)} %select_n.88), kind=kLoop, calls=%fused_computation.38 | loop fusion | flops 28672 | bytes 286728 | tf_op jit(solution)/shard_map/jit(dynamic_index_in_dim)/squeeze | solution.py:79
  1.7 2.1 %collective-permute-start = (bf16[16,1792]{1,0:T(8,128)(2,1)S(1)}, bf16[16,1792]{1,0:T(8,128)(2,1)S(1)}, u32[]{:S(2)}, u32[]{:S(2)}) collective-permute-start(bf16[16,1792]{1,0:T(8,128)(2,1)S(1)} %get-tuple-element.27), channel_id=1, source_target_pairs={{0,2},{2,0},{1,3},{3,1},{4,6},{6,4},{5,7},{7,5},{8,10},{10,8},{9,1... | collective-permute-start | bytes 172040 | tf_op jit(solution)/shard_map/ppermute | solution.py:80
  4.3 2.2 %pick_blocks.1 = (bf16[576,128]{1,0:T(8,128)(2,1)}, bf16[576,128]{1,0:T(8,128)(2,1)}) custom-call(s32[3]{0:T(128)} %pad_add_fusion.first_ref, s32[1]{0:T(128)} %bitcast.18.row_ref, s32[2,4]{1,0:T(2,128)} %blocks_ref.1, bf16[2,576,512]{2,1,0:T(8,128)(2,1)} %bitcast.53), custom_call_target="tpu_custom_call" | custom-call | tf_op jit(solution)/shard_map/pick_blocks/pallas_call | solution.py:88
  6.6 1.3 %collective-permute-start.8 = (bf16[576,128]{1,0:T(8,128)(2,1)}, bf16[576,128]{1,0:T(8,128)(2,1)S(1)}, u32[]{:S(2)}, u32[]{:S(2)}) collective-permute-start(bf16[576,128]{1,0:T(8,128)(2,1)} %get-tuple-element.6), channel_id=1, source_target_pairs={{0,4},{4,0},{8,12},{12,8},{1,5},{5,1},{9,13},{13,9},{2,6},{6,2},{1... | collective-permute-start | bytes 442376 | tf_op jit(solution)/shard_map/ppermute | solution.py:95
  11.5 0.8 %fusion.30 = (f32[2]{0:T(128)S(1)}, bf16[2,1792]{1,0:T(2,128)(2,1)S(1)}) fusion(f32[2,1792]{1,0:T(2,128)S(1)} %multiply_reduce_fusion.1, f32[2,1792]{1,0:T(2,128)S(1)} %multiply_reduce_fusion, bf16[2,1792]{1,0:T(2,128)(2,1)} %param.16), kind=kLoop, calls=%fused_computation.47 | loop fusion | flops 25086 | bytes 43016 | tf_op jit(solution)/shard_map/reduce_sum | solution.py:114
  12.3 3.4 %fusion.46 = f32[2,1536]{1,0:T(2,128)S(1)} fusion(bf16[1792,1536]{1,0:T(8,128)(2,1)} %param.21, bf16[2,1792]{1,0:T(2,128)(2,1)S(1)} %get-tuple-element.24, f32[1792]{0:T(1024)} %param.20), kind=kOutput, calls=%fused_computation.84 | convolution fusion | flops 11020800 | bytes 5531648 | tf_op jit(solution)/shard_map/dot_general | solution.py:115
  16.1 1.5 %collective-permute-start.3 = (f32[2,1664]{1,0:T(2,128)S(1)}, f32[2,1664]{1,0:T(2,128)S(1)}, u32[]{:S(2)}, u32[]{:S(2)}) collective-permute-start(f32[2,1664]{1,0:T(2,128)S(1)} %concatenate.12), channel_id=1, source_target_pairs={{0,12},{4,0},{8,4},{12,8},{1,13},{5,1},{9,5},{13,9},{2,14},{6,2},{... | collective-permute-start | bytes 39944 | tf_op jit(solution)/shard_map/ppermute | solution.py:121
  17.6 0.9 %collective-permute-start.2 = (f32[2,1664]{1,0:T(2,128)S(1)}, f32[2,1664]{1,0:T(2,128)S(1)}, u32[]{:S(2)}, u32[]{:S(2)}) collective-permute-start(f32[2,1664]{1,0:T(2,128)S(1)} %concatenate.12), channel_id=1, source_target_pairs={{0,8},{4,12},{8,0},{12,4},{1,9},{5,13},{9,1},{13,5},{2,10},{6,14},... | collective-permute-start | bytes 39944 | tf_op jit(solution)/shard_map/ppermute | solution.py:121
  18.5 1.4 %collective-permute-start.1 = (f32[2,1664]{1,0:T(2,128)S(1)}, f32[2,1664]{1,0:T(2,128)S(1)}, u32[]{:S(2)}, u32[]{:S(2)}) collective-permute-start(f32[2,1664]{1,0:T(2,128)S(1)} %concatenate.12), channel_id=1, source_target_pairs={{0,4},{4,8},{8,12},{12,0},{1,5},{5,9},{9,13},{13,1},{2,6},{6,10},{... | collective-permute-start | bytes 39944 | tf_op jit(solution)/shard_map/ppermute | solution.py:121
  19.9 1.2 %collective-permute-done.2 = f32[2,1664]{1,0:T(2,128)S(1)} collective-permute-done((f32[2,1664]{1,0:T(2,128)S(1)}, f32[2,1664]{1,0:T(2,128)S(1)}, u32[]{:S(2)}, u32[]{:S(2)}) %collective-permute-start.2) | collective-permute-done | bytes 13344 | tf_op jit(solution)/shard_map/ppermute | solution.py:121
  21.1 1.7 %collective-permute-done.1 = f32[2,1664]{1,0:T(2,128)S(1)} collective-permute-done((f32[2,1664]{1,0:T(2,128)S(1)}, f32[2,1664]{1,0:T(2,128)S(1)}, u32[]{:S(2)}, u32[]{:S(2)}) %collective-permute-start.1) | collective-permute-done | bytes 13344 | tf_op jit(solution)/shard_map/ppermute | solution.py:121
  23.9 2.7 %collective-permute-start.4 = (bf16[8,2,128]{2,1,0:T(2,128)(2,1)S(1)}, bf16[8,2,128]{2,1,0:T(2,128)(2,1)S(1)}, u32[]{:S(2)}, u32[]{:S(2)}) collective-permute-start(bf16[8,2,128]{2,1,0:T(2,128)(2,1)S(1)} %bitcast.55), channel_id=1, source_target_pairs={{0,1},{1,0},{2,3},{3,2},{4,5},{5,4},{6,7},{7,6},{8,9},{9,8},{10,11... | collective-permute-start | bytes 12296 | tf_op jit(solution)/shard_map/ppermute | solution.py:132
  26.7 6.2 %convolution_convert_fusion.1 = bf16[2,16,192]{2,0,1:T(2,128)(2,1)S(1)} fusion(bf16[1536,16,192]{0,2,1:T(8,128)(2,1)} %param.24, f32[2,1664]{1,0:T(2,128)S(1)} %add_add_fusion, f32[2]{0:T(128)S(1)} %add_rsqrt_fusion, f32[2]{0:T(128)S(1)} %get-tuple-element.19, f32[1536]{0:T(1024)S(1)} %copy-done.4), kind=kOutput, calls=%fused_computation.20 | convolution fusion | flops 18892800 | bytes 9470976 | tf_op jit(solution)/shard_map/rq,qnd->rnd/dot_general | solution.py:147
  33.7 2.0 %collective-permute-start.7 = (bf16[2,8,2,128]{3,2,1,0:T(2,128)(2,1)S(1)}, bf16[2,8,2,128]{3,2,1,0:T(2,128)(2,1)S(1)}, u32[]{:S(2)}, u32[]{:S(2)}) collective-permute-start(bf16[2,8,2,128]{3,2,1,0:T(2,128)(2,1)S(1)} %broadcast_select_fusion), channel_id=1, source_target_pairs={{0,12},{4,0},{8,4},{12,8},{1,13},{5,1},{9,5},{13,9},{2,14},{6,2},{... | collective-permute-start | bytes 24584 | tf_op jit(solution)/shard_map/ppermute | solution.py:136
  36.1 1.4 %collective-permute-start.5 = (bf16[2,8,2,128]{3,2,1,0:T(2,128)(2,1)S(1)}, bf16[2,8,2,128]{3,2,1,0:T(2,128)(2,1)S(1)}, u32[]{:S(2)}, u32[]{:S(2)}) collective-permute-start(bf16[2,8,2,128]{3,2,1,0:T(2,128)(2,1)S(1)} %broadcast_select_fusion), channel_id=1, source_target_pairs={{0,4},{4,8},{8,12},{12,0},{1,5},{5,9},{9,13},{13,1},{2,6},{6,10},{... | collective-permute-start | bytes 24584 | tf_op jit(solution)/shard_map/ppermute | solution.py:136
  37.5 1.1 %fusion.13 = f32[2,256]{1,0:T(2,128)S(1)} fusion(bf16[2,256,128]{2,1,0:T(8,128)(2,1)} %param.29, f32[2,2,8]{2,1,0:T(2,128)S(1)} %get-tuple-element.32, bf16[2,8,2,128]{3,2,1,0:T(2,128)(2,1)S(1)} %broadcast_select_fusion), kind=kOutput, calls=%fused_computation.21 | convolution fusion | flops 2121216 | bytes 141440 | tf_op jit(solution)/shard_map/hnrd,rtd->rhnt/dot_general | solution.py:141
  38.6 4.8 %collective-permute-done.9 = bf16[576,128]{1,0:T(8,128)(2,1)S(1)} collective-permute-done((bf16[576,128]{1,0:T(8,128)(2,1)S(1)}, bf16[576,128]{1,0:T(8,128)(2,1)S(1)}, u32[]{:S(2)}, u32[]{:S(2)}) %collective-permute-start.9) | collective-permute-done | bytes 147488 | tf_op jit(solution)/shard_map/ppermute | solution.py:98
  43.6 1.1 %fusion.16 = f32[2,256]{1,0:T(2,128)S(1)} fusion(bf16[2,256,128]{2,1,0:T(8,128)(2,1)} %param.29, f32[2,2,8]{2,1,0:T(2,128)S(1)} %get-tuple-element.30, bf16[2,8,2,128]{3,2,1,0:T(2,128)(2,1)S(1)} %collective-permute-done.7), kind=kOutput, calls=%fused_computation.24 | convolution fusion | flops 2121216 | bytes 141440 | tf_op jit(solution)/shard_map/hnrd,rtd->rhnt/dot_general | solution.py:141
  44.6 1.1 %fusion.15 = f32[2,256]{1,0:T(2,128)S(1)} fusion(bf16[2,256,128]{2,1,0:T(8,128)(2,1)} %param.29, f32[2,2,8]{2,1,0:T(2,128)S(1)} %get-tuple-element.31, bf16[2,8,2,128]{3,2,1,0:T(2,128)(2,1)S(1)} %collective-permute-done.6), kind=kOutput, calls=%fused_computation.23 | convolution fusion | flops 2121216 | bytes 141440 | tf_op jit(solution)/shard_map/hnrd,rtd->rhnt/dot_general | solution.py:141
  45.7 2.7 %collective-permute-done.10 = bf16[576,128]{1,0:T(8,128)(2,1)S(1)} collective-permute-done((bf16[576,128]{1,0:T(8,128)(2,1)S(1)}, bf16[576,128]{1,0:T(8,128)(2,1)S(1)}, u32[]{:S(2)}, u32[]{:S(2)}) %collective-permute-start.10) | collective-permute-done | bytes 147488 | tf_op jit(solution)/shard_map/ppermute | solution.py:100
  48.5 1.4 %collective-permute-start.11 = (bf16[576,256]{1,0:T(8,128)(2,1)S(1)}, bf16[576,256]{1,0:T(8,128)(2,1)S(1)}, u32[]{:S(2)}, u32[]{:S(2)}) collective-permute-start(bf16[576,256]{1,0:T(8,128)(2,1)S(1)} %get-tuple-element.26), channel_id=1, source_target_pairs={{0,1},{1,0},{2,3},{3,2},{4,5},{5,4},{6,7},{7,6},{8,9},{9,8},{10,11... | collective-permute-start | bytes 884744 | tf_op jit(solution)/shard_map/ppermute | solution.py:102
  49.9 1.1 %fusion.14 = f32[2,256]{1,0:T(2,128)S(1)} fusion(bf16[2,256,128]{2,1,0:T(8,128)(2,1)} %param.29, f32[2,2,8]{2,1,0:T(2,128)S(1)} %get-tuple-element.29, bf16[2,8,2,128]{3,2,1,0:T(2,128)(2,1)S(1)} %collective-permute-done.5), kind=kOutput, calls=%fused_computation.22 | convolution fusion | flops 2121216 | bytes 141440 | tf_op jit(solution)/shard_map/hnrd,rtd->rhnt/dot_general | solution.py:141
  52.9 1.3 %fusion.4 = bf16[2,16,512]{2,1,0:T(8,128)(2,1)S(1)} fusion(bf16[2,576,256]{2,1,0:T(8,128)(2,1)} %copy-done.1, f32[2,16]{1,0:T(2,128)S(1)} %fusion.50, f32[2,16,256]{2,1,0:T(8,128)S(1)} %fusion.12, pred[2,256]{1,0:T(4,128)(4,1)S(1)} %add_compare_fusion), kind=kOutput, calls=%fused_computation.6 | convolution fusion | flops 8446239 | bytes 624640 | tf_op jit(solution)/shard_map/rnt,rct->rnc/dot_general | solution.py:159
  54.2 2.0 %fusion.17 = bf16[2,16,128]{2,0,1:T(2,128)(2,1)S(1)} fusion(bf16[16,512,128]{2,1,0:T(8,128)(2,1)} %param.27, bf16[2,16,512]{2,1,0:T(8,128)(2,1)S(1)} %fusion.4), kind=kOutput, calls=%fused_computation.26 | convolution fusion | flops 4198400 | bytes 2138112 | tf_op jit(solution)/shard_map/rnc,ncv->rnv/dot_general | solution.py:163
  (66 shorter events, 9.4 us)
Async XLA Ops:
  0.6 22.7 %copy-start = (bf16[1536,8,128]{2,1,0:T(8,128)(2,1)S(1)}, bf16[1536,8,128]{2,1,0:T(8,128)(2,1)}, u32[]{:S(2)}) copy-start(bf16[1536,8,128]{2,1,0:T(8,128)(2,1)} %param.26) | copy-start | bytes 9437188
  1.7 9.7 %collective-permute-start = (bf16[16,1792]{1,0:T(8,128)(2,1)S(1)}, bf16[16,1792]{1,0:T(8,128)(2,1)S(1)}, u32[]{:S(2)}, u32[]{:S(2)}) collective-permute-start(bf16[16,1792]{1,0:T(8,128)(2,1)S(1)} %get-tuple-element.27), channel_id=1, source_target_pairs={{0,2},{2,0},{1,3},{3,1},{4,6},{6,4},{5,7},{7,5},{8,10},{10,8},{9,1... | collective-permute-start | bytes 172040 | tf_op jit(solution)/shard_map/ppermute | solution.py:80
  6.6 9.2 %copy-start.6 = (f32[1792]{0:T(1024)S(1)}, f32[1792]{0:T(1024)}, u32[]{:S(2)}) copy-start(f32[1792]{0:T(1024)} %param.20) | copy-start | bytes 21508
  6.6 26.9 %collective-permute-start.8 = (bf16[576,128]{1,0:T(8,128)(2,1)}, bf16[576,128]{1,0:T(8,128)(2,1)S(1)}, u32[]{:S(2)}, u32[]{:S(2)}) collective-permute-start(bf16[576,128]{1,0:T(8,128)(2,1)} %get-tuple-element.6), channel_id=1, source_target_pairs={{0,4},{4,0},{8,12},{12,8},{1,5},{5,1},{9,13},{13,9},{2,6},{6,2},{1... | collective-permute-start | bytes 442376 | tf_op jit(solution)/shard_map/ppermute | solution.py:95
  11.3 4.4 %copy-start.8 = (bf16[1792,64]{0,1:T(8,128)(2,1)S(1)}, bf16[1792,64]{0,1:T(8,128)(2,1)}, u32[]{:S(2)}) copy-start(bf16[1792,64]{0,1:T(8,128)(2,1)} %param.22) | copy-start | bytes 688132
  11.3 12.0 %copy-start.4 = (f32[1536]{0:T(1024)S(1)}, f32[1536]{0:T(1024)}, u32[]{:S(2)}) copy-start(f32[1536]{0:T(1024)} %param.23) | copy-start | bytes 18436
  12.3 11.6 %copy-start.5 = (bf16[2,1792]{1,0:T(2,128)(2,1)}, bf16[2,1792]{1,0:T(2,128)(2,1)S(1)}, u32[]{:S(2)}) copy-start(bf16[2,1792]{1,0:T(2,128)(2,1)S(1)} %get-tuple-element.24) | copy-start | bytes 21508
  16.1 3.8 %collective-permute-start.3 = (f32[2,1664]{1,0:T(2,128)S(1)}, f32[2,1664]{1,0:T(2,128)S(1)}, u32[]{:S(2)}, u32[]{:S(2)}) collective-permute-start(f32[2,1664]{1,0:T(2,128)S(1)} %concatenate.12), channel_id=1, source_target_pairs={{0,12},{4,0},{8,4},{12,8},{1,13},{5,1},{9,5},{13,9},{2,14},{6,2},{... | collective-permute-start | bytes 39944 | tf_op jit(solution)/shard_map/ppermute | solution.py:121
  17.6 3.5 %collective-permute-start.2 = (f32[2,1664]{1,0:T(2,128)S(1)}, f32[2,1664]{1,0:T(2,128)S(1)}, u32[]{:S(2)}, u32[]{:S(2)}) collective-permute-start(f32[2,1664]{1,0:T(2,128)S(1)} %concatenate.12), channel_id=1, source_target_pairs={{0,8},{4,12},{8,0},{12,4},{1,9},{5,13},{9,1},{13,5},{2,10},{6,14},... | collective-permute-start | bytes 39944 | tf_op jit(solution)/shard_map/ppermute | solution.py:121
  18.5 4.4 %collective-permute-start.1 = (f32[2,1664]{1,0:T(2,128)S(1)}, f32[2,1664]{1,0:T(2,128)S(1)}, u32[]{:S(2)}, u32[]{:S(2)}) collective-permute-start(f32[2,1664]{1,0:T(2,128)S(1)} %concatenate.12), channel_id=1, source_target_pairs={{0,4},{4,8},{8,12},{12,0},{1,5},{5,9},{9,13},{13,1},{2,6},{6,10},{... | collective-permute-start | bytes 39944 | tf_op jit(solution)/shard_map/ppermute | solution.py:121
  23.9 9.0 %copy-start.2 = (bf16[16,128,512]{2,1,0:T(8,128)(2,1)S(1)}, bf16[16,128,512]{2,1,0:T(8,128)(2,1)}, u32[]{:S(2)}) copy-start(bf16[16,128,512]{2,1,0:T(8,128)(2,1)} %param.25) | copy-start | bytes 6291460
  23.9 9.5 %copy-start.3 = (bf16[576,128]{1,0:T(8,128)(2,1)S(1)}, bf16[576,128]{1,0:T(8,128)(2,1)}, u32[]{:S(2)}) copy-start(bf16[576,128]{1,0:T(8,128)(2,1)} %get-tuple-element.5) | copy-start | bytes 442372
  23.9 9.7 %collective-permute-start.4 = (bf16[8,2,128]{2,1,0:T(2,128)(2,1)S(1)}, bf16[8,2,128]{2,1,0:T(2,128)(2,1)S(1)}, u32[]{:S(2)}, u32[]{:S(2)}) collective-permute-start(bf16[8,2,128]{2,1,0:T(2,128)(2,1)S(1)} %bitcast.55), channel_id=1, source_target_pairs={{0,1},{1,0},{2,3},{3,2},{4,5},{5,4},{6,7},{7,6},{8,9},{9,8},{10,11... | collective-permute-start | bytes 12296 | tf_op jit(solution)/shard_map/ppermute | solution.py:132
  32.9 18.1 %copy-start.7 = (s32[2]{0:T(128)S(1)}, s32[2]{0:T(128)}, u32[]{:S(2)}) copy-start(s32[2]{0:T(128)} %param.30) | copy-start | bytes 28
  33.5 9.9 %collective-permute-start.9 = (bf16[576,128]{1,0:T(8,128)(2,1)S(1)}, bf16[576,128]{1,0:T(8,128)(2,1)S(1)}, u32[]{:S(2)}, u32[]{:S(2)}) collective-permute-start(bf16[576,128]{1,0:T(8,128)(2,1)S(1)} %add.186), channel_id=1, source_target_pairs={{0,8},{4,12},{8,0},{12,4},{1,9},{5,13},{9,1},{13,5},{2,10},{6,14},... | collective-permute-start | bytes 442376 | tf_op jit(solution)/shard_map/ppermute | solution.py:98
  33.7 9.9 %collective-permute-start.7 = (bf16[2,8,2,128]{3,2,1,0:T(2,128)(2,1)S(1)}, bf16[2,8,2,128]{3,2,1,0:T(2,128)(2,1)S(1)}, u32[]{:S(2)}, u32[]{:S(2)}) collective-permute-start(bf16[2,8,2,128]{3,2,1,0:T(2,128)(2,1)S(1)} %broadcast_select_fusion), channel_id=1, source_target_pairs={{0,12},{4,0},{8,4},{12,8},{1,13},{5,1},{9,5},{13,9},{2,14},{6,2},{... | collective-permute-start | bytes 24584 | tf_op jit(solution)/shard_map/ppermute | solution.py:136
  35.6 9.0 %collective-permute-start.6 = (bf16[2,8,2,128]{3,2,1,0:T(2,128)(2,1)S(1)}, bf16[2,8,2,128]{3,2,1,0:T(2,128)(2,1)S(1)}, u32[]{:S(2)}, u32[]{:S(2)}) collective-permute-start(bf16[2,8,2,128]{3,2,1,0:T(2,128)(2,1)S(1)} %broadcast_select_fusion), channel_id=1, source_target_pairs={{0,8},{4,12},{8,0},{12,4},{1,9},{5,13},{9,1},{13,5},{2,10},{6,14},... | collective-permute-start | bytes 24584 | tf_op jit(solution)/shard_map/ppermute | solution.py:136
  36.1 13.8 %collective-permute-start.5 = (bf16[2,8,2,128]{3,2,1,0:T(2,128)(2,1)S(1)}, bf16[2,8,2,128]{3,2,1,0:T(2,128)(2,1)S(1)}, u32[]{:S(2)}, u32[]{:S(2)}) collective-permute-start(bf16[2,8,2,128]{3,2,1,0:T(2,128)(2,1)S(1)} %broadcast_select_fusion), channel_id=1, source_target_pairs={{0,4},{4,8},{8,12},{12,0},{1,5},{5,9},{9,13},{13,1},{2,6},{6,10},{... | collective-permute-start | bytes 24584 | tf_op jit(solution)/shard_map/ppermute | solution.py:136
  43.5 5.0 %collective-permute-start.10 = (bf16[576,128]{1,0:T(8,128)(2,1)S(1)}, bf16[576,128]{1,0:T(8,128)(2,1)S(1)}, u32[]{:S(2)}, u32[]{:S(2)}) collective-permute-start(bf16[576,128]{1,0:T(8,128)(2,1)S(1)} %add.187), channel_id=1, source_target_pairs={{0,4},{4,0},{8,12},{12,8},{1,5},{5,1},{9,13},{13,9},{2,6},{6,2},{1... | collective-permute-start | bytes 442376 | tf_op jit(solution)/shard_map/ppermute | solution.py:100
  48.5 3.2 %collective-permute-start.11 = (bf16[576,256]{1,0:T(8,128)(2,1)S(1)}, bf16[576,256]{1,0:T(8,128)(2,1)S(1)}, u32[]{:S(2)}, u32[]{:S(2)}) collective-permute-start(bf16[576,256]{1,0:T(8,128)(2,1)S(1)} %get-tuple-element.26), channel_id=1, source_target_pairs={{0,1},{1,0},{2,3},{3,2},{4,5},{5,4},{6,7},{7,6},{8,9},{9,8},{10,11... | collective-permute-start | bytes 884744 | tf_op jit(solution)/shard_map/ppermute | solution.py:102
  51.7 0.8 %copy-start.1 = (bf16[2,576,256]{2,1,0:T(8,128)(2,1)}, bf16[2,576,256]{2,1,0:T(8,128)(2,1)S(1)}, u32[]{:S(2)}) copy-start(bf16[2,576,256]{2,1,0:T(8,128)(2,1)S(1)} %maximum_select_fusion) | copy-start | bytes 1769476

commit v2 on v1

v2 whole, which is shorter than its diff:
```python
import functools

import jax
import jax.numpy as jnp
from jax import lax
from jax.experimental import pallas as pl
from jax.experimental.pallas import tpu as pltpu
from jax.sharding import PartitionSpec as P

D = 7168
KVLORA = 512
ROPE = 64
NOPE = 128
IHEADS = 64
IDIM = 128
BLK = 64
LANES = 128


epsilon = 1e-06
very_low = -1e30

SMEM = pl.BlockSpec(memory_space=pltpu.SMEM)
VMEM = pl.BlockSpec(memory_space=pltpu.VMEM)
HBM = pl.BlockSpec(memory_space=pltpu.HBM)
NT = (((1,), (1,)), ((), ()))


def shifted(size, step):
    return [(i, (i + step) % size) for i in range(size)]


def swapped(size, bit):
    return [(i, i ^ bit) for i in range(size)]


def limits(mib):
    return pltpu.CompilerParams(vmem_limit_bytes=mib << 20)


def cost(mib):
    return pl.CostEstimate(flops=0, bytes_accessed=mib << 20, transcendentals=0)


def in_hbm(array):
    return pltpu.with_memory_space_constraint(array, pltpu.HBM)


def in_vmem(array):
    return pltpu.with_memory_space_constraint(array, pltpu.VMEM)


def prepare(
    first_ref, blocks_ref, cache_ref, slots_ref, down_ref, out_ref, own_ref, down_out_ref, tiles, sems, own_sem, down_sem
):
    own_copy = pltpu.make_async_copy(slots_ref.at[first_ref[2]], own_ref, own_sem)
    down_copy = pltpu.make_async_copy(down_ref, down_out_ref, down_sem)
    row = first_ref[0]
    width = cache_ref.shape[1]
    count = tiles.shape[0]
    spot = []
    for slot in range(count):
        local = blocks_ref[row, slot] - first_ref[1]
        owned = (local >= 0) & (local < cache_ref.shape[2] // BLK)
        local = jnp.where(owned, local, 0)
        begin = pl.multiple_of(local // 2 * LANES, LANES)
        copy = pltpu.make_async_copy(cache_ref.at[row, :, pl.ds(begin, LANES)], tiles.at[slot], sems.at[slot])
        copy.start()
        spot.append((copy, owned, (local % 2) != (slot % 2)))
    own_copy.start()
    down_copy.start()
    lane = lax.broadcasted_iota(jnp.int32, (width, LANES), 1)
    for pair in range(count // 2):
        total = jnp.zeros((width, LANES), jnp.float32)
        for side in range(2):
            copy, owned, swap = spot[2 * pair + side]
            copy.wait()
            tile = tiles[2 * pair + side].astype(jnp.float32)
            tile = jnp.where(swap, pltpu.roll(tile, BLK, 1), tile)
            total = jnp.where((lane // BLK == side) & owned, tile, total)
        out_ref[:, pair * LANES : (pair + 1) * LANES] = total.astype(out_ref.dtype)
    own_copy.wait()
    down_copy.wait()


def combine_down(
    sources, group_ref, slot_ref, gate_ref, residual_ref, gain_ref, own_ref, *refs
):
    received = refs[:sources]
    down_ref, igate_ref, hidden_ref, part_ref = refs[sources:]
    rows, features = residual_ref.shape
    capacity = own_ref.shape[0]
    group = group_ref[0]
    place = lax.broadcasted_iota(jnp.int32, (capacity, 1), 0)
    routed = [jnp.zeros((1, features), jnp.float32)] * rows
    for step, ref in enumerate((own_ref, *received)):
        source = lax.rem(group + len(received) + 1 - step, len(received) + 1)
        piece = (ref[...] if step == 0 else ref[pl.ds(group, 1)][0]).astype(jnp.float32)
        for r in range(rows):
            weight = jnp.zeros((capacity, 1), jnp.float32)
            for k in range(slot_ref.shape[1]):
                weight = weight + jnp.where(place == slot_ref[r, k] - source * capacity, gate_ref[r, k], 0.0)
            routed[r] = routed[r] + jnp.sum(weight * piece, axis=0, keepdims=True)
    hidden = (residual_ref[...].astype(jnp.float32) + jnp.concatenate(routed, axis=0)).astype(jnp.bfloat16)
    hidden_ref[...] = hidden
    widened = hidden.astype(jnp.float32)
    scaled = (widened * gain_ref[...]).astype(jnp.bfloat16)
    qlora = down_ref.shape[1]
    squares = jnp.sum(widened * widened, axis=1, keepdims=True)
    part_ref[:, qlora + LANES :] = jnp.broadcast_to(squares, (rows, LANES))
    gates = lax.dot_general(scaled, igate_ref[...], NT, preferred_element_type=jnp.float32)
    part_ref[:, qlora : qlora + LANES] = jnp.concatenate([gates, gates], axis=1)
    part_ref[:, :qlora] = jnp.dot(scaled, down_ref[...], preferred_element_type=jnp.float32)


def attend(
    first_ref, blocks_ref, lengths_ref, latent_ref, mine_ref, theirs_ref, up_ref, absorb_ref, value_ref, out_ref,
    up, absorb, value, absorbed, rotary, up_sem, absorb_sem, value_sem,
):
    heads = up_ref.shape[0]
    up_copies, absorb_copies = [], []
    for n in range(heads):
        up_copies.append(pltpu.make_async_copy(up_ref.at[n], up.at[n], up_sem.at[n]))
        up_copies[-1].start()
        absorb_copies.append(pltpu.make_async_copy(absorb_ref.at[n], absorb.at[n], absorb_sem.at[n]))
        absorb_copies[-1].start()
    value_copy = pltpu.make_async_copy(value_ref, value, value_sem)
    value_copy.start()
    latent = latent_ref[...]
    rows = latent.shape[0]
    for n in range(heads):
        up_copies[n].wait()
        projected = lax.dot_general(latent, up[n], NT, preferred_element_type=jnp.float32).astype(jnp.bfloat16)
        absorb_copies[n].wait()
        query = jnp.dot(projected[:, :NOPE], absorb[n], preferred_element_type=jnp.float32)
        for r in range(rows):
            absorbed[r, n : n + 1, :] = query[r : r + 1]
            rotary[r, n : n + 1, :] = projected[r : r + 1, NOPE:].astype(jnp.float32)
    this = first_ref[0]
    shape = (1, mine_ref.shape[1])
    lane = lax.broadcasted_iota(jnp.int32, shape, 1)
    attended = []
    for row, cache_ref in ((this, mine_ref), (1 - this, theirs_ref)):
        position = lane % BLK
        for slot in range(blocks_ref.shape[1]):
            position = position + jnp.where(lane // BLK == slot, blocks_ref[row, slot] * BLK, 0)
        live = position < lengths_ref[row]
        cache = cache_ref[...]
        logits = jnp.dot(
            absorbed[pl.ds(row, 1)][0].astype(jnp.bfloat16), cache[:KVLORA], preferred_element_type=jnp.float32
        ) + jnp.dot(rotary[pl.ds(row, 1)][0].astype(jnp.bfloat16), cache[KVLORA:], preferred_element_type=jnp.float32)
        masked = jnp.where(live, logits * (NOPE + ROPE) ** -0.5, very_low)
        weights = jnp.where(live, jnp.exp(masked - jnp.max(masked, axis=1, keepdims=True)), 0.0)
        total = jnp.sum(weights, axis=1, keepdims=True)
        merged = lax.dot_general(
            weights.astype(jnp.bfloat16), cache[:KVLORA], NT, preferred_element_type=jnp.float32
        )
        attended.append(merged / total)
    attended = jnp.concatenate(attended, axis=0).astype(jnp.bfloat16)
    value_copy.wait()
    head = lax.broadcasted_iota(jnp.int32, (2 * heads, value_ref.shape[2]), 0) % heads
    result = jnp.zeros(head.shape, jnp.float32)
    for n in range(heads):
        product = jnp.dot(attended, value[n], preferred_element_type=jnp.float32)
        result = jnp.where(head == n, product, result)
    for k, row in enumerate((this, 1 - this)):
        out_ref[pl.ds(row, 1)] = result[k * heads : (k + 1) * heads].astype(out_ref.dtype)[None]


def score(pieces, first_ref, lengths_ref, gates_ref, keys_ref, *refs):
    gathered = refs[:pieces]
    out_ref, queries = refs[pieces:]
    heads = gathered[0].shape[1]
    order = lax.broadcasted_iota(jnp.int32, (IHEADS, IHEADS), 0)
    head = order
    rows, span = out_ref.shape
    for k, ref in enumerate(gathered):
        for side in range(2):
            spot = 2 * k + side
            begin = first_ref[1 + k] + jnp.where(first_ref[0] == side, 0, heads)
            head = jnp.where(order // heads == spot, begin + order % heads, head)
            for r in range(rows):
                queries[r, spot * heads : (spot + 1) * heads, :] = ref[side, :, r, :].astype(jnp.float32)
    base = first_ref[1 + pieces]
    position = base + lax.broadcasted_iota(jnp.int32, (1, span), 1)
    for r in range(rows):
        logits = lax.dot_general(
            queries[r].astype(jnp.bfloat16), keys_ref[r], NT, preferred_element_type=jnp.float32
        )
        gates = jnp.where(lax.broadcasted_iota(jnp.int32, head.shape, 1) == head, gates_ref[r : r + 1, :], 0.0)
        gates = jnp.sum(gates, axis=1, keepdims=True)
        raw = jnp.sum(gates * jnp.maximum(logits, 0.0), axis=0, keepdims=True)
        out_ref[r : r + 1, :] = jnp.where(position < lengths_ref[r], raw, 0.0)


def local(
    residual,
    expert_out,
    combine_slot,
    combine_gate,
    attn_gain,
    query_down,
    index_gate,
    latent_gain,
    query_up,
    key_absorb,
    index_query,
    value_up,
    latent_cache,
    index_keys,
    lengths,
    block_list,
):
    n_ctx, n_dp, n_hp = (lax.axis_size(name) for name in ("ctx", "dp", "hp"))
    c, d, h = (lax.axis_index(name) for name in ("ctx", "dp", "hp"))
    rows, features = residual.shape
    qlora = query_down.shape[1]
    selected = block_list.shape[1]
    span, width = latent_cache.shape[1:]
    heads = value_up.shape[0]
    f32, bf16 = jnp.float32, jnp.bfloat16

    slots = expert_out[0]
    received = [lax.ppermute(slots, "dp", shifted(n_dp, step)) for step in range(1, n_dp)]

    place = jnp.stack([h, c * (span // BLK), d]).astype(jnp.int32)
    mine, own, down = pl.pallas_call(
        prepare,
        out_shape=(
            pltpu.VMEM((width, selected * BLK), bf16),
            pltpu.VMEM(slots.shape[1:], bf16),
            pltpu.VMEM(query_down.shape, bf16),
        ),
        in_specs=[SMEM, SMEM, HBM, HBM, HBM],
        out_specs=(VMEM, VMEM, VMEM),
        scratch_shapes=[
            pltpu.VMEM((selected, width, LANES), bf16),
            pltpu.SemaphoreType.DMA((selected,)),
            pltpu.SemaphoreType.DMA,
            pltpu.SemaphoreType.DMA,
        ],
        compiler_params=limits(8),
        cost_estimate=cost(1),
        name="prepare",
    )(place, block_list, in_hbm(jnp.swapaxes(latent_cache, 1, 2)), in_hbm(slots), in_hbm(query_down))
    neighbour = lax.ppermute(mine, "ctx", swapped(n_ctx, 1))
    received, mine = lax.optimization_barrier((received, mine))

    hidden, part = pl.pallas_call(
        functools.partial(combine_down, len(received)),
        out_shape=(
            jax.ShapeDtypeStruct((rows, features), bf16),
            pltpu.VMEM((rows, qlora + 2 * LANES), f32),
        ),
        in_specs=[SMEM] * 3 + [VMEM] * (5 + len(received)),
        out_specs=(VMEM, VMEM),
        compiler_params=limits(8),
        cost_estimate=cost(64),
        name="combine_down",
    )(
        d.reshape(1).astype(jnp.int32), combine_slot, combine_gate, residual, attn_gain.reshape(1, -1), in_vmem(own),
        *received, in_vmem(down), index_gate.T,
    )

    mine, part = lax.optimization_barrier((mine + neighbour, part))
    bit = 2
    while bit < n_ctx:
        mine = mine + lax.ppermute(mine, "ctx", swapped(n_ctx, bit))
        bit *= 2

    total = part
    for step in range(1, n_ctx):
        total = total + lax.ppermute(part, "ctx", swapped(n_ctx, step))
    scale = lax.rsqrt(total[:, qlora + LANES : qlora + LANES + 1] / D + epsilon)
    latent_sum = total[:, :qlora] * scale
    head_gate = total[:, qlora : qlora + IHEADS] * (scale * IHEADS**-0.5 * IDIM**-0.5)
    latent_scale = lax.rsqrt(jnp.mean(latent_sum * latent_sum, axis=-1, keepdims=True) + epsilon)
    latent = (latent_sum * latent_scale * latent_gain).astype(bf16)

    index_local = jnp.einsum("rq,qnd->nrd", latent, index_query, preferred_element_type=f32).astype(bf16)
    index_pair = jnp.stack([index_local, lax.ppermute(index_local, "hp", swapped(n_hp, 1))])
    gathered = [index_pair] + [lax.ppermute(index_pair, "ctx", swapped(n_ctx, step)) for step in range(1, n_ctx)]
    index_heads, index_span = index_local.shape[0], index_keys.shape[1]
    sources = [jnp.bitwise_xor(c, step) * n_hp * index_heads for step in range(n_ctx)]
    theirs = lax.ppermute(mine, "hp", swapped(n_hp, 1))
    latent, index_pair = lax.optimization_barrier((latent, index_pair))
    attn_out = pl.pallas_call(
        attend,
        out_shape=jax.ShapeDtypeStruct((rows, heads, value_up.shape[2]), bf16),
        in_specs=[SMEM, SMEM, SMEM, VMEM, VMEM, VMEM, HBM, HBM, HBM],
        out_specs=VMEM,
        scratch_shapes=[
            pltpu.VMEM((heads, query_up.shape[2], qlora), bf16),
            pltpu.VMEM(key_absorb.shape, bf16),
            pltpu.VMEM(value_up.shape, bf16),
            pltpu.VMEM((rows, heads, KVLORA), f32),
            pltpu.VMEM((rows, heads, ROPE), f32),
            pltpu.SemaphoreType.DMA((heads,)),
            pltpu.SemaphoreType.DMA((heads,)),
            pltpu.SemaphoreType.DMA,
        ],
        compiler_params=limits(24),
        cost_estimate=cost(14),
        name="attend",
    )(
        place, block_list, lengths, latent, mine, theirs, in_hbm(jnp.transpose(query_up, (1, 2, 0))),
        in_hbm(key_absorb), in_hbm(value_up),
    )
    gathered, attn_out = lax.optimization_barrier((gathered, attn_out))
    index_scores = pl.pallas_call(
        functools.partial(score, n_ctx),
        out_shape=jax.ShapeDtypeStruct((rows, index_span), f32),
        in_specs=[SMEM, SMEM, VMEM, VMEM] + [VMEM] * n_ctx,
        out_specs=VMEM,
        scratch_shapes=[pltpu.VMEM((rows, IHEADS, IDIM), f32)],
        compiler_params=limits(4),
        cost_estimate=cost(2),
        name="score",
    )(
        jnp.stack([h, *sources, (c * n_hp + h) * index_span]).astype(jnp.int32), lengths, head_gate, index_keys,
        *gathered,
    )

    return (hidden, index_scores, attn_out)

def solution(mesh):
    placed = (
        P(("groups", "dp"), "ctx"),
        P(("groups", "dp"), None, None, "ctx"),
        P(("groups", "dp"), None),
        P(("groups", "dp"), None),
        P("ctx"),
        P("ctx", None),
        P("ctx", None),
        P(),
        P(None, ("ctx", "hp"), None),
        P(("ctx", "hp"), None, None),
        P(None, ("ctx", "hp"), None),
        P(("ctx", "hp"), None, None),
        P(("groups", "dp"), "ctx", None),
        P(("groups", "dp"), ("ctx", "hp"), None),
        P(("groups", "dp")),
        P(("groups", "dp"), None),
    )
    return jax.shard_map(
        local,
        mesh=mesh,
        in_specs=placed,
        out_specs=(
            P(("groups", "dp"), "ctx"),
            P(("groups", "dp"), ("ctx", "hp")),
            P(("groups", "dp"), ("ctx", "hp"), None),
        ),
        check_vma=False,
    )
```

time: 57.2 us -> 54.6 us (0.955)
  matrix products: 18.5 us -> 0.52 us
  Pallas kernels: 2.22 us -> 19.5 us
  starting transfers between devices: 15.3 us -> 23.2 us
  other arithmetic: 6.51 us -> 1.72 us
  waiting for transfers between devices: 10.6 us -> 6.95 us
  local copies, waits for them, and re-layouts: 2.85 us -> 0.98 us
    dot_general x12 -> x1, matrix products: 18.5 us -> 0.52 us  [local(): jnp.einsum('rq,qnd->nrd', latent, index_query, preferred_element_type=f32)]
    pallas_call x1 -> x4, Pallas kernels: 2.22 us -> 19.5 us  [the longest x1 12.6 us: local(): pl.pallas_call(attend, out_shape=jax.ShapeDtypeStruct((rows, heads, value...]
    ppermute x11 -> x10, starting transfers between devices: 13.9 us -> 21.4 us  [the longest x1 8.82 us: local(): lax.ppermute(index_local, 'hp', swapped(n_hp, 1))]
    ppermute x11 -> x10, waiting for transfers between devices: 10.5 us -> 6.95 us  [the longest x1 2.71 us: local(): lax.ppermute(slots, 'dp', shifted(n_dp, step))]
    reduce_sum x4 -> x0, other arithmetic: 1.85 us -> none  [the longest x1 0.83 us: local(): squares = jnp.sum(widened * widened, axis=1, keepdims=True)]
    add x5 -> x3, other arithmetic: 0.11 us -> 1.13 us  [the longest x1 1.04 us: local(): mine = mine + lax.ppermute(mine, 'ctx', swapped(n_ctx, bit))]
    squeeze x1 -> x0, other arithmetic: 1.01 us -> none  [local(): piece = lax.dynamic_index_in_dim(expert_out[0], (d + step) % n_dp, 0, False)]
    slice x2 -> x0, local copies, waits for them, and re-layouts: 0.84 us -> none  [the longest x1 0.82 us: local(): block_list[:, half:]]
  transfers between devices with their start and end apart: 12 -> 11, of which waited for: 4 -> 4; matrix products, arithmetic and copies ran while one was open for 38% -> 4% of each run, Pallas kernels for 4% -> 27%
where the time goes in v2:
time: 54.6 us; the launch traced here: 53.7 us
  starting transfers between devices  23.2 us (42%)
  Pallas kernels  19.5 us (36%)
  waiting for transfers between devices  6.95 us (13%)
  other arithmetic  1.72 us (3%)
  local copies, waits for them, and re-layouts  0.98 us (2%)
  between operations  0.81 us (1%)
    pallas_call x1, Pallas kernels, local(): pl.pallas_call(attend, out_shape=jax.ShapeDtypeStruct((rows, heads, value...  12.6 us
    ppermute x1, starting transfers between devices, local(): lax.ppermute(index_local, 'hp', swapped(n_hp, 1))  8.82 us
    ppermute x3, starting transfers between devices, local(): total = total + lax.ppermute(part, 'ctx', swapped(n_ctx, step))  3.61 us
    ppermute x3, starting transfers between devices, local(): lax.ppermute(index_pair, 'ctx', swapped(n_ctx, step))  3.61 us
    pallas_call x1, Pallas kernels, local(): pl.pallas_call(prepare, out_shape=(pltpu.VMEM((width, selected * BLK), bf...  3.55 us
    ppermute x1, waiting for transfers between devices, local(): lax.ppermute(slots, 'dp', shifted(n_dp, step))  2.71 us
    ppermute x1, waiting for transfers between devices, local(): mine = mine + lax.ppermute(mine, 'ctx', swapped(n_ctx, bit))  2.38 us
    ppermute x1, starting transfers between devices, local(): neighbour = lax.ppermute(mine, 'ctx', swapped(n_ctx, 1))  2.19 us
  transfers between devices with their start and end apart: 11, of which 4 were waited for; matrix products, arithmetic and copies ran while one was open for 4% of the time, Pallas kernels for 27%

profile of v2, /device:TPU:1, one launch (start us, length us, event | category | flops | bytes accessed | tf_op | source)
XLA Modules:
  0.0 53.7 jit_solution(10098971218715401663)
XLA Ops:
  0.7 0.8 %copy-done.4 = s32[2,4]{1,0:T(2,128)S(1)} copy-done((s32[2,4]{1,0:T(2,128)S(1)}, s32[2,4]{1,0:T(2,128)}, u32[]{:S(2)}) %copy-start.4) | copy-done | bytes 56
  1.6 3.5 %prepare.1 = (bf16[576,256]{1,0:T(8,128)(2,1)S(1)}, bf16[16,1792]{1,0:T(8,128)(2,1)S(1)}, bf16[1792,1536]{1,0:T(8,128)(2,1)S(1)}) custom-call(s32[3]{0:T(128)S(1)} %pad_add_fusion.first_ref, s32[2,4]{1,0:T(2,128)S(1)} %copy-done.4, bf16[2,576,512]{2,1,0:T(8,128)(2,1)} %bitcast.21, bf16[2,16,1792]{2,1,0:T(8,128)(2,1)} %bitcast.22, bf16[1792,1536]{1,0:T(8,128)(2,1)} %down_ref.1), custom_call_target="tpu_custom_call" | custom-call | bytes 1048576 | tf_op jit(solution)/shard_map/prepare/pallas_call | solution.py:227
  5.2 2.2 %collective-permute-start.1 = (bf16[576,256]{1,0:T(8,128)(2,1)S(1)}, bf16[576,256]{1,0:T(8,128)(2,1)S(1)}, u32[]{:S(2)}, u32[]{:S(2)}) collective-permute-start(bf16[576,256]{1,0:T(8,128)(2,1)S(1)} %get-tuple-element.23), channel_id=1, source_target_pairs={{0,4},{4,0},{8,12},{12,8},{1,5},{5,1},{9,13},{13,9},{2,6},{6,2},{1... | collective-permute-start | bytes 884744 | tf_op jit(solution)/shard_map/ppermute | solution.py:246
  7.3 1.2 %collective-permute-start = (bf16[2,16,1792]{2,1,0:T(8,128)(2,1)S(1)}, bf16[2,16,1792]{2,1,0:T(8,128)(2,1)S(1)}, u32[]{:S(2)}, u32[]{:S(2)}) collective-permute-start(bf16[2,16,1792]{2,1,0:T(8,128)(2,1)S(1)} %bitcast.23), channel_id=1, source_target_pairs={{0,2},{2,0},{1,3},{3,1},{4,6},{6,4},{5,7},{7,5},{8,10},{10,8},{9,1... | collective-permute-start | bytes 344072 | tf_op jit(solution)/shard_map/ppermute | solution.py:224
  8.6 2.7 %collective-permute-done.refs_0_ = bf16[2,16,1792]{2,1,0:T(8,128)(2,1)S(1)} collective-permute-done((bf16[2,16,1792]{2,1,0:T(8,128)(2,1)S(1)}, bf16[2,16,1792]{2,1,0:T(8,128)(2,1)S(1)}, u32[]{:S(2)}, u32[]{:S(2)}) %collective-permute-start) | collective-permute-done | bytes 114720 | tf_op jit(solution)/shard_map/ppermute | solution.py:224
  11.3 2.0 %combine_down.1 = (bf16[2,1792]{1,0:T(2,128)(2,1)}, f32[2,1792]{1,0:T(2,128)S(1)}) custom-call(s32[1]{0:T(128)} %bitcast.group_ref, s32[2,8]{1,0:T(2,128)S(1)} %copy-done.7, f32[2,8]{1,0:T(2,128)S(1)} %copy-done.8, bf16[2,1792]{1,0:T(2,128)(2,1)S(1)} %copy-done.3, f32[1,1792]{1,0:T(1,128)S(1)} %reshape.22.gain_ref, ...), custom_call_target="tpu_custom_call" | custom-call | bytes 67108864 | tf_op jit(solution)/shard_map/combine_down/pallas_call | solution.py:249
  13.3 0.7 %collective-permute-done.1 = bf16[576,256]{1,0:T(8,128)(2,1)S(1)} collective-permute-done((bf16[576,256]{1,0:T(8,128)(2,1)S(1)}, bf16[576,256]{1,0:T(8,128)(2,1)S(1)}, u32[]{:S(2)}, u32[]{:S(2)}) %collective-permute-start.1) | collective-permute-done | bytes 294944 | tf_op jit(solution)/shard_map/ppermute | solution.py:246
  14.2 3.2 %collective-permute-start.4 = (f32[2,1792]{1,0:T(2,128)S(1)}, f32[2,1792]{1,0:T(2,128)S(1)}, u32[]{:S(2)}, u32[]{:S(2)}) collective-permute-start(f32[2,1792]{1,0:T(2,128)S(1)} %get-tuple-element.25), channel_id=1, source_target_pairs={{0,12},{4,8},{8,4},{12,0},{1,13},{5,9},{9,5},{13,1},{2,14},{6,10},... | collective-permute-start | bytes 43016 | tf_op jit(solution)/shard_map/ppermute | solution.py:273
  17.4 0.4 collective-permute-start.2
  17.8 2.0 %collective-permute-start.9 = (bf16[576,256]{1,0:T(8,128)(2,1)S(1)}, bf16[576,256]{1,0:T(8,128)(2,1)}, u32[]{:S(2)}, u32[]{:S(2)}) collective-permute-start(bf16[576,256]{1,0:T(8,128)(2,1)S(1)} %add.30), channel_id=1, source_target_pairs={{0,8},{4,12},{8,0},{12,4},{1,9},{5,13},{9,1},{13,5},{2,10},{6,14},... | collective-permute-start | bytes 884744 | tf_op jit(solution)/shard_map/ppermute | solution.py:268
  19.8 1.1 %collective-permute-done.3 = f32[2,1792]{1,0:T(2,128)S(1)} collective-permute-done((f32[2,1792]{1,0:T(2,128)S(1)}, f32[2,1792]{1,0:T(2,128)S(1)}, u32[]{:S(2)}, u32[]{:S(2)}) %collective-permute-start.3) | collective-permute-done | bytes 14368 | tf_op jit(solution)/shard_map/ppermute | solution.py:273
  20.9 0.2 fusion.8
  21.0 0.2 multiply_reduce_fusion
  21.2 0.1 multiply_convert_fusion.latent_ref
  21.3 0.5 fusion.2
  21.9 8.8 %collective-permute-start.5 = (bf16[8,2,128]{2,1,0:T(2,128)(2,1)S(1)}, bf16[8,2,128]{2,1,0:T(2,128)(2,1)S(1)}, u32[]{:S(2)}, u32[]{:S(2)}) collective-permute-start(bf16[8,2,128]{2,1,0:T(2,128)(2,1)S(1)} %bitcast.24), channel_id=1, source_target_pairs={{0,1},{1,0},{2,3},{3,2},{4,5},{5,4},{6,7},{7,6},{8,9},{9,8},{10,11... | collective-permute-start | bytes 12296 | tf_op jit(solution)/shard_map/ppermute | solution.py:281
  30.7 0.1 stack.46.first_ref
  30.8 2.4 %collective-permute-done.9 = bf16[576,256]{1,0:T(8,128)(2,1)} collective-permute-done((bf16[576,256]{1,0:T(8,128)(2,1)S(1)}, bf16[576,256]{1,0:T(8,128)(2,1)}, u32[]{:S(2)}, u32[]{:S(2)}) %collective-permute-start.9) | collective-permute-done | bytes 294944 | tf_op jit(solution)/shard_map/ppermute | solution.py:268
  33.2 1.0 %add.36.mine_ref = bf16[576,256]{1,0:T(8,128)(2,1)S(1)} add(bf16[576,256]{1,0:T(8,128)(2,1)S(1)} %add.30, bf16[576,256]{1,0:T(8,128)(2,1)} %collective-permute-done.9) | non-fusion elementwise | flops 147456 | bytes 884736 | tf_op jit(solution)/shard_map/add | solution.py:268
  34.2 1.7 %collective-permute-start.10 = (bf16[576,256]{1,0:T(8,128)(2,1)S(1)}, bf16[576,256]{1,0:T(8,128)(2,1)S(1)}, u32[]{:S(2)}, u32[]{:S(2)}) collective-permute-start(bf16[576,256]{1,0:T(8,128)(2,1)S(1)} %add.36.mine_ref), channel_id=1, source_target_pairs={{0,1},{1,0},{2,3},{3,2},{4,5},{5,4},{6,7},{7,6},{8,9},{9,8},{10,11... | collective-permute-start | bytes 884744 | tf_op jit(solution)/shard_map/ppermute | solution.py:285
  36.0 2.6 %collective-permute-start.8 = (bf16[2,8,2,128]{3,2,1,0:T(2,128)(2,1)S(1)}, bf16[2,8,2,128]{3,2,1,0:T(2,128)(2,1)S(1)}, u32[]{:S(2)}, u32[]{:S(2)}) collective-permute-start(bf16[2,8,2,128]{3,2,1,0:T(2,128)(2,1)S(1)} %pad_maximum_fusion.refs_0_), channel_id=1, source_target_pairs={{0,12},{4,8},{8,4},{12,0},{1,13},{5,9},{9,5},{13,1},{2,14},{6,10},... | collective-permute-start | bytes 24584 | tf_op jit(solution)/shard_map/ppermute | solution.py:282
  38.6 1.0 %collective-permute-start.6 = (bf16[2,8,2,128]{3,2,1,0:T(2,128)(2,1)S(1)}, bf16[2,8,2,128]{3,2,1,0:T(2,128)(2,1)S(1)}, u32[]{:S(2)}, u32[]{:S(2)}) collective-permute-start(bf16[2,8,2,128]{3,2,1,0:T(2,128)(2,1)S(1)} %pad_maximum_fusion.refs_0_), channel_id=1, source_target_pairs={{0,4},{4,0},{8,12},{12,8},{1,5},{5,1},{9,13},{13,9},{2,6},{6,2},{1... | collective-permute-start | bytes 24584 | tf_op jit(solution)/shard_map/ppermute | solution.py:282
  39.7 12.6 %attend.1 = bf16[2,16,128]{2,1,0:T(8,128)(2,1)} custom-call(s32[3]{0:T(128)S(1)} %pad_add_fusion.first_ref, s32[2,4]{1,0:T(2,128)S(1)} %copy-done.5, s32[2]{0:T(128)S(1)} %copy-done.6, bf16[2,1536]{1,0:T(2,128)(2,1)S(1)} %multiply_convert_fusion.latent_ref, bf16[576,256]{1,0:T(8,128)(2,1)S(1)} %add.36.mine_ref, ...), custom_call_target="tpu_custom_call" | custom-call | bytes 14680064 | tf_op jit(solution)/shard_map/attend/pallas_call | solution.py:287
  52.3 1.3 %score.1 = f32[2,256]{1,0:T(2,128)} custom-call(s32[6]{0:T(128)S(1)} %stack.46.first_ref, s32[2]{0:T(128)S(1)} %copy-done.6, f32[2,64]{1,0:T(2,128)S(1)} %slice_multiply_fusion.2.gates_ref, bf16[2,256,128]{2,1,0:T(8,128)(2,1)S(1)} %copy-done.2, bf16[2,8,2,128]{3,2,1,0:T(2,128)(2,1)S(1)} %pad_maximum_fusion.refs_0_, ...), custom_call_target="tpu_custom_call" | custom-call | bytes 2097152 | tf_op jit(solution)/shard_map/score/pallas_call | solution.py:310
  (39 shorter events, 0.3 us)
Async XLA Ops:
  0.6 20.7 %copy-start = (bf16[1536,8,128]{2,1,0:T(8,128)(2,1)S(1)}, bf16[1536,8,128]{2,1,0:T(8,128)(2,1)}, u32[]{:S(2)}) copy-start(bf16[1536,8,128]{2,1,0:T(8,128)(2,1)} %param.26) | copy-start | bytes 9437188
  0.7 0.8 %copy-start.4 = (s32[2,4]{1,0:T(2,128)S(1)}, s32[2,4]{1,0:T(2,128)}, u32[]{:S(2)}) copy-start(s32[2,4]{1,0:T(2,128)} %blocks_ref.3) | copy-start | bytes 100
  1.6 5.8 %copy-start.9 = (bf16[1,2,16,1792]{3,2,1,0:T(8,128)(2,1)S(1)}, bf16[1,2,16,1792]{3,2,1,0:T(8,128)(2,1)}, u32[]{:S(2)}) copy-start(bf16[1,2,16,1792]{3,2,1,0:T(8,128)(2,1)} %param.17) | copy-start | bytes 344068
  1.6 7.0 %copy-start.11 = (f32[1792]{0:T(1024)S(1)}, f32[1792]{0:T(1024)}, u32[]{:S(2)}) copy-start(f32[1792]{0:T(1024)} %param.20) | copy-start | bytes 21508
  1.6 9.7 %copy-start.1 = (bf16[1792,64]{0,1:T(8,128)(2,1)S(1)}, bf16[1792,64]{0,1:T(8,128)(2,1)}, u32[]{:S(2)}) copy-start(bf16[1792,64]{0,1:T(8,128)(2,1)} %param.22) | copy-start | bytes 688132
  1.6 9.7 %copy-start.3 = (bf16[2,1792]{1,0:T(2,128)(2,1)S(1)}, bf16[2,1792]{1,0:T(2,128)(2,1)}, u32[]{:S(2)}) copy-start(bf16[2,1792]{1,0:T(2,128)(2,1)} %residual_ref.1) | copy-start | bytes 21508
  1.6 9.7 %copy-start.7 = (s32[2,8]{1,0:T(2,128)S(1)}, s32[2,8]{1,0:T(2,128)}, u32[]{:S(2)}) copy-start(s32[2,8]{1,0:T(2,128)} %slot_ref.1) | copy-start | bytes 196
  1.6 9.7 %copy-start.8 = (f32[2,8]{1,0:T(2,128)S(1)}, f32[2,8]{1,0:T(2,128)}, u32[]{:S(2)}) copy-start(f32[2,8]{1,0:T(2,128)} %gate_ref.1) | copy-start | bytes 196
  5.2 8.9 %collective-permute-start.1 = (bf16[576,256]{1,0:T(8,128)(2,1)S(1)}, bf16[576,256]{1,0:T(8,128)(2,1)S(1)}, u32[]{:S(2)}, u32[]{:S(2)}) collective-permute-start(bf16[576,256]{1,0:T(8,128)(2,1)S(1)} %get-tuple-element.23), channel_id=1, source_target_pairs={{0,4},{4,0},{8,12},{12,8},{1,5},{5,1},{9,13},{13,9},{2,6},{6,2},{1... | collective-permute-start | bytes 884744 | tf_op jit(solution)/shard_map/ppermute | solution.py:246
  7.3 3.9 %collective-permute-start = (bf16[2,16,1792]{2,1,0:T(8,128)(2,1)S(1)}, bf16[2,16,1792]{2,1,0:T(8,128)(2,1)S(1)}, u32[]{:S(2)}, u32[]{:S(2)}) collective-permute-start(bf16[2,16,1792]{2,1,0:T(8,128)(2,1)S(1)} %bitcast.23), channel_id=1, source_target_pairs={{0,2},{2,0},{1,3},{3,1},{4,6},{6,4},{5,7},{7,5},{8,10},{10,8},{9,1... | collective-permute-start | bytes 344072 | tf_op jit(solution)/shard_map/ppermute | solution.py:224
  11.3 9.9 %copy-start.10 = (f32[1536]{0:T(1024)S(1)}, f32[1536]{0:T(1024)}, u32[]{:S(2)}) copy-start(f32[1536]{0:T(1024)} %param.23) | copy-start | bytes 18436
  13.3 26.3 %copy-start.5 = (s32[2,4]{1,0:T(2,128)S(1)}, s32[2,4]{1,0:T(2,128)}, u32[]{:S(2)}) copy-start(s32[2,4]{1,0:T(2,128)} %blocks_ref.3) | copy-start | bytes 100
  13.3 26.3 %copy-start.6 = (s32[2]{0:T(128)S(1)}, s32[2]{0:T(128)}, u32[]{:S(2)}) copy-start(s32[2]{0:T(128)} %lengths_ref.3) | copy-start | bytes 28
  14.2 5.6 %collective-permute-start.4 = (f32[2,1792]{1,0:T(2,128)S(1)}, f32[2,1792]{1,0:T(2,128)S(1)}, u32[]{:S(2)}, u32[]{:S(2)}) collective-permute-start(f32[2,1792]{1,0:T(2,128)S(1)} %get-tuple-element.25), channel_id=1, source_target_pairs={{0,12},{4,8},{8,4},{12,0},{1,13},{5,9},{9,5},{13,1},{2,14},{6,10},... | collective-permute-start | bytes 43016 | tf_op jit(solution)/shard_map/ppermute | solution.py:273
  17.4 3.5 %collective-permute-start.3 = (f32[2,1792]{1,0:T(2,128)S(1)}, f32[2,1792]{1,0:T(2,128)S(1)}, u32[]{:S(2)}, u32[]{:S(2)}) collective-permute-start(f32[2,1792]{1,0:T(2,128)S(1)} %get-tuple-element.25), channel_id=1, source_target_pairs={{0,8},{4,12},{8,0},{12,4},{1,9},{5,13},{9,1},{13,5},{2,10},{6,14},... | collective-permute-start | bytes 43016 | tf_op jit(solution)/shard_map/ppermute | solution.py:273
  17.4 3.5 %collective-permute-start.2 = (f32[2,1792]{1,0:T(2,128)S(1)}, f32[2,1792]{1,0:T(2,128)S(1)}, u32[]{:S(2)}, u32[]{:S(2)}) collective-permute-start(f32[2,1792]{1,0:T(2,128)S(1)} %get-tuple-element.25), channel_id=1, source_target_pairs={{0,4},{4,0},{8,12},{12,8},{1,5},{5,1},{9,13},{13,9},{2,6},{6,2},{1... | collective-permute-start | bytes 43016 | tf_op jit(solution)/shard_map/ppermute | solution.py:273
  17.8 15.4 %collective-permute-start.9 = (bf16[576,256]{1,0:T(8,128)(2,1)S(1)}, bf16[576,256]{1,0:T(8,128)(2,1)}, u32[]{:S(2)}, u32[]{:S(2)}) collective-permute-start(bf16[576,256]{1,0:T(8,128)(2,1)S(1)} %add.30), channel_id=1, source_target_pairs={{0,8},{4,12},{8,0},{12,4},{1,9},{5,13},{9,1},{13,5},{2,10},{6,14},... | collective-permute-start | bytes 884744 | tf_op jit(solution)/shard_map/ppermute | solution.py:268
  21.9 14.1 %collective-permute-start.5 = (bf16[8,2,128]{2,1,0:T(2,128)(2,1)S(1)}, bf16[8,2,128]{2,1,0:T(2,128)(2,1)S(1)}, u32[]{:S(2)}, u32[]{:S(2)}) collective-permute-start(bf16[8,2,128]{2,1,0:T(2,128)(2,1)S(1)} %bitcast.24), channel_id=1, source_target_pairs={{0,1},{1,0},{2,3},{3,2},{4,5},{5,4},{6,7},{7,6},{8,9},{9,8},{10,11... | collective-permute-start | bytes 12296 | tf_op jit(solution)/shard_map/ppermute | solution.py:281
  34.2 5.4 %collective-permute-start.10 = (bf16[576,256]{1,0:T(8,128)(2,1)S(1)}, bf16[576,256]{1,0:T(8,128)(2,1)S(1)}, u32[]{:S(2)}, u32[]{:S(2)}) collective-permute-start(bf16[576,256]{1,0:T(8,128)(2,1)S(1)} %add.36.mine_ref), channel_id=1, source_target_pairs={{0,1},{1,0},{2,3},{3,2},{4,5},{5,4},{6,7},{7,6},{8,9},{9,8},{10,11... | collective-permute-start | bytes 884744 | tf_op jit(solution)/shard_map/ppermute | solution.py:285
  36.0 16.3 %collective-permute-start.8 = (bf16[2,8,2,128]{3,2,1,0:T(2,128)(2,1)S(1)}, bf16[2,8,2,128]{3,2,1,0:T(2,128)(2,1)S(1)}, u32[]{:S(2)}, u32[]{:S(2)}) collective-permute-start(bf16[2,8,2,128]{3,2,1,0:T(2,128)(2,1)S(1)} %pad_maximum_fusion.refs_0_), channel_id=1, source_target_pairs={{0,12},{4,8},{8,4},{12,0},{1,13},{5,9},{9,5},{13,1},{2,14},{6,10},... | collective-permute-start | bytes 24584 | tf_op jit(solution)/shard_map/ppermute | solution.py:282
  38.6 13.7 %collective-permute-start.7 = (bf16[2,8,2,128]{3,2,1,0:T(2,128)(2,1)S(1)}, bf16[2,8,2,128]{3,2,1,0:T(2,128)(2,1)S(1)}, u32[]{:S(2)}, u32[]{:S(2)}) collective-permute-start(bf16[2,8,2,128]{3,2,1,0:T(2,128)(2,1)S(1)} %pad_maximum_fusion.refs_0_), channel_id=1, source_target_pairs={{0,8},{4,12},{8,0},{12,4},{1,9},{5,13},{9,1},{13,5},{2,10},{6,14},... | collective-permute-start | bytes 24584 | tf_op jit(solution)/shard_map/ppermute | solution.py:282
  38.6 13.7 %collective-permute-start.6 = (bf16[2,8,2,128]{3,2,1,0:T(2,128)(2,1)S(1)}, bf16[2,8,2,128]{3,2,1,0:T(2,128)(2,1)S(1)}, u32[]{:S(2)}, u32[]{:S(2)}) collective-permute-start(bf16[2,8,2,128]{3,2,1,0:T(2,128)(2,1)S(1)} %pad_maximum_fusion.refs_0_), channel_id=1, source_target_pairs={{0,4},{4,0},{8,12},{12,8},{1,5},{5,1},{9,13},{13,9},{2,6},{6,2},{1... | collective-permute-start | bytes 24584 | tf_op jit(solution)/shard_map/ppermute | solution.py:282
  39.7 12.7 %copy-start.2 = (bf16[2,256,128]{2,1,0:T(8,128)(2,1)S(1)}, bf16[2,256,128]{2,1,0:T(8,128)(2,1)}, u32[]{:S(2)}) copy-start(bf16[2,256,128]{2,1,0:T(8,128)(2,1)} %keys_ref.1) | copy-start | bytes 393220

commit v3 on v2

v3 whole, which is shorter than its diff:
```python
import functools

import jax
import jax.numpy as jnp
from jax import lax
from jax.experimental import pallas as pl
from jax.experimental.pallas import tpu as pltpu
from jax.sharding import PartitionSpec as P

D = 7168
KVLORA = 512
ROPE = 64
NOPE = 128
IHEADS = 64
IDIM = 128
BLK = 64
LANES = 128


epsilon = 1e-06
very_low = -1e30

SMEM = pl.BlockSpec(memory_space=pltpu.SMEM)
VMEM = pl.BlockSpec(memory_space=pltpu.VMEM)
HBM = pl.BlockSpec(memory_space=pltpu.HBM)
NT = (((1,), (1,)), ((), ()))


def shifted(size, step):
    return [(i, (i + step) % size) for i in range(size)]


def swapped(size, bit):
    return [(i, i ^ bit) for i in range(size)]


def limits(mib):
    return pltpu.CompilerParams(vmem_limit_bytes=mib << 20)


def cost(mib):
    return pl.CostEstimate(flops=0, bytes_accessed=mib << 20, transcendentals=0)


def in_hbm(array):
    return pltpu.with_memory_space_constraint(array, pltpu.HBM)


def in_vmem(array):
    return pltpu.with_memory_space_constraint(array, pltpu.VMEM)


def pick_blocks(place, blocks_ref, cache_ref, keep_ref, send_ref, tiles, sems):
    row = place[0]
    width = cache_ref.shape[1]
    count = tiles.shape[0]
    spot = []
    for slot in range(count):
        local = blocks_ref[row, lax.rem(slot + place[2] * (count // 2), count)] - place[1]
        owned = (local >= 0) & (local < cache_ref.shape[2] // BLK)
        local = jnp.where(owned, local, 0)
        begin = pl.multiple_of(local // 2 * LANES, LANES)
        copy = pltpu.make_async_copy(cache_ref.at[row, :, pl.ds(begin, LANES)], tiles.at[slot], sems.at[slot])
        copy.start()
        spot.append((copy, owned, (local % 2) != (slot % 2)))
    lane = lax.broadcasted_iota(jnp.int32, (width, LANES), 1)
    for pair in range(count // 2):
        total = jnp.zeros((width, LANES), jnp.float32)
        for side in range(2):
            copy, owned, swap = spot[2 * pair + side]
            copy.wait()
            tile = tiles[2 * pair + side].astype(jnp.float32)
            tile = jnp.where(swap, pltpu.roll(tile, BLK, 1), tile)
            total = jnp.where((lane // BLK == side) & owned, tile, total)
        out_ref = keep_ref if 4 * pair < count else send_ref
        begin = pair % (count // 4) * LANES
        out_ref[:, begin : begin + LANES] = total.astype(out_ref.dtype)


def prepare(
    sources, place, blocks_ref, lengths_ref, slot_ref, gate_ref, slots_ref, residual_ref, gain_ref, igate_ref, down_ref,
    base_ref, weight_ref, live_ref, limit_ref, gain_out_ref, igate_out_ref, down_out_ref, own, residual, sems,
):
    this, group = place[0], place[3]
    moved = (
        (down_ref, down_out_ref), (slots_ref.at[group], own), (residual_ref, residual), (gain_ref, gain_out_ref),
        (igate_ref, igate_out_ref),
    )
    moves = [pltpu.make_async_copy(source, target, sems.at[k]) for k, (source, target) in enumerate(moved)]
    for move in moves:
        move.start()
    rows = residual.shape[0]
    count = blocks_ref.shape[1]
    lane = lax.broadcasted_iota(jnp.int32, (1, live_ref.shape[1]), 1)
    for k, row in enumerate((this, 1 - this)):
        position = lane % BLK
        for slot in range(count):
            block = blocks_ref[row, lax.rem(slot + place[2] * (count // 2), count)]
            position = position + jnp.where(lane // BLK == slot, block * BLK, 0)
        live_ref[k : k + 1, :] = (position < lengths_ref[row]).astype(jnp.float32)
    position = place[4] + lax.broadcasted_iota(jnp.int32, (1, limit_ref.shape[1]), 1)
    for r in range(rows):
        limit_ref[r : r + 1, :] = (position < lengths_ref[r]).astype(jnp.float32)
    capacity = own.shape[0]
    spot = lax.broadcasted_iota(jnp.int32, (capacity, LANES), 0)
    weights = []
    for step in range(sources + 1):
        source = lax.rem(group + sources + 1 - step, sources + 1)
        for r in range(rows):
            weight = jnp.zeros(spot.shape, jnp.float32)
            for k in range(slot_ref.shape[1]):
                weight = jnp.where(spot == slot_ref[r, k] - source * capacity, gate_ref[r, k], weight)
            if step == 0:
                weights.append(weight[:, :1])
            else:
                weight_ref[step - 1, r] = weight
    for move in moves[1:]:
        move.wait()
    for r in range(rows):
        routed = jnp.sum(weights[r] * own[...].astype(jnp.float32), axis=0, keepdims=True)
        base_ref[r : r + 1, :] = residual[r : r + 1].astype(jnp.float32) + routed
    moves[0].wait()


def combine_down(
    sources, place, base_ref, weight_ref, gain_ref, igate_ref, down_ref, *refs
):
    received = refs[:sources]
    hidden_ref, part_ref = refs[sources:]
    rows = base_ref.shape[0]
    group = place[3]
    routed = [base_ref[r : r + 1, :] for r in range(rows)]
    for k, ref in enumerate(received):
        piece = ref[pl.ds(group, 1)][0].astype(jnp.float32)
        for r in range(rows):
            routed[r] = routed[r] + jnp.sum(weight_ref[k, r][:, :1] * piece, axis=0, keepdims=True)
    hidden = jnp.concatenate(routed, axis=0).astype(jnp.bfloat16)
    hidden_ref[...] = hidden
    widened = hidden.astype(jnp.float32)
    scaled = (widened * gain_ref[...].reshape(1, -1)).astype(jnp.bfloat16)
    qlora = down_ref.shape[1]
    squares = jnp.sum(widened * widened, axis=1, keepdims=True)
    part_ref[:, qlora + LANES :] = jnp.broadcast_to(squares, (rows, LANES))
    gates = lax.dot_general(scaled, igate_ref[...], NT, preferred_element_type=jnp.float32)
    part_ref[:, qlora : qlora + LANES] = jnp.concatenate([gates, gates], axis=1)
    part_ref[:, :qlora] = jnp.dot(scaled, down_ref[...], preferred_element_type=jnp.float32)


def project(chunk, begin, latent_ref, up_ref, absorb_ref, *refs):
    extra = (len(refs) - 5) // 3
    later = refs[:extra]
    absorbed, rotary = refs[extra : extra + 2]
    brought = refs[extra + 2 : 2 * extra + 2]
    turned, up, sems = refs[2 * extra + 2 : 2 * extra + 5]
    heads = turned.shape[0]
    rows, qlora = latent_ref.shape
    copies = []
    for k in range(heads // chunk):
        span = pl.ds(k * chunk, chunk)
        copies.append(pltpu.make_async_copy(up_ref.at[pl.ds(begin + k * chunk, chunk)], up.at[span], sems.at[k]))
        copies[-1].start()
    moves = []
    for k in range(extra):
        moves.append(pltpu.make_async_copy(later[k], brought[k], refs[2 * extra + 5 + k]))
        moves[-1].start()
    column = latent_ref[...].astype(jnp.float32)
    column = jnp.concatenate([column, jnp.zeros((LANES - rows, qlora), jnp.float32)], axis=0)
    column = jnp.transpose(column).astype(jnp.bfloat16)
    for k, copy in enumerate(copies):
        copy.wait()
        for n in range(k * chunk, (k + 1) * chunk):
            turned[n] = jnp.dot(up[n], column, preferred_element_type=jnp.float32)
    for n in range(heads):
        projected = jnp.transpose(turned[n])[:rows].astype(jnp.bfloat16)
        query = jnp.dot(projected[:, :NOPE], absorb_ref[begin + n], preferred_element_type=jnp.float32)
        for r in range(rows):
            absorbed[r, n : n + 1, :] = query[r : r + 1].astype(jnp.bfloat16).astype(jnp.float32)
            rotary[r, n : n + 1, :] = projected[r : r + 1, NOPE:].astype(jnp.float32)
    for move in moves:
        move.wait()


def attend(place, live_ref, *refs):
    parts = (len(refs) - 4) // 2
    absorbed, rotary = refs[:parts], refs[parts : 2 * parts]
    mine_ref, theirs_ref, value_ref, out_ref = refs[2 * parts :]
    heads = value_ref.shape[0]
    this = place[0]
    attended = []
    for k, (row, cache_ref) in enumerate(((this, mine_ref), (1 - this, theirs_ref))):
        live = live_ref[k : k + 1, :] > 0.0
        cache = cache_ref[...]
        content = jnp.concatenate([ref[pl.ds(row, 1)][0] for ref in absorbed], axis=0).astype(jnp.bfloat16)
        turn = jnp.concatenate([ref[pl.ds(row, 1)][0] for ref in rotary], axis=0).astype(jnp.bfloat16)
        logits = jnp.dot(content, cache[:KVLORA], preferred_element_type=jnp.float32) + jnp.dot(
            turn, cache[KVLORA:], preferred_element_type=jnp.float32
        )
        masked = jnp.where(live, logits * (NOPE + ROPE) ** -0.5, very_low)
        weights = jnp.where(live, jnp.exp(masked - jnp.max(masked, axis=1, keepdims=True)), 0.0)
        total = jnp.sum(weights, axis=1, keepdims=True)
        merged = lax.dot_general(
            weights.astype(jnp.bfloat16), cache[:KVLORA], NT, preferred_element_type=jnp.float32
        )
        attended.append(merged / total)
    attended = jnp.concatenate(attended, axis=0).astype(jnp.bfloat16)
    head = lax.broadcasted_iota(jnp.int32, (2 * heads, value_ref.shape[2]), 0) % heads
    result = jnp.zeros(head.shape, jnp.float32)
    for n in range(heads):
        product = jnp.dot(attended, value_ref[n], preferred_element_type=jnp.float32)
        result = jnp.where(head == n, product, result)
    for k, row in enumerate((this, 1 - this)):
        out_ref[pl.ds(row, 1)] = result[k * heads : (k + 1) * heads].astype(out_ref.dtype)[None]


def score(pieces, place, limit_ref, gates_ref, keys_ref, *refs):
    gathered = refs[:pieces]
    out_ref, queries = refs[pieces:]
    heads = gathered[0].shape[1]
    order = lax.broadcasted_iota(jnp.int32, (IHEADS, IHEADS), 0)
    head = order
    rows = out_ref.shape[0]
    for k, ref in enumerate(gathered):
        for side in range(2):
            spot = 2 * k + side
            begin = place[5 + k] + jnp.where(place[0] == side, 0, heads)
            head = jnp.where(order // heads == spot, begin + order % heads, head)
            for r in range(rows):
                queries[r, spot * heads : (spot + 1) * heads, :] = ref[side, :, r, :].astype(jnp.float32)
    for r in range(rows):
        logits = lax.dot_general(
            queries[r].astype(jnp.bfloat16), keys_ref[r], NT, preferred_element_type=jnp.float32
        )
        gates = jnp.where(lax.broadcasted_iota(jnp.int32, head.shape, 1) == head, gates_ref[r : r + 1, :], 0.0)
        gates = jnp.sum(gates, axis=1, keepdims=True)
        raw = jnp.sum(gates * jnp.maximum(logits, 0.0), axis=0, keepdims=True)
        out_ref[r : r + 1, :] = jnp.where(limit_ref[r : r + 1, :] > 0.0, raw, 0.0)


def local(
    residual,
    expert_out,
    combine_slot,
    combine_gate,
    attn_gain,
    query_down,
    index_gate,
    latent_gain,
    query_up,
    key_absorb,
    index_query,
    value_up,
    latent_cache,
    index_keys,
    lengths,
    block_list,
):
    n_ctx, n_dp, n_hp = (lax.axis_size(name) for name in ("ctx", "dp", "hp"))
    c, d, h = (lax.axis_index(name) for name in ("ctx", "dp", "hp"))
    rows, features = residual.shape
    qlora = query_down.shape[1]
    selected = block_list.shape[1]
    span, width = latent_cache.shape[1:]
    heads = value_up.shape[0]
    f32, bf16 = jnp.float32, jnp.bfloat16

    slots = expert_out[0]
    received = [lax.ppermute(slots, "dp", shifted(n_dp, step)) for step in range(1, n_dp)]

    index_heads, index_span = index_query.shape[1], index_keys.shape[1]
    sources = [jnp.bitwise_xor(c, step) * n_hp * index_heads for step in range(n_ctx)]
    scalars = [h, c * (span // BLK), c % 2, d, (c * n_hp + h) * index_span, *sources]
    place = in_vmem(jnp.stack(scalars).astype(jnp.int32))
    half = pltpu.VMEM((width, selected // 2 * BLK), bf16)
    mine, send = pl.pallas_call(
        pick_blocks,
        out_shape=(half, half),
        in_specs=[SMEM, SMEM, HBM],
        out_specs=(VMEM, VMEM),
        scratch_shapes=[pltpu.VMEM((selected, width, LANES), bf16), pltpu.SemaphoreType.DMA((selected,))],
        compiler_params=limits(6),
        name="pick_blocks",
    )(place, in_hbm(block_list), in_hbm(jnp.swapaxes(latent_cache, 1, 2)))
    upper, lower = (lax.ppermute(x, "ctx", swapped(n_ctx, 1)) for x in (send[: width // 2], send[width // 2 :]))
    mine, residual = lax.optimization_barrier((mine, residual))
    *ready, live, limit, gain, igate, down = pl.pallas_call(
        functools.partial(prepare, len(received)),
        out_shape=(
            pltpu.VMEM((rows, features), f32),
            pltpu.VMEM((len(received), rows, slots.shape[1], LANES), f32),
            pltpu.VMEM((rows, selected * BLK), f32),
            pltpu.VMEM((rows, index_span), f32),
            pltpu.VMEM(attn_gain.shape, f32),
            pltpu.VMEM(index_gate.shape[::-1], bf16),
            pltpu.VMEM(query_down.shape, bf16),
        ),
        in_specs=[SMEM] * 5 + [HBM] * 5,
        out_specs=(VMEM,) * 7,
        scratch_shapes=[
            pltpu.VMEM(slots.shape[1:], bf16),
            pltpu.VMEM(residual.shape, bf16),
            pltpu.SemaphoreType.DMA((5,)),
        ],
        compiler_params=limits(4),
        name="prepare",
    )(
        place,
        *map(in_hbm, (block_list, lengths, combine_slot, combine_gate)),
        *map(in_hbm, (slots, residual, attn_gain, index_gate.T, query_down)),
    )
    ready = [*ready, gain, igate, down]
    received, ready = lax.optimization_barrier((received, ready))

    hidden, part = pl.pallas_call(
        functools.partial(combine_down, len(received)),
        out_shape=(
            jax.ShapeDtypeStruct((rows, features), bf16),
            pltpu.VMEM((rows, qlora + 2 * LANES), f32),
        ),
        in_specs=[SMEM] + [VMEM] * (5 + len(received)),
        out_specs=(VMEM, VMEM),
        compiler_params=limits(8),
        cost_estimate=cost(10),
        name="combine_down",
    )(place, *map(in_vmem, ready), *received)

    mine, upper, lower, part = lax.optimization_barrier((mine, upper, lower, part))
    mine = mine + jnp.concatenate([upper, lower], axis=0)
    mine, part = lax.optimization_barrier((mine, part))
    crossed = [lax.ppermute(mine, "ctx", swapped(n_ctx, 2))]

    parts = [part] + [lax.ppermute(part, "ctx", swapped(n_ctx, step)) for step in range(1, n_ctx)]
    total = functools.reduce(jnp.add, parts)
    scale = lax.rsqrt(total[:, qlora + LANES : qlora + LANES + 1] / D + epsilon)
    latent_sum = total[:, :qlora] * scale
    head_gate = total[:, qlora : qlora + IHEADS] * (scale * IHEADS**-0.5 * IDIM**-0.5)
    latent_scale = lax.rsqrt(jnp.mean(latent_sum * latent_sum, axis=-1, keepdims=True) + epsilon)
    latent = (latent_sum * latent_scale * latent_gain).astype(bf16)

    index_local = jnp.einsum("rq,qnd->nrd", latent, index_query, preferred_element_type=f32).astype(bf16)
    index_other = lax.ppermute(index_local, "hp", swapped(n_hp, 1))
    index_pair = jnp.stack([index_local, index_other])
    gathered = [index_pair] + [lax.ppermute(index_pair, "ctx", swapped(n_ctx, step)) for step in range(1, n_ctx)]

    def project_part(begin, count, latent, later):
        group = 2 if count % 2 == 0 else 1
        return pl.pallas_call(
            functools.partial(project, group, begin),
            out_shape=(
                pltpu.VMEM((rows, count, KVLORA), f32),
                pltpu.VMEM((rows, count, ROPE), f32),
                *(pltpu.VMEM(array.shape, array.dtype) for array in later),
            ),
            in_specs=[VMEM, HBM, VMEM] + [HBM] * len(later),
            out_specs=(VMEM,) * (2 + len(later)),
            scratch_shapes=[
                pltpu.VMEM((count, query_up.shape[2], LANES), f32),
                pltpu.VMEM((count, query_up.shape[2], qlora), bf16),
                pltpu.SemaphoreType.DMA((count // group,)),
                *(pltpu.SemaphoreType.DMA for _ in later),
            ],
            compiler_params=limits(10),
            name="project",
        )(in_vmem(latent), in_hbm(jnp.transpose(query_up, (1, 2, 0))), in_vmem(key_absorb), *map(in_hbm, later))

    lead = max(1, heads * 3 // 4)
    latent, index_pair = lax.optimization_barrier((latent, index_pair))
    first = project_part(0, lead, latent, ())
    first, mine, crossed, gathered = lax.optimization_barrier((first, mine, crossed, gathered))
    mine = functools.reduce(jnp.add, crossed, mine)
    bit = 4
    while bit < n_ctx:
        mine = mine + lax.ppermute(mine, "ctx", swapped(n_ctx, bit))
        bit *= 2
    mine, latent = lax.optimization_barrier((mine, latent))
    other = lax.ppermute(mine, "ctx", swapped(n_ctx, 1))
    *second, value, keys = project_part(lead, heads - lead, latent, (value_up, index_keys))
    second, mine, other = lax.optimization_barrier((second, mine, other))
    mine = jnp.concatenate([mine, other], axis=1)
    theirs = lax.ppermute(mine, "hp", swapped(n_hp, 1))
    index_scores = pl.pallas_call(
        functools.partial(score, n_ctx),
        out_shape=jax.ShapeDtypeStruct((rows, index_span), f32),
        in_specs=[SMEM] + [VMEM] * (3 + n_ctx),
        out_specs=VMEM,
        scratch_shapes=[pltpu.VMEM((rows, IHEADS, IDIM), f32)],
        compiler_params=limits(4),
        cost_estimate=cost(2),
        name="score",
    )(place, *map(in_vmem, (limit, head_gate, keys, *gathered)))

    index_scores, mine = lax.optimization_barrier((index_scores, mine))
    attn_out = pl.pallas_call(
        attend,
        out_shape=jax.ShapeDtypeStruct((rows, heads, value_up.shape[2]), bf16),
        in_specs=[SMEM] + [VMEM] * 8,
        out_specs=VMEM,
        compiler_params=limits(8),
        name="attend",
    )(place, *map(in_vmem, (live, first[0], second[0], first[1], second[1], mine, theirs, value)))
    return (hidden, index_scores, attn_out)


def solution(mesh):
    placed = (
        P(("groups", "dp"), "ctx"),
        P(("groups", "dp"), None, None, "ctx"),
        P(("groups", "dp"), None),
        P(("groups", "dp"), None),
        P("ctx"),
        P("ctx", None),
        P("ctx", None),
        P(),
        P(None, ("ctx", "hp"), None),
        P(("ctx", "hp"), None, None),
        P(None, ("ctx", "hp"), None),
        P(("ctx", "hp"), None, None),
        P(("groups", "dp"), "ctx", None),
        P(("groups", "dp"), ("ctx", "hp"), None),
        P(("groups", "dp")),
        P(("groups", "dp"), None),
    )
    return jax.shard_map(
        local,
        mesh=mesh,
        in_specs=placed,
        out_specs=(
            P(("groups", "dp"), "ctx"),
            P(("groups", "dp"), ("ctx", "hp")),
            P(("groups", "dp"), ("ctx", "hp"), None),
        ),
        check_vma=False,
    )
```

time: 54.6 us -> 42.7 us (0.78); the launches traced: 53.7 us -> 42.4 us
  starting transfers between devices: 23.2 us -> 19.6 us
  waiting for transfers between devices: 6.95 us -> 3.54 us
  Pallas kernels: 19.5 us -> 17.2 us
  other arithmetic: 1.72 us -> 0.62 us
  local copies, waits for them, and re-layouts: 0.98 us -> 0.18 us
    pallas_call x1, Pallas kernels: 12.6 us -> 2.04 us  [local(): pl.pallas_call(attend, out_shape=jax.ShapeDtypeStruct((rows, heads, value...]
    pallas_call x1 -> x4, Pallas kernels: 3.55 us -> 12.3 us  [the longest x2 6.66 us: project_part(): pl.pallas_call(functools.partial(project, group, begin), out_shape=(pltpu...]
    ppermute x6 -> x8, starting transfers between devices: 16.6 us -> 11.4 us  [the longest x1 4.08 us: local(): index_other = lax.ppermute(index_local, 'hp', swapped(n_hp, 1))]
    ppermute x1, waiting for transfers between devices: 2.71 us -> 0.01 us  [local(): lax.ppermute(slots, 'dp', shifted(n_dp, step))]
    add x3, other arithmetic: 1.13 us -> 0.1 us  [the longest x1 0.04 us: local(): mine = mine + jnp.concatenate([upper, lower], axis=0)]
    ppermute x1, starting transfers between devices: 1.21 us -> 2.11 us  [local(): lax.ppermute(slots, 'dp', shifted(n_dp, step))]
    unnamed x24 -> x7, local copies, waits for them, and re-layouts: 0.89 us -> 0.05 us
    ppermute x6 -> x8, waiting for transfers between devices: 4.23 us -> 3.53 us  [the longest x1 1.59 us: local(): other = lax.ppermute(mine, 'ctx', swapped(n_ctx, 1))]
  transfers between devices with their start and end apart: 11 -> 13, of which waited for: 4 -> 3; matrix products, arithmetic and copies ran while one was open for 4% -> 3% of each run, Pallas kernels for 27% -> 36%
where the time goes in v3:
time: 42.7 us; the launch traced here: 42.4 us
  starting transfers between devices  19.6 us (46%)
  Pallas kernels  17.2 us (40%)
  waiting for transfers between devices  3.54 us (8%)
  between operations  0.83 us (2%)
  other arithmetic  0.62 us (1%)
  matrix products  0.52 us (1%)
    pallas_call x2, Pallas kernels, project_part(): pl.pallas_call(functools.partial(project, group, begin), out_shape=(pltpu...  6.66 us
    ppermute x1, starting transfers between devices, local(): index_other = lax.ppermute(index_local, 'hp', swapped(n_hp, 1))  4.08 us
    ppermute x3, starting transfers between devices, local(): lax.ppermute(part, 'ctx', swapped(n_ctx, step))  3.75 us
    ppermute x3, starting transfers between devices, local(): lax.ppermute(index_pair, 'ctx', swapped(n_ctx, step))  3.61 us
    pallas_call x1, Pallas kernels, local(): pl.pallas_call(functools.partial(prepare, len(received)), out_shape=(pltp...  3.5 us
    ppermute x1, starting transfers between devices, local(): theirs = lax.ppermute(mine, 'hp', swapped(n_hp, 1))  2.39 us
    pallas_call x1, Pallas kernels, local(): pl.pallas_call(pick_blocks, out_shape=(half, half), in_specs=[SMEM, SMEM,...  2.13 us
    ppermute x1, starting transfers between devices, local(): lax.ppermute(slots, 'dp', shifted(n_dp, step))  2.11 us
  transfers between devices with their start and end apart: 13, of which 3 were waited for; matrix products, arithmetic and copies ran while one was open for 3% of the time, Pallas kernels for 36%

profile of v3, /device:TPU:1, one launch (start us, length us, event | category | flops | bytes accessed | tf_op | source)
XLA Modules:
  0.0 42.4 jit_solution(14739336399335783383)
XLA Ops:
  0.6 2.1 %collective-permute-start = (bf16[2,16,1792]{2,1,0:T(8,128)(2,1)}, bf16[2,16,1792]{2,1,0:T(8,128)(2,1)S(1)}, u32[]{:S(2)}, u32[]{:S(2)}) collective-permute-start(bf16[2,16,1792]{2,1,0:T(8,128)(2,1)} %bitcast.24), channel_id=1, source_target_pairs={{0,2},{2,0},{1,3},{3,1},{4,6},{6,4},{5,7},{7,5},{8,10},{10,8},{9,1... | collective-permute-start | bytes 344072 | tf_op jit(solution)/shard_map/ppermute | solution.py:267
  2.8 2.1 %pick_blocks.1 = (bf16[576,128]{1,0:T(8,128)(2,1)S(1)}, bf16[576,128]{1,0:T(8,128)(2,1)S(1)}) custom-call(s32[9]{0:T(128)S(1)} %stack.48.place, s32[2,4]{1,0:T(2,128)} %blocks_ref.3, bf16[2,576,512]{2,1,0:T(8,128)(2,1)} %bitcast.22), custom_call_target="tpu_custom_call" | custom-call | tf_op jit(solution)/shard_map/pick_blocks/pallas_call | solution.py:274
  5.0 1.4 %collective-permute-start.2 = (bf16[288,128]{1,0:T(8,128)(2,1)S(1)}, bf16[288,128]{1,0:T(8,128)(2,1)S(1)}, u32[]{:S(2)}, u32[]{:S(2)}) collective-permute-start(bf16[288,128]{1,0:T(8,128)(2,1)S(1)} %get-tuple-element.101), channel_id=1, source_target_pairs={{0,4},{4,0},{8,12},{12,8},{1,5},{5,1},{9,13},{13,9},{2,6},{6,2},{1... | collective-permute-start | bytes 221192 | tf_op jit(solution)/shard_map/ppermute | solution.py:283
  6.4 0.2 collective-permute-start.1
  6.5 3.5 %prepare.1 = (f32[2,1792]{1,0:T(2,128)S(1)}, f32[1,2,16,128]{3,2,1,0:T(8,128)S(1)}, f32[2,256]{1,0:T(2,128)S(1)}, f32[2,256]{1,0:T(2,128)S(1)}, f32[1792]{0:T(10...) custom-call(s32[9]{0:T(128)S(1)} %stack.48.place, s32[2,4]{1,0:T(2,128)} %blocks_ref.3, ...), custom_call_target="tpu_custom_call" | custom-call | tf_op jit(solution)/shard_map/prepare/pallas_call | solution.py:285
  10.0 1.5 %combine_down.1 = (bf16[2,1792]{1,0:T(2,128)(2,1)}, f32[2,1792]{1,0:T(2,128)S(1)}) custom-call(s32[9]{0:T(128)S(1)} %stack.48.place, f32[2,1792]{1,0:T(2,128)S(1)} %get-tuple-element.58.base_ref, f32[1,2,16,128]{3,2,1,0:T(8,128)S(1)} %get-tuple-element.59.weight_ref, f32[1792]{0:T(1024)S(1)} %get-tuple-element.60.gain_ref, ...), custom_call_target="tpu_custom_call" | custom-call | bytes 10485760 | tf_op jit(solution)/shard_map/combine_down/pallas_call | solution.py:313
  11.7 3.4 %collective-permute-start.5 = (f32[2,1792]{1,0:T(2,128)S(1)}, f32[2,1792]{1,0:T(2,128)S(1)}, u32[]{:S(2)}, u32[]{:S(2)}) collective-permute-start(f32[2,1792]{1,0:T(2,128)S(1)} %get-tuple-element.73), channel_id=1, source_target_pairs={{0,12},{4,8},{8,4},{12,0},{1,13},{5,9},{9,5},{13,1},{2,14},{6,10},... | collective-permute-start | bytes 43016 | tf_op jit(solution)/shard_map/ppermute | solution.py:331
  15.0 0.4 collective-permute-start.3
  15.4 2.0 %collective-permute-start.7 = (bf16[576,128]{1,0:T(8,128)(2,1)S(1)}, bf16[576,128]{1,0:T(8,128)(2,1)S(1)}, u32[]{:S(2)}, u32[]{:S(2)}) collective-permute-start(bf16[576,128]{1,0:T(8,128)(2,1)S(1)} %maximum_add_fusion), channel_id=1, source_target_pairs={{0,8},{4,12},{8,0},{12,4},{1,9},{5,13},{9,1},{13,5},{2,10},{6,14},... | collective-permute-start | bytes 442376 | tf_op jit(solution)/shard_map/ppermute | solution.py:329
  17.4 1.1 %collective-permute-done.4 = f32[2,1792]{1,0:T(2,128)S(1)} collective-permute-done((f32[2,1792]{1,0:T(2,128)S(1)}, f32[2,1792]{1,0:T(2,128)S(1)}, u32[]{:S(2)}, u32[]{:S(2)}) %collective-permute-start.4) | collective-permute-done | bytes 14368 | tf_op jit(solution)/shard_map/ppermute | solution.py:331
  18.5 0.2 fusion.8
  18.7 0.2 multiply_reduce_fusion
  19.0 0.5 %fusion.2 = bf16[2,8,128]{2,0,1:T(2,128)(2,1)S(1)} fusion(bf16[1536,8,128]{2,1,0:T(8,128)(2,1)S(1)} %copy-done, bf16[2,1536]{1,0:T(2,128)(2,1)S(1)} %multiply_convert_fusion.latent_ref), kind=kOutput, calls=%fused_computation.2 | convolution fusion | flops 6293504 | bytes 3155968 | tf_op jit(solution)/shard_map/rq,qnd->nrd/dot_general | solution.py:339
  19.5 4.1 %collective-permute-start.6 = (bf16[8,2,128]{2,1,0:T(2,128)(2,1)S(1)}, bf16[8,2,128]{2,1,0:T(2,128)(2,1)S(1)}, u32[]{:S(2)}, u32[]{:S(2)}) collective-permute-start(bf16[8,2,128]{2,1,0:T(2,128)(2,1)S(1)} %bitcast.26), channel_id=1, source_target_pairs={{0,1},{1,0},{2,3},{3,2},{4,5},{5,4},{6,7},{7,6},{8,9},{9,8},{10,11... | collective-permute-start | bytes 12296 | tf_op jit(solution)/shard_map/ppermute | solution.py:340
  23.6 0.8 %collective-permute-done.6 = bf16[8,2,128]{2,1,0:T(2,128)(2,1)S(1)} collective-permute-done((bf16[8,2,128]{2,1,0:T(2,128)(2,1)S(1)}, bf16[8,2,128]{2,1,0:T(2,128)(2,1)S(1)}, u32[]{:S(2)}, u32[]{:S(2)}) %collective-permute-start.6) | collective-permute-done | bytes 4128 | tf_op jit(solution)/shard_map/ppermute | solution.py:340
  24.4 0.1 collective-permute-start.10
  24.5 0.6 %collective-permute-start.9 = (bf16[2,8,2,128]{3,2,1,0:T(2,128)(2,1)S(1)}, bf16[2,8,2,128]{3,2,1,0:T(2,128)(2,1)S(1)}, u32[]{:S(2)}, u32[]{:S(2)}) collective-permute-start(bf16[2,8,2,128]{3,2,1,0:T(2,128)(2,1)S(1)} %pad_maximum_fusion.refs_0_), channel_id=1, source_target_pairs={{0,8},{4,12},{8,0},{12,4},{1,9},{5,13},{9,1},{13,5},{2,10},{6,14},... | collective-permute-start | bytes 24584 | tf_op jit(solution)/shard_map/ppermute | solution.py:342
  25.2 2.9 %collective-permute-start.8 = (bf16[2,8,2,128]{3,2,1,0:T(2,128)(2,1)S(1)}, bf16[2,8,2,128]{3,2,1,0:T(2,128)(2,1)S(1)}, u32[]{:S(2)}, u32[]{:S(2)}) collective-permute-start(bf16[2,8,2,128]{3,2,1,0:T(2,128)(2,1)S(1)} %pad_maximum_fusion.refs_0_), channel_id=1, source_target_pairs={{0,4},{4,0},{8,12},{12,8},{1,5},{5,1},{9,13},{13,9},{2,6},{6,2},{1... | collective-permute-start | bytes 24584 | tf_op jit(solution)/shard_map/ppermute | solution.py:342
  28.1 4.3 %project.2 = (f32[2,12,512]{2,1,0:T(8,128)S(1)}, f32[2,12,64]{2,1,0:T(8,128)S(1)}) custom-call(bf16[2,1536]{1,0:T(2,128)(2,1)S(1)} %multiply_convert_fusion.latent_ref, bf16[16,192,1536]{2,1,0:T(8,128)(2,1)} %bitcast.20, bf16[16,128,512]{2,1,0:T(8,128)(2,1)S(1)} %copy-done.1), custom_call_target="tpu_custom_call" | custom-call | tf_op jit(solution)/shard_map/project/pallas_call | solution.py:346
  32.5 2.4 %project.3 = (f32[2,4,512]{2,1,0:T(4,128)S(1)}, f32[2,4,64]{2,1,0:T(4,128)S(1)}, bf16[16,512,128]{2,1,0:T(8,128)(2,1)S(1)}, bf16[2,256,128]{2,1,0:T(8,128)(2,1)S(1)}) custom-call(bf16[2,1536]{1,0:T(2,128)(2,1)S(1)} %multiply_convert_fusion.latent_ref, bf16[16,192,1536]{2,1,0:T(8,128)(2,1)} %bitcast.21, bf16[16,128,512]{2,1,0:T(8,128)(2,1)S(1)} %copy-done.1, ...), custom_call_target="tpu_custom_call" | custom-call | tf_op jit(solution)/shard_map/project/pallas_call | solution.py:346
  34.9 1.6 %collective-permute-done.11 = bf16[576,128]{1,0:T(8,128)(2,1)S(1)} collective-permute-done((bf16[576,128]{1,0:T(8,128)(2,1)S(1)}, bf16[576,128]{1,0:T(8,128)(2,1)S(1)}, u32[]{:S(2)}, u32[]{:S(2)}) %collective-permute-start.11) | collective-permute-done | bytes 147488 | tf_op jit(solution)/shard_map/ppermute | solution.py:375
  36.6 2.4 %collective-permute-start.12 = (bf16[576,256]{1,0:T(8,128)(2,1)S(1)}, bf16[576,256]{1,0:T(8,128)(2,1)S(1)}, u32[]{:S(2)}, u32[]{:S(2)}) collective-permute-start(bf16[576,256]{1,0:T(8,128)(2,1)S(1)} %constant_dynamic-update-slice_fusion.refs_4_), channel_id=1, source_target_pairs={{0,1},{1,0},{2,3},{3,2},{4,5},{5,4},{6,7},{7,6},{8,9},{9,8},{10,11... | collective-permute-start | bytes 884744 | tf_op jit(solution)/shard_map/ppermute | solution.py:379
  39.0 1.3 %score.1 = f32[2,256]{1,0:T(2,128)} custom-call(s32[9]{0:T(128)S(1)} %stack.48.place, f32[2,256]{1,0:T(2,128)S(1)} %get-tuple-element.65.limit_ref, f32[2,64]{1,0:T(2,128)S(1)} %slice_multiply_fusion.2.gates_ref, bf16[2,256,128]{2,1,0:T(8,128)(2,1)S(1)} %get-tuple-element.81.keys_ref, bf16[2,8,2,128]{3,2,1,0:T(2,128)(2,1)S(1)} %pad_maximum_fusion.refs_0_, ...), custom_call_target="tpu_custom_call" | custom-call | bytes 2097152 | tf_op jit(solution)/shard_map/score/pallas_call | solution.py:380
  40.4 2.0 %attend.1 = bf16[2,16,128]{2,1,0:T(8,128)(2,1)} custom-call(s32[9]{0:T(128)S(1)} %stack.48.place, f32[2,256]{1,0:T(2,128)S(1)} %get-tuple-element.92.live_ref, f32[2,12,512]{2,1,0:T(8,128)S(1)} %get-tuple-element.93.refs_0_, f32[2,4,512]{2,1,0:T(4,128)S(1)} %get-tuple-element.94.refs_1_, f32[2,12,64]{2,1,0:T(8,128)S(1)} %get-tuple-element.95.refs_2_, ...), custom_call_target="tpu_custom_call" | custom-call | tf_op jit(solution)/shard_map/attend/pallas_call | solution.py:392
  (29 shorter events, 0.6 us)
Async XLA Ops:
  0.6 18.4 %copy-start = (bf16[1536,8,128]{2,1,0:T(8,128)(2,1)S(1)}, bf16[1536,8,128]{2,1,0:T(8,128)(2,1)}, u32[]{:S(2)}) copy-start(bf16[1536,8,128]{2,1,0:T(8,128)(2,1)} %param.26) | copy-start | bytes 9437188
  0.6 9.4 %collective-permute-start = (bf16[2,16,1792]{2,1,0:T(8,128)(2,1)}, bf16[2,16,1792]{2,1,0:T(8,128)(2,1)S(1)}, u32[]{:S(2)}, u32[]{:S(2)}) collective-permute-start(bf16[2,16,1792]{2,1,0:T(8,128)(2,1)} %bitcast.24), channel_id=1, source_target_pairs={{0,2},{2,0},{1,3},{3,1},{4,6},{6,4},{5,7},{7,5},{8,10},{10,8},{9,1... | collective-permute-start | bytes 344072 | tf_op jit(solution)/shard_map/ppermute | solution.py:267
  5.0 6.6 %collective-permute-start.2 = (bf16[288,128]{1,0:T(8,128)(2,1)S(1)}, bf16[288,128]{1,0:T(8,128)(2,1)S(1)}, u32[]{:S(2)}, u32[]{:S(2)}) collective-permute-start(bf16[288,128]{1,0:T(8,128)(2,1)S(1)} %get-tuple-element.101), channel_id=1, source_target_pairs={{0,4},{4,0},{8,12},{12,8},{1,5},{5,1},{9,13},{13,9},{2,6},{6,2},{1... | collective-permute-start | bytes 221192 | tf_op jit(solution)/shard_map/ppermute | solution.py:283
  6.4 5.2 %collective-permute-start.1 = (bf16[288,128]{1,0:T(8,128)(2,1)S(1)}, bf16[288,128]{1,0:T(8,128)(2,1)S(1)}, u32[]{:S(2)}, u32[]{:S(2)}) collective-permute-start(bf16[288,128]{1,0:T(8,128)(2,1)S(1)} %get-tuple-element.102), channel_id=1, source_target_pairs={{0,4},{4,0},{8,12},{12,8},{1,5},{5,1},{9,13},{13,9},{2,6},{6,2},{1... | collective-permute-start | bytes 221192 | tf_op jit(solution)/shard_map/ppermute | solution.py:283
  10.0 8.8 %copy-start.2 = (f32[1536]{0:T(1024)S(1)}, f32[1536]{0:T(1024)}, u32[]{:S(2)}) copy-start(f32[1536]{0:T(1024)} %param.23) | copy-start | bytes 18436
  11.6 16.5 %copy-start.1 = (bf16[16,128,512]{2,1,0:T(8,128)(2,1)S(1)}, bf16[16,128,512]{2,1,0:T(8,128)(2,1)}, u32[]{:S(2)}) copy-start(bf16[16,128,512]{2,1,0:T(8,128)(2,1)} %absorb_ref.3) | copy-start | bytes 6291460
  11.7 5.8 %collective-permute-start.5 = (f32[2,1792]{1,0:T(2,128)S(1)}, f32[2,1792]{1,0:T(2,128)S(1)}, u32[]{:S(2)}, u32[]{:S(2)}) collective-permute-start(f32[2,1792]{1,0:T(2,128)S(1)} %get-tuple-element.73), channel_id=1, source_target_pairs={{0,12},{4,8},{8,4},{12,0},{1,13},{5,9},{9,5},{13,1},{2,14},{6,10},... | collective-permute-start | bytes 43016 | tf_op jit(solution)/shard_map/ppermute | solution.py:331
  15.0 3.5 %collective-permute-start.4 = (f32[2,1792]{1,0:T(2,128)S(1)}, f32[2,1792]{1,0:T(2,128)S(1)}, u32[]{:S(2)}, u32[]{:S(2)}) collective-permute-start(f32[2,1792]{1,0:T(2,128)S(1)} %get-tuple-element.73), channel_id=1, source_target_pairs={{0,8},{4,12},{8,0},{12,4},{1,9},{5,13},{9,1},{13,5},{2,10},{6,14},... | collective-permute-start | bytes 43016 | tf_op jit(solution)/shard_map/ppermute | solution.py:331
  15.0 3.5 %collective-permute-start.3 = (f32[2,1792]{1,0:T(2,128)S(1)}, f32[2,1792]{1,0:T(2,128)S(1)}, u32[]{:S(2)}, u32[]{:S(2)}) collective-permute-start(f32[2,1792]{1,0:T(2,128)S(1)} %get-tuple-element.73), channel_id=1, source_target_pairs={{0,4},{4,0},{8,12},{12,8},{1,5},{5,1},{9,13},{13,9},{2,6},{6,2},{1... | collective-permute-start | bytes 43016 | tf_op jit(solution)/shard_map/ppermute | solution.py:331
  15.4 17.0 %collective-permute-start.7 = (bf16[576,128]{1,0:T(8,128)(2,1)S(1)}, bf16[576,128]{1,0:T(8,128)(2,1)S(1)}, u32[]{:S(2)}, u32[]{:S(2)}) collective-permute-start(bf16[576,128]{1,0:T(8,128)(2,1)S(1)} %maximum_add_fusion), channel_id=1, source_target_pairs={{0,8},{4,12},{8,0},{12,4},{1,9},{5,13},{9,1},{13,5},{2,10},{6,14},... | collective-permute-start | bytes 442376 | tf_op jit(solution)/shard_map/ppermute | solution.py:329
  19.5 4.9 %collective-permute-start.6 = (bf16[8,2,128]{2,1,0:T(2,128)(2,1)S(1)}, bf16[8,2,128]{2,1,0:T(2,128)(2,1)S(1)}, u32[]{:S(2)}, u32[]{:S(2)}) collective-permute-start(bf16[8,2,128]{2,1,0:T(2,128)(2,1)S(1)} %bitcast.26), channel_id=1, source_target_pairs={{0,1},{1,0},{2,3},{3,2},{4,5},{5,4},{6,7},{7,6},{8,9},{9,8},{10,11... | collective-permute-start | bytes 12296 | tf_op jit(solution)/shard_map/ppermute | solution.py:340
  24.4 7.9 %collective-permute-start.10 = (bf16[2,8,2,128]{3,2,1,0:T(2,128)(2,1)S(1)}, bf16[2,8,2,128]{3,2,1,0:T(2,128)(2,1)S(1)}, u32[]{:S(2)}, u32[]{:S(2)}) collective-permute-start(bf16[2,8,2,128]{3,2,1,0:T(2,128)(2,1)S(1)} %pad_maximum_fusion.refs_0_), channel_id=1, source_target_pairs={{0,12},{4,8},{8,4},{12,0},{1,13},{5,9},{9,5},{13,1},{2,14},{6,10},... | collective-permute-start | bytes 24584 | tf_op jit(solution)/shard_map/ppermute | solution.py:342
  24.5 7.8 %collective-permute-start.9 = (bf16[2,8,2,128]{3,2,1,0:T(2,128)(2,1)S(1)}, bf16[2,8,2,128]{3,2,1,0:T(2,128)(2,1)S(1)}, u32[]{:S(2)}, u32[]{:S(2)}) collective-permute-start(bf16[2,8,2,128]{3,2,1,0:T(2,128)(2,1)S(1)} %pad_maximum_fusion.refs_0_), channel_id=1, source_target_pairs={{0,8},{4,12},{8,0},{12,4},{1,9},{5,13},{9,1},{13,5},{2,10},{6,14},... | collective-permute-start | bytes 24584 | tf_op jit(solution)/shard_map/ppermute | solution.py:342
  25.2 7.2 %collective-permute-start.8 = (bf16[2,8,2,128]{3,2,1,0:T(2,128)(2,1)S(1)}, bf16[2,8,2,128]{3,2,1,0:T(2,128)(2,1)S(1)}, u32[]{:S(2)}, u32[]{:S(2)}) collective-permute-start(bf16[2,8,2,128]{3,2,1,0:T(2,128)(2,1)S(1)} %pad_maximum_fusion.refs_0_), channel_id=1, source_target_pairs={{0,4},{4,0},{8,12},{12,8},{1,5},{5,1},{9,13},{13,9},{2,6},{6,2},{1... | collective-permute-start | bytes 24584 | tf_op jit(solution)/shard_map/ppermute | solution.py:342
  32.4 4.1 %collective-permute-start.11 = (bf16[576,128]{1,0:T(8,128)(2,1)S(1)}, bf16[576,128]{1,0:T(8,128)(2,1)S(1)}, u32[]{:S(2)}, u32[]{:S(2)}) collective-permute-start(bf16[576,128]{1,0:T(8,128)(2,1)S(1)} %add.41), channel_id=1, source_target_pairs={{0,4},{4,0},{8,12},{12,8},{1,5},{5,1},{9,13},{13,9},{2,6},{6,2},{1... | collective-permute-start | bytes 442376 | tf_op jit(solution)/shard_map/ppermute | solution.py:375
  36.6 3.8 %collective-permute-start.12 = (bf16[576,256]{1,0:T(8,128)(2,1)S(1)}, bf16[576,256]{1,0:T(8,128)(2,1)S(1)}, u32[]{:S(2)}, u32[]{:S(2)}) collective-permute-start(bf16[576,256]{1,0:T(8,128)(2,1)S(1)} %constant_dynamic-update-slice_fusion.refs_4_), channel_id=1, source_target_pairs={{0,1},{1,0},{2,3},{3,2},{4,5},{5,4},{6,7},{7,6},{8,9},{9,8},{10,11... | collective-permute-start | bytes 884744 | tf_op jit(solution)/shard_map/ppermute | solution.py:379

commit v4 on v3

v4 whole, which is shorter than its diff:
```python
import functools

import jax
import jax.numpy as jnp
from jax import lax
from jax.experimental import pallas as pl
from jax.experimental.pallas import tpu as pltpu
from jax.sharding import PartitionSpec as P

D = 7168
KVLORA = 512
ROPE = 64
NOPE = 128
IHEADS = 64
IDIM = 128
BLK = 64
LANES = 128


epsilon = 1e-06
very_low = -1e30

SMEM = pl.BlockSpec(memory_space=pltpu.SMEM)
VMEM = pl.BlockSpec(memory_space=pltpu.VMEM)
HBM = pl.BlockSpec(memory_space=pltpu.HBM)
NT = (((1,), (1,)), ((), ()))


def shifted(size, step):
    return [(i, (i + step) % size) for i in range(size)]


def swapped(size, bit):
    return [(i, i ^ bit) for i in range(size)]


def limits(mib):
    return pltpu.CompilerParams(vmem_limit_bytes=mib << 20)


def in_hbm(array):
    return pltpu.with_memory_space_constraint(array, pltpu.HBM)


def in_vmem(array):
    return pltpu.with_memory_space_constraint(array, pltpu.VMEM)


def prepare(
    sources, place, blocks_hbm, lengths_hbm, slot_hbm, gate_hbm, cache_ref, slots_ref, residual_ref, gain_ref, igate_ref, down_ref,
    keep_ref, send_ref, base_ref, weight_ref, live_ref, limit_ref, gain_out_ref, igate_out_ref, down_out_ref,
    blocks_ref, lengths_ref, slot_ref, gate_ref, cache, own, residual, scalar_sems, sems,
):
    this, group = place[0], place[3]
    width = cache_ref.shape[1]
    count = blocks_hbm.shape[1]
    scalars = ((blocks_hbm, blocks_ref), (lengths_hbm, lengths_ref), (slot_hbm, slot_ref), (gate_hbm, gate_ref))
    fetched = [pltpu.make_async_copy(source, target, scalar_sems.at[k]) for k, (source, target) in enumerate(scalars)]
    for copy in fetched:
        copy.start()
    moved = (
        (down_ref, down_out_ref), (cache_ref.at[this], cache), (slots_ref.at[group], own), (residual_ref, residual), (gain_ref, gain_out_ref),
        (igate_ref, igate_out_ref),
    )
    moves = [pltpu.make_async_copy(source, target, sems.at[k]) for k, (source, target) in enumerate(moved)]
    for move in (*moves[1:], moves[0]):
        move.start()
    for copy in fetched:
        copy.wait()
    spots = []
    for slot in range(count):
        local = blocks_ref[this, lax.rem(slot + place[2] * (count // 2), count)] - place[1]
        owned = (local >= 0) & (local < cache_ref.shape[2] // BLK)
        local = jnp.where(owned, local, 0)
        begin = pl.multiple_of(local // 2 * LANES, LANES)
        spots.append((begin, owned, (local % 2) != (slot % 2)))
    rows = residual.shape[0]
    lane = lax.broadcasted_iota(jnp.int32, (1, live_ref.shape[1]), 1)
    for k, row in enumerate((this, 1 - this)):
        position = lane % BLK
        for slot in range(count):
            block = blocks_ref[row, lax.rem(slot + place[2] * (count // 2), count)]
            position = position + jnp.where(lane // BLK == slot, block * BLK, 0)
        live_ref[k : k + 1, :] = (position < lengths_ref[row]).astype(jnp.float32)
    position = place[4] + lax.broadcasted_iota(jnp.int32, (1, limit_ref.shape[1]), 1)
    for r in range(rows):
        limit_ref[r : r + 1, :] = (position < lengths_ref[r]).astype(jnp.float32)
    capacity = own.shape[0]
    spot = lax.broadcasted_iota(jnp.int32, (capacity, LANES), 0)
    weights = []
    for step in range(sources + 1):
        source = lax.rem(group + sources + 1 - step, sources + 1)
        for r in range(rows):
            weight = jnp.zeros(spot.shape, jnp.float32)
            for k in range(slot_ref.shape[1]):
                weight = jnp.where(spot == slot_ref[r, k] - source * capacity, gate_ref[r, k], weight)
            if step == 0:
                weights.append(weight[:, :1])
            else:
                weight_ref[step - 1, r] = weight
    moves[1].wait()
    lane = lax.broadcasted_iota(jnp.int32, (width, LANES), 1)
    for pair in range(count // 2):
        total = jnp.zeros((width, LANES), jnp.float32)
        for side in range(2):
            begin, owned, swap = spots[2 * pair + side]
            tile = cache[:, pl.ds(begin, LANES)].astype(jnp.float32)
            tile = jnp.where(swap, pltpu.roll(tile, BLK, 1), tile)
            total = jnp.where((lane // BLK == side) & owned, tile, total)
        out_ref = keep_ref if 4 * pair < count else send_ref
        begin = pair % (count // 4) * LANES
        out_ref[:, begin : begin + LANES] = total.astype(out_ref.dtype)
    for move in moves[2:]:
        move.wait()
    for r in range(rows):
        routed = jnp.sum(weights[r] * own[...].astype(jnp.float32), axis=0, keepdims=True)
        base_ref[r : r + 1, :] = residual[r : r + 1].astype(jnp.float32) + routed
    moves[0].wait()


def combine_down(
    sources, place, base_ref, weight_ref, gain_ref, igate_ref, down_ref, *refs
):
    received = refs[:sources]
    hidden_ref, part_ref = refs[sources:]
    rows = base_ref.shape[0]
    group = place[3]
    routed = [base_ref[r : r + 1, :] for r in range(rows)]
    for k, ref in enumerate(received):
        piece = ref[pl.ds(group, 1)][0].astype(jnp.float32)
        for r in range(rows):
            routed[r] = routed[r] + jnp.sum(weight_ref[k, r][:, :1] * piece, axis=0, keepdims=True)
    hidden = jnp.concatenate(routed, axis=0).astype(jnp.bfloat16)
    hidden_ref[...] = hidden
    widened = hidden.astype(jnp.float32)
    scaled = (widened * gain_ref[...].reshape(1, -1)).astype(jnp.bfloat16)
    qlora = down_ref.shape[1]
    squares = jnp.sum(widened * widened, axis=1, keepdims=True)
    part_ref[:, qlora + LANES :] = jnp.broadcast_to(squares, (rows, LANES))
    gates = lax.dot_general(scaled, igate_ref[...], NT, preferred_element_type=jnp.float32)
    part_ref[:, qlora : qlora + LANES] = jnp.concatenate([gates, gates], axis=1)
    part_ref[:, :qlora] = jnp.dot(scaled, down_ref[...], preferred_element_type=jnp.float32)


def attend_row(live, content, turn, cache):
    logits = jnp.dot(content, cache[:KVLORA], preferred_element_type=jnp.float32) + jnp.dot(
        turn, cache[KVLORA:], preferred_element_type=jnp.float32
    )
    masked = jnp.where(live, logits * (NOPE + ROPE) ** -0.5, very_low)
    weights = jnp.where(live, jnp.exp(masked - jnp.max(masked, axis=1, keepdims=True)), 0.0)
    total = jnp.sum(weights, axis=1, keepdims=True)
    merged = lax.dot_general(weights.astype(jnp.bfloat16), cache[:KVLORA], NT, preferred_element_type=jnp.float32)
    return merged / total


def attend_first(place, live_ref, absorbed, rotary, cache_ref, out_ref):
    row = place[0]
    live = live_ref[:1, :] > 0.0
    out_ref[...] = attend_row(live, absorbed[pl.ds(row, 1)][0], rotary[pl.ds(row, 1)][0], cache_ref[...])


def finish(
    pieces, place, live_ref, absorbed, rotary, first_ref, cache_ref, value_ref, limit_ref, gates_ref, keys_ref, *refs
):
    gathered = refs[:pieces]
    out_ref, scores_ref, queries = refs[pieces:]
    index_heads = gathered[0].shape[1]
    order = lax.broadcasted_iota(jnp.int32, (IHEADS, IHEADS), 0)
    head = order
    for k, ref in enumerate(gathered):
        for side in range(2):
            spot = 2 * k + side
            begin = place[5 + k] + jnp.where(place[0] == side, 0, index_heads)
            head = jnp.where(order // index_heads == spot, begin + order % index_heads, head)
            for r in range(scores_ref.shape[0]):
                queries[r, spot * index_heads : (spot + 1) * index_heads, :] = ref[side, :, r, :].astype(jnp.float32)
    for r in range(scores_ref.shape[0]):
        logits = lax.dot_general(
            queries[r].astype(jnp.bfloat16), keys_ref[r], NT, preferred_element_type=jnp.float32
        )
        gates = jnp.where(lax.broadcasted_iota(jnp.int32, head.shape, 1) == head, gates_ref[r : r + 1, :], 0.0)
        gates = jnp.sum(gates, axis=1, keepdims=True)
        raw = jnp.sum(gates * jnp.maximum(logits, 0.0), axis=0, keepdims=True)
        scores_ref[r : r + 1, :] = jnp.where(limit_ref[r : r + 1, :] > 0.0, raw, 0.0)
    heads = value_ref.shape[0]
    this = place[0]
    row = 1 - this
    live = live_ref[1:, :] > 0.0
    second = attend_row(live, absorbed[pl.ds(row, 1)][0], rotary[pl.ds(row, 1)][0], cache_ref[...])
    attended = jnp.concatenate([first_ref[...], second], axis=0).astype(jnp.bfloat16)
    head = lax.broadcasted_iota(jnp.int32, (2 * heads, value_ref.shape[2]), 0) % heads
    result = jnp.zeros(head.shape, jnp.float32)
    for n in range(heads):
        product = jnp.dot(attended, value_ref[n], preferred_element_type=jnp.float32)
        result = jnp.where(head == n, product, result)
    for k, row in enumerate((this, 1 - this)):
        out_ref[pl.ds(row, 1)] = result[k * heads : (k + 1) * heads].astype(out_ref.dtype)[None]


def local(
    residual,
    expert_out,
    combine_slot,
    combine_gate,
    attn_gain,
    query_down,
    index_gate,
    latent_gain,
    query_up,
    key_absorb,
    index_query,
    value_up,
    latent_cache,
    index_keys,
    lengths,
    block_list,
):
    n_ctx, n_dp, n_hp = (lax.axis_size(name) for name in ("ctx", "dp", "hp"))
    c, d, h = (lax.axis_index(name) for name in ("ctx", "dp", "hp"))
    rows, features = residual.shape
    qlora = query_down.shape[1]
    selected = block_list.shape[1]
    span, width = latent_cache.shape[1:]
    heads = value_up.shape[0]
    f32, bf16 = jnp.float32, jnp.bfloat16

    slots = expert_out[0]
    received = [lax.ppermute(slots, "dp", shifted(n_dp, step)) for step in range(1, n_dp)]

    index_heads, index_span = index_query.shape[1], index_keys.shape[1]
    sources = [jnp.bitwise_xor(c, step) * n_hp * index_heads for step in range(n_ctx)]
    scalars = [h, c * (span // BLK), c % 2, d, (c * n_hp + h) * index_span, *sources]
    place = in_vmem(jnp.stack(scalars).astype(jnp.int32))
    half = pltpu.VMEM((width, selected // 2 * BLK), bf16)
    mine, send, *ready, live, limit, gain, igate, down = pl.pallas_call(
        functools.partial(prepare, len(received)),
        out_shape=(
            half,
            half,
            pltpu.VMEM((rows, features), f32),
            pltpu.VMEM((len(received), rows, slots.shape[1], LANES), f32),
            pltpu.VMEM((rows, selected * BLK), f32),
            pltpu.VMEM((rows, index_span), f32),
            pltpu.VMEM(attn_gain.shape, f32),
            pltpu.VMEM(index_gate.shape[::-1], bf16),
            pltpu.VMEM(query_down.shape, bf16),
        ),
        in_specs=[SMEM] + [HBM] * 10,
        out_specs=(VMEM,) * 9,
        scratch_shapes=[
            pltpu.SMEM(block_list.shape, jnp.int32),
            pltpu.SMEM(lengths.shape, jnp.int32),
            pltpu.SMEM(combine_slot.shape, jnp.int32),
            pltpu.SMEM(combine_gate.shape, f32),
            pltpu.VMEM((width, span), bf16),
            pltpu.VMEM(slots.shape[1:], bf16),
            pltpu.VMEM(residual.shape, bf16),
            pltpu.SemaphoreType.DMA((4,)),
            pltpu.SemaphoreType.DMA((6,)),
        ],
        compiler_params=limits(6),
        name="prepare",
    )(
        place,
        *map(in_hbm, (block_list, lengths, combine_slot, combine_gate)),
        *map(in_hbm, (jnp.swapaxes(latent_cache, 1, 2), slots, residual, attn_gain, index_gate.T, query_down)),
    )
    upper, lower = (lax.ppermute(x, "ctx", swapped(n_ctx, 1)) for x in (send[: width // 2], send[width // 2 :]))
    ready = [*ready, gain, igate, down]
    received, ready = lax.optimization_barrier((received, ready))

    hidden, part = pl.pallas_call(
        functools.partial(combine_down, len(received)),
        out_shape=(
            jax.ShapeDtypeStruct((rows, features), bf16),
            pltpu.VMEM((rows, qlora + 2 * LANES), f32),
        ),
        in_specs=[SMEM] + [VMEM] * (5 + len(received)),
        out_specs=(VMEM, VMEM),
        compiler_params=limits(8),
        cost_estimate=pl.CostEstimate(flops=10000000000, bytes_accessed=0, transcendentals=0),
        name="combine_down",
    )(place, *map(in_vmem, ready), *received)

    mine, upper, lower, _ = lax.optimization_barrier((mine, upper, lower, part))
    mine = mine + jnp.concatenate([upper, lower], axis=0)
    crossed = [lax.ppermute(mine, "ctx", swapped(n_ctx, 2))]

    parts = [part] + [lax.ppermute(part, "ctx", swapped(n_ctx, step)) for step in range(1, n_ctx)]
    total = functools.reduce(jnp.add, parts)
    scale = lax.rsqrt(total[:, qlora + LANES : qlora + LANES + 1] / D + epsilon)
    latent_sum = total[:, :qlora] * scale
    head_gate = total[:, qlora : qlora + IHEADS] * (scale * IHEADS**-0.5 * IDIM**-0.5)
    latent_scale = lax.rsqrt(jnp.mean(latent_sum * latent_sum, axis=-1, keepdims=True) + epsilon)
    latent = (latent_sum * latent_scale * latent_gain).astype(bf16)

    index_local = jnp.einsum("rq,qnd->nrd", latent, index_query, preferred_element_type=f32).astype(bf16)
    index_other = lax.ppermute(index_local, "hp", swapped(n_hp, 1))
    projected = jnp.einsum("rq,qnd->rnd", latent, query_up, preferred_element_type=f32).astype(bf16)
    absorbed = jnp.einsum("rnk,nkc->rnc", projected[:, :, :NOPE], key_absorb, preferred_element_type=f32).astype(bf16)
    rotary = projected[:, :, NOPE:]
    index_local, index_other, mine, crossed, absorbed, rotary = lax.optimization_barrier(
        (index_local, index_other, mine, crossed, absorbed, rotary)
    )
    index_pair = jnp.stack([index_local, index_other])
    gathered = [index_pair] + [lax.ppermute(index_pair, "ctx", swapped(n_ctx, step)) for step in range(1, n_ctx)]

    mine = functools.reduce(jnp.add, crossed, mine)
    bit = 4
    while bit < n_ctx:
        mine = mine + lax.ppermute(mine, "ctx", swapped(n_ctx, bit))
        bit *= 2
    other = lax.ppermute(mine, "ctx", swapped(n_ctx, 1))
    mine = jnp.concatenate([mine, other], axis=1)
    theirs = lax.ppermute(mine, "hp", swapped(n_hp, 1))
    attended = pl.pallas_call(
        attend_first,
        out_shape=pltpu.VMEM((heads, KVLORA), f32),
        in_specs=[SMEM] + [VMEM] * 4,
        out_specs=VMEM,
        compiler_params=limits(4),
        cost_estimate=pl.CostEstimate(flops=20000000000, bytes_accessed=0, transcendentals=0),
        name="attend_first",
    )(place, *map(in_vmem, (live, absorbed, rotary, mine)))
    gathered, attended = lax.optimization_barrier((gathered, attended))
    attn_out, index_scores = pl.pallas_call(
        functools.partial(finish, n_ctx),
        out_shape=(
            jax.ShapeDtypeStruct((rows, heads, value_up.shape[2]), bf16),
            jax.ShapeDtypeStruct((rows, index_span), f32),
        ),
        in_specs=[SMEM] + [VMEM] * (9 + n_ctx),
        out_specs=(VMEM, VMEM),
        scratch_shapes=[pltpu.VMEM((rows, IHEADS, IDIM), f32)],
        compiler_params=limits(8),
        name="finish",
    )(
        place,
        *map(in_vmem, (live, absorbed, rotary, attended, theirs, value_up, limit, head_gate, index_keys, *gathered)),
    )
    return (hidden, index_scores, attn_out)


def solution(mesh):
    placed = (
        P(("groups", "dp"), "ctx"),
        P(("groups", "dp"), None, None, "ctx"),
        P(("groups", "dp"), None),
        P(("groups", "dp"), None),
        P("ctx"),
        P("ctx", None),
        P("ctx", None),
        P(),
        P(None, ("ctx", "hp"), None),
        P(("ctx", "hp"), None, None),
        P(None, ("ctx", "hp"), None),
        P(("ctx", "hp"), None, None),
        P(("groups", "dp"), "ctx", None),
        P(("groups", "dp"), ("ctx", "hp"), None),
        P(("groups", "dp")),
        P(("groups", "dp"), None),
    )
    return jax.shard_map(
        local,
        mesh=mesh,
        in_specs=placed,
        out_specs=(
            P(("groups", "dp"), "ctx"),
            P(("groups", "dp"), ("ctx", "hp")),
            P(("groups", "dp"), ("ctx", "hp"), None),
        ),
        check_vma=False,
    )
```

time: 42.7 us -> 35.4 us (0.83)
  Pallas kernels: 17.2 us -> 8.05 us
  matrix products: 0.52 us -> 3.49 us
  starting transfers between devices: 19.6 us -> 18.7 us
  waiting for transfers between devices: 3.54 us -> 2.97 us
    pallas_call x6 -> x3, Pallas kernels: 15.6 us -> 6.53 us  [the longest x1 3.52 us: local(): pl.pallas_call(functools.partial(prepare, len(received)), out_shape=(half...]
    dot_general x0 -> x2, matrix products: none -> 2.93 us  [the longest x1 2.55 us: local(): jnp.einsum('rq,qnd->rnd', latent, query_up, preferred_element_type=f32)]
    ppermute x1, starting transfers between devices: 2.39 us -> 1.5 us  [local(): theirs = lax.ppermute(mine, 'hp', swapped(n_hp, 1))]
    ppermute x1, waiting for transfers between devices: 0.82 us -> 0.4 us  [local(): index_other = lax.ppermute(index_local, 'hp', swapped(n_hp, 1))]
  transfers between devices with their start and end apart: 13 -> 13, of which waited for: 3 -> 4; matrix products, arithmetic and copies ran while one was open for 3% -> 12% of each run, Pallas kernels for 36% -> 17%
where the time goes in v4:
time: 35.4 us; the launch traced here: 35.2 us
  starting transfers between devices  18.7 us (53%)
  Pallas kernels  8.05 us (23%)
  matrix products  3.49 us (10%)
  waiting for transfers between devices  2.97 us (8%)
  between operations  0.81 us (2%)
  local copies, waits for them, and re-layouts  0.57 us (2%)
  other arithmetic  0.57 us (2%)
    ppermute x1, starting transfers between devices, local(): index_other = lax.ppermute(index_local, 'hp', swapped(n_hp, 1))  4.14 us
    ppermute x3, starting transfers between devices, local(): lax.ppermute(part, 'ctx', swapped(n_ctx, step))  3.7 us
    ppermute x3, starting transfers between devices, local(): lax.ppermute(index_pair, 'ctx', swapped(n_ctx, step))  3.61 us
    pallas_call x1, Pallas kernels, local(): pl.pallas_call(functools.partial(prepare, len(received)), out_shape=(half...  3.52 us
    dot_general x1, matrix products, local(): jnp.einsum('rq,qnd->rnd', latent, query_up, preferred_element_type=f32)  2.55 us
    ppermute x1, starting transfers between devices, local(): lax.ppermute(slots, 'dp', shifted(n_dp, step))  2.11 us
    ppermute x1, starting transfers between devices, local(): crossed = [lax.ppermute(mine, 'ctx', swapped(n_ctx, 2))]  2.08 us
    pallas_call x1, Pallas kernels, local(): pl.pallas_call(functools.partial(finish, n_ctx), out_shape=(jax.ShapeDtyp...  2.04 us
  transfers between devices with their start and end apart: 13, of which 4 were waited for; matrix products, arithmetic and copies ran while one was open for 12% of the time, Pallas kernels for 17%

profile of v4, /device:TPU:1, one launch (start us, length us, event | category | flops | bytes accessed | tf_op | source)
XLA Modules:
  0.0 35.2 jit_solution(8907623540488568945)
XLA Ops:
  0.6 2.1 %collective-permute-start = (bf16[2,16,1792]{2,1,0:T(8,128)(2,1)}, bf16[2,16,1792]{2,1,0:T(8,128)(2,1)S(1)}, u32[]{:S(2)}, u32[]{:S(2)}) collective-permute-start(bf16[2,16,1792]{2,1,0:T(8,128)(2,1)} %bitcast.32), channel_id=1, source_target_pairs={{0,2},{2,0},{1,3},{3,1},{4,6},{6,4},{5,7},{7,5},{8,10},{10,8},{9,1... | collective-permute-start | bytes 344072 | tf_op jit(solution)/shard_map/ppermute | solution.py:228
  2.8 3.5 %prepare.1 = (bf16[576,128]{1,0:T(8,128)(2,1)S(1)}, bf16[576,128]{1,0:T(8,128)(2,1)S(1)}, f32[2,1792]{1,0:T(2,128)S(1)}, f32[1,2,16,128]{3,2,1,0:T(8,128)S(1)}, ...) custom-call(s32[9]{0:T(128)S(1)} %stack.48.place, ...), custom_call_target="tpu_custom_call" | custom-call | tf_op jit(solution)/shard_map/prepare/pallas_call | solution.py:235
  6.4 1.4 %collective-permute-start.6 = (bf16[288,128]{1,0:T(8,128)(2,1)S(1)}, bf16[288,128]{1,0:T(8,128)(2,1)S(1)}, u32[]{:S(2)}, u32[]{:S(2)}) collective-permute-start(bf16[288,128]{1,0:T(8,128)(2,1)S(1)} %get-tuple-element.71), channel_id=1, source_target_pairs={{0,4},{4,0},{8,12},{12,8},{1,5},{5,1},{9,13},{13,9},{2,6},{6,2},{1... | collective-permute-start | bytes 221192 | tf_op jit(solution)/shard_map/ppermute | solution.py:268
  7.7 0.2 collective-permute-start.5
  7.9 1.5 %combine_down.1 = (bf16[2,1792]{1,0:T(2,128)(2,1)}, f32[2,1792]{1,0:T(2,128)S(1)}) custom-call(s32[9]{0:T(128)S(1)} %stack.48.place, f32[2,1792]{1,0:T(2,128)S(1)} %get-tuple-element.41.base_ref, f32[1,2,16,128]{3,2,1,0:T(8,128)S(1)} %get-tuple-element.42.weight_ref, f32[1792]{0:T(1024)S(1)} %get-tuple-element.43.gain_ref, ...), custom_call_target="tpu_custom_call" | custom-call | flops 10000000000 | tf_op jit(solution)/shard_map/combine_down/pallas_call | solution.py:272
  9.5 3.3 %collective-permute-start.3 = (f32[2,1792]{1,0:T(2,128)S(1)}, f32[2,1792]{1,0:T(2,128)S(1)}, u32[]{:S(2)}, u32[]{:S(2)}) collective-permute-start(f32[2,1792]{1,0:T(2,128)S(1)} %get-tuple-element.49), channel_id=1, source_target_pairs={{0,12},{4,8},{8,4},{12,0},{1,13},{5,9},{9,5},{13,1},{2,14},{6,10},... | collective-permute-start | bytes 43016 | tf_op jit(solution)/shard_map/ppermute | solution.py:289
  12.8 0.4 %collective-permute-start.1 = (f32[2,1792]{1,0:T(2,128)S(1)}, f32[2,1792]{1,0:T(2,128)S(1)}, u32[]{:S(2)}, u32[]{:S(2)}) collective-permute-start(f32[2,1792]{1,0:T(2,128)S(1)} %get-tuple-element.49), channel_id=1, source_target_pairs={{0,4},{4,0},{8,12},{12,8},{1,5},{5,1},{9,13},{13,9},{2,6},{6,2},{1... | collective-permute-start | bytes 43016 | tf_op jit(solution)/shard_map/ppermute | solution.py:289
  13.2 2.1 %collective-permute-start.7 = (bf16[576,128]{1,0:T(8,128)(2,1)S(1)}, bf16[576,128]{1,0:T(8,128)(2,1)S(1)}, u32[]{:S(2)}, u32[]{:S(2)}) collective-permute-start(bf16[576,128]{1,0:T(8,128)(2,1)S(1)} %maximum_add_fusion), channel_id=1, source_target_pairs={{0,8},{4,12},{8,0},{12,4},{1,9},{5,13},{9,1},{13,5},{2,10},{6,14},... | collective-permute-start | bytes 442376 | tf_op jit(solution)/shard_map/ppermute | solution.py:287
  15.3 1.0 %collective-permute-done.2 = f32[2,1792]{1,0:T(2,128)S(1)} collective-permute-done((f32[2,1792]{1,0:T(2,128)S(1)}, f32[2,1792]{1,0:T(2,128)S(1)}, u32[]{:S(2)}, u32[]{:S(2)}) %collective-permute-start.2) | collective-permute-done | bytes 14368 | tf_op jit(solution)/shard_map/ppermute | solution.py:289
  16.4 0.2 multiply_reduce_fusion
  16.7 0.6 %fusion.5 = bf16[8,2,128]{2,1,0:T(2,128)(2,1)S(1)} fusion(bf16[1536,8,128]{2,1,0:T(8,128)(2,1)S(1)} %copy-done, f32[2,1792]{1,0:T(2,128)S(1)} %add_add_fusion, f32[2]{0:T(128)S(1)} %add_rsqrt_fusion, f32[2]{0:T(128)S(1)} %get-tuple-element.70, f32[1536]{0:T(1024)S(1)} %copy-done.4), kind=kOutput, calls=%fused_computation.3 | convolution fusion | flops 6305792 | bytes 3171328 | tf_op jit(solution)/shard_map/rq,qnd->nrd/dot_general | solution.py:297
  17.3 2.6 %fusion.11 = bf16[2,16,192]{2,0,1:T(2,128)(2,1)S(1)} fusion(bf16[1536,16,192]{0,2,1:T(8,128)(2,1)S(1)} %bitcast.29, f32[2,1792]{1,0:T(2,128)S(1)} %add_add_fusion, f32[2]{0:T(128)S(1)} %add_rsqrt_fusion, f32[2]{0:T(128)S(1)} %get-tuple-element.70, f32[1536]{0:T(1024)S(1)} %copy-done.4), kind=kOutput, calls=%fused_computation.16 | convolution fusion | flops 18886656 | bytes 9470976 | tf_op jit(solution)/shard_map/rq,qnd->rnd/dot_general | solution.py:299
  19.9 4.1 %collective-permute-start.4 = (bf16[8,2,128]{2,1,0:T(2,128)(2,1)S(1)}, bf16[8,2,128]{2,1,0:T(2,128)(2,1)S(1)}, u32[]{:S(2)}, u32[]{:S(2)}) collective-permute-start(bf16[8,2,128]{2,1,0:T(2,128)(2,1)S(1)} %fusion.5), channel_id=1, source_target_pairs={{0,1},{1,0},{2,3},{3,2},{4,5},{5,4},{6,7},{7,6},{8,9},{9,8},{10,11... | collective-permute-start | bytes 12296 | tf_op jit(solution)/shard_map/ppermute | solution.py:298
  24.0 0.4 %fusion.9 = bf16[16,2,512]{2,1,0:T(2,128)(2,1)S(1)} fusion(bf16[16,128,512]{2,1,0:T(8,128)(2,1)S(1)} %copy-done.3, bf16[2,16,128]{2,1,0:T(8,128)(2,1)S(1)} %copy.41), kind=kOutput, calls=%fused_computation.14 | convolution fusion | flops 4194304 | bytes 2138112 | tf_op jit(solution)/shard_map/rnk,nkc->rnc/dot_general | solution.py:300
  24.4 0.4 %collective-permute-done.4 = bf16[8,2,128]{2,1,0:T(2,128)(2,1)S(1)} collective-permute-done((bf16[8,2,128]{2,1,0:T(2,128)(2,1)S(1)}, bf16[8,2,128]{2,1,0:T(2,128)(2,1)S(1)}, u32[]{:S(2)}, u32[]{:S(2)}) %collective-permute-start.4) | collective-permute-done | bytes 4128 | tf_op jit(solution)/shard_map/ppermute | solution.py:298
  25.0 1.8 %collective-permute-start.10 = (bf16[2,8,2,128]{3,2,1,0:T(2,128)(2,1)S(1)}, bf16[2,8,2,128]{3,2,1,0:T(2,128)(2,1)S(1)}, u32[]{:S(2)}, u32[]{:S(2)}) collective-permute-start(bf16[2,8,2,128]{3,2,1,0:T(2,128)(2,1)S(1)} %pad_maximum_fusion.1.refs_0_), channel_id=1, source_target_pairs={{0,12},{4,8},{8,4},{12,0},{1,13},{5,9},{9,5},{13,1},{2,14},{6,10},... | collective-permute-start | bytes 24584 | tf_op jit(solution)/shard_map/ppermute | solution.py:306
  26.9 0.9 %collective-permute-start.9 = (bf16[2,8,2,128]{3,2,1,0:T(2,128)(2,1)S(1)}, bf16[2,8,2,128]{3,2,1,0:T(2,128)(2,1)S(1)}, u32[]{:S(2)}, u32[]{:S(2)}) collective-permute-start(bf16[2,8,2,128]{3,2,1,0:T(2,128)(2,1)S(1)} %pad_maximum_fusion.1.refs_0_), channel_id=1, source_target_pairs={{0,8},{4,12},{8,0},{12,4},{1,9},{5,13},{9,1},{13,5},{2,10},{6,14},... | collective-permute-start | bytes 24584 | tf_op jit(solution)/shard_map/ppermute | solution.py:306
  27.7 0.9 %collective-permute-start.8 = (bf16[2,8,2,128]{3,2,1,0:T(2,128)(2,1)S(1)}, bf16[2,8,2,128]{3,2,1,0:T(2,128)(2,1)S(1)}, u32[]{:S(2)}, u32[]{:S(2)}) collective-permute-start(bf16[2,8,2,128]{3,2,1,0:T(2,128)(2,1)S(1)} %pad_maximum_fusion.1.refs_0_), channel_id=1, source_target_pairs={{0,4},{4,0},{8,12},{12,8},{1,5},{5,1},{9,13},{13,9},{2,6},{6,2},{1... | collective-permute-start | bytes 24584 | tf_op jit(solution)/shard_map/ppermute | solution.py:306
  28.7 1.4 %collective-permute-done.11 = bf16[576,128]{1,0:T(8,128)(2,1)S(1)} collective-permute-done((bf16[576,128]{1,0:T(8,128)(2,1)S(1)}, bf16[576,128]{1,0:T(8,128)(2,1)S(1)}, u32[]{:S(2)}, u32[]{:S(2)}) %collective-permute-start.11) | collective-permute-done | bytes 147488 | tf_op jit(solution)/shard_map/ppermute | solution.py:313
  30.1 1.5 %collective-permute-start.12 = (bf16[576,256]{1,0:T(8,128)(2,1)S(1)}, bf16[576,256]{1,0:T(8,128)(2,1)S(1)}, u32[]{:S(2)}, u32[]{:S(2)}) collective-permute-start(bf16[576,256]{1,0:T(8,128)(2,1)S(1)} %pad_maximum_fusion.cache_ref), channel_id=1, source_target_pairs={{0,1},{1,0},{2,3},{3,2},{4,5},{5,4},{6,7},{7,6},{8,9},{9,8},{10,11... | collective-permute-start | bytes 884744 | tf_op jit(solution)/shard_map/ppermute | solution.py:315
  31.6 1.0 %attend_first.1.first_ref = f32[16,512]{1,0:T(8,128)S(1)} custom-call(s32[9]{0:T(128)S(1)} %stack.48.place, f32[2,256]{1,0:T(2,128)S(1)} %get-tuple-element.48.live_ref, bf16[2,16,512]{2,1,0:T(8,128)(2,1)S(1)} %bitcast.26, bf16[2,16,64]{2,1,0:T(8,128)(2,1)S(1)} %copy.42.rotary, bf16[576,256]{1,0:T(8,128)(2,1)S(1)} %pad_maximum_fusion.cache_ref), custom_call_target="tpu_custom_call" | custom-call | flops 20000000000 | tf_op jit(solution)/shard_map/attend_first/pallas_call | solution.py:316
  32.6 0.2 collective-permute-done.12.cache_ref
  32.8 0.4 %copy-done.1 = bf16[16,512,128]{2,1,0:T(8,128)(2,1)S(1)} copy-done((bf16[16,512,128]{2,1,0:T(8,128)(2,1)S(1)}, bf16[16,512,128]{2,1,0:T(8,128)(2,1)}, u32[]{:S(2)}) %copy-start.1) | copy-done | bytes 2097176
  33.2 2.0 %finish.1 = (bf16[2,16,128]{2,1,0:T(8,128)(2,1)}, f32[2,256]{1,0:T(2,128)}) custom-call(s32[9]{0:T(128)S(1)} %stack.48.place, f32[2,256]{1,0:T(2,128)S(1)} %get-tuple-element.48.live_ref, bf16[2,16,512]{2,1,0:T(8,128)(2,1)S(1)} %bitcast.27, bf16[2,16,64]{2,1,0:T(8,128)(2,1)S(1)} %copy.42.rotary, f32[16,512]{1,0:T(8,128)S(1)} %attend_first.1.first_ref, ...), custom_call_target="tpu_custom_call" | custom-call | tf_op jit(solution)/shard_map/finish/pallas_call | solution.py:326
  (42 shorter events, 0.7 us)
Async XLA Ops:
  0.6 16.0 %copy-start = (bf16[1536,8,128]{2,1,0:T(8,128)(2,1)S(1)}, bf16[1536,8,128]{2,1,0:T(8,128)(2,1)}, u32[]{:S(2)}) copy-start(bf16[1536,8,128]{2,1,0:T(8,128)(2,1)} %param.26) | copy-start | bytes 9437188
  0.6 7.3 %collective-permute-start = (bf16[2,16,1792]{2,1,0:T(8,128)(2,1)}, bf16[2,16,1792]{2,1,0:T(8,128)(2,1)S(1)}, u32[]{:S(2)}, u32[]{:S(2)}) collective-permute-start(bf16[2,16,1792]{2,1,0:T(8,128)(2,1)} %bitcast.32), channel_id=1, source_target_pairs={{0,2},{2,0},{1,3},{3,1},{4,6},{6,4},{5,7},{7,5},{8,10},{10,8},{9,1... | collective-permute-start | bytes 344072 | tf_op jit(solution)/shard_map/ppermute | solution.py:228
  6.4 6.8 %collective-permute-start.6 = (bf16[288,128]{1,0:T(8,128)(2,1)S(1)}, bf16[288,128]{1,0:T(8,128)(2,1)S(1)}, u32[]{:S(2)}, u32[]{:S(2)}) collective-permute-start(bf16[288,128]{1,0:T(8,128)(2,1)S(1)} %get-tuple-element.71), channel_id=1, source_target_pairs={{0,4},{4,0},{8,12},{12,8},{1,5},{5,1},{9,13},{13,9},{2,6},{6,2},{1... | collective-permute-start | bytes 221192 | tf_op jit(solution)/shard_map/ppermute | solution.py:268
  7.7 5.4 %collective-permute-start.5 = (bf16[288,128]{1,0:T(8,128)(2,1)S(1)}, bf16[288,128]{1,0:T(8,128)(2,1)S(1)}, u32[]{:S(2)}, u32[]{:S(2)}) collective-permute-start(bf16[288,128]{1,0:T(8,128)(2,1)S(1)} %get-tuple-element.72), channel_id=1, source_target_pairs={{0,4},{4,0},{8,12},{12,8},{1,5},{5,1},{9,13},{13,9},{2,6},{6,2},{1... | collective-permute-start | bytes 221192 | tf_op jit(solution)/shard_map/ppermute | solution.py:268
  7.9 9.3 %slice-start = ((s8[9437184]{0:T(1024)(128)(4,1)}), s8[4194304]{0:T(1024)(128)(4,1)S(1)}, s32[]{:S(2)}) async-start(s8[9437184]{0:T(1024)(128)(4,1)} %bitcast.28), calls=%async_computation | async-start | bytes 8388608
  7.9 8.7 %copy-start.4 = (f32[1536]{0:T(1024)S(1)}, f32[1536]{0:T(1024)}, u32[]{:S(2)}) copy-start(f32[1536]{0:T(1024)} %param.23) | copy-start | bytes 18436
  7.9 9.3 %slice-start.1 = ((s8[9437184]{0:T(1024)(128)(4,1)}), s8[4194304]{0:T(1024)(128)(4,1)S(1)}, s32[]{:S(2)}) async-start(s8[9437184]{0:T(1024)(128)(4,1)} %bitcast.28), calls=%async_computation.1 | async-start | bytes 8388608
  7.9 9.3 %slice-start.2 = ((s8[9437184]{0:T(1024)(128)(4,1)}), s8[1048576]{0:T(1024)(128)(4,1)S(1)}, s32[]{:S(2)}) async-start(s8[9437184]{0:T(1024)(128)(4,1)} %bitcast.28), calls=%async_computation.2 | async-start | bytes 2097152
  9.5 5.8 %collective-permute-start.3 = (f32[2,1792]{1,0:T(2,128)S(1)}, f32[2,1792]{1,0:T(2,128)S(1)}, u32[]{:S(2)}, u32[]{:S(2)}) collective-permute-start(f32[2,1792]{1,0:T(2,128)S(1)} %get-tuple-element.49), channel_id=1, source_target_pairs={{0,12},{4,8},{8,4},{12,0},{1,13},{5,9},{9,5},{13,1},{2,14},{6,10},... | collective-permute-start | bytes 43016 | tf_op jit(solution)/shard_map/ppermute | solution.py:289
  12.8 3.5 %collective-permute-start.2 = (f32[2,1792]{1,0:T(2,128)S(1)}, f32[2,1792]{1,0:T(2,128)S(1)}, u32[]{:S(2)}, u32[]{:S(2)}) collective-permute-start(f32[2,1792]{1,0:T(2,128)S(1)} %get-tuple-element.49), channel_id=1, source_target_pairs={{0,8},{4,12},{8,0},{12,4},{1,9},{5,13},{9,1},{13,5},{2,10},{6,14},... | collective-permute-start | bytes 43016 | tf_op jit(solution)/shard_map/ppermute | solution.py:289
  12.8 3.5 %collective-permute-start.1 = (f32[2,1792]{1,0:T(2,128)S(1)}, f32[2,1792]{1,0:T(2,128)S(1)}, u32[]{:S(2)}, u32[]{:S(2)}) collective-permute-start(f32[2,1792]{1,0:T(2,128)S(1)} %get-tuple-element.49), channel_id=1, source_target_pairs={{0,4},{4,0},{8,12},{12,8},{1,5},{5,1},{9,13},{13,9},{2,6},{6,2},{1... | collective-permute-start | bytes 43016 | tf_op jit(solution)/shard_map/ppermute | solution.py:289
  13.2 11.6 %collective-permute-start.7 = (bf16[576,128]{1,0:T(8,128)(2,1)S(1)}, bf16[576,128]{1,0:T(8,128)(2,1)S(1)}, u32[]{:S(2)}, u32[]{:S(2)}) collective-permute-start(bf16[576,128]{1,0:T(8,128)(2,1)S(1)} %maximum_add_fusion), channel_id=1, source_target_pairs={{0,8},{4,12},{8,0},{12,4},{1,9},{5,13},{9,1},{13,5},{2,10},{6,14},... | collective-permute-start | bytes 442376 | tf_op jit(solution)/shard_map/ppermute | solution.py:287
  17.2 6.8 %copy-start.3 = (bf16[16,128,512]{2,1,0:T(8,128)(2,1)S(1)}, bf16[16,128,512]{2,1,0:T(8,128)(2,1)}, u32[]{:S(2)}) copy-start(bf16[16,128,512]{2,1,0:T(8,128)(2,1)} %param.25) | copy-start | bytes 6291460
  19.9 5.0 %collective-permute-start.4 = (bf16[8,2,128]{2,1,0:T(2,128)(2,1)S(1)}, bf16[8,2,128]{2,1,0:T(2,128)(2,1)S(1)}, u32[]{:S(2)}, u32[]{:S(2)}) collective-permute-start(bf16[8,2,128]{2,1,0:T(2,128)(2,1)S(1)} %fusion.5), channel_id=1, source_target_pairs={{0,1},{1,0},{2,3},{3,2},{4,5},{5,4},{6,7},{7,6},{8,9},{9,8},{10,11... | collective-permute-start | bytes 12296 | tf_op jit(solution)/shard_map/ppermute | solution.py:298
  24.9 5.2 %collective-permute-start.11 = (bf16[576,128]{1,0:T(8,128)(2,1)S(1)}, bf16[576,128]{1,0:T(8,128)(2,1)S(1)}, u32[]{:S(2)}, u32[]{:S(2)}) collective-permute-start(bf16[576,128]{1,0:T(8,128)(2,1)S(1)} %add.41), channel_id=1, source_target_pairs={{0,4},{4,0},{8,12},{12,8},{1,5},{5,1},{9,13},{13,9},{2,6},{6,2},{1... | collective-permute-start | bytes 442376 | tf_op jit(solution)/shard_map/ppermute | solution.py:313
  25.0 7.5 %collective-permute-start.10 = (bf16[2,8,2,128]{3,2,1,0:T(2,128)(2,1)S(1)}, bf16[2,8,2,128]{3,2,1,0:T(2,128)(2,1)S(1)}, u32[]{:S(2)}, u32[]{:S(2)}) collective-permute-start(bf16[2,8,2,128]{3,2,1,0:T(2,128)(2,1)S(1)} %pad_maximum_fusion.1.refs_0_), channel_id=1, source_target_pairs={{0,12},{4,8},{8,4},{12,0},{1,13},{5,9},{9,5},{13,1},{2,14},{6,10},... | collective-permute-start | bytes 24584 | tf_op jit(solution)/shard_map/ppermute | solution.py:306
  26.9 5.7 %collective-permute-start.9 = (bf16[2,8,2,128]{3,2,1,0:T(2,128)(2,1)S(1)}, bf16[2,8,2,128]{3,2,1,0:T(2,128)(2,1)S(1)}, u32[]{:S(2)}, u32[]{:S(2)}) collective-permute-start(bf16[2,8,2,128]{3,2,1,0:T(2,128)(2,1)S(1)} %pad_maximum_fusion.1.refs_0_), channel_id=1, source_target_pairs={{0,8},{4,12},{8,0},{12,4},{1,9},{5,13},{9,1},{13,5},{2,10},{6,14},... | collective-permute-start | bytes 24584 | tf_op jit(solution)/shard_map/ppermute | solution.py:306
  27.7 4.8 %collective-permute-start.8 = (bf16[2,8,2,128]{3,2,1,0:T(2,128)(2,1)S(1)}, bf16[2,8,2,128]{3,2,1,0:T(2,128)(2,1)S(1)}, u32[]{:S(2)}, u32[]{:S(2)}) collective-permute-start(bf16[2,8,2,128]{3,2,1,0:T(2,128)(2,1)S(1)} %pad_maximum_fusion.1.refs_0_), channel_id=1, source_target_pairs={{0,4},{4,0},{8,12},{12,8},{1,5},{5,1},{9,13},{13,9},{2,6},{6,2},{1... | collective-permute-start | bytes 24584 | tf_op jit(solution)/shard_map/ppermute | solution.py:306
  30.1 2.7 %collective-permute-start.12 = (bf16[576,256]{1,0:T(8,128)(2,1)S(1)}, bf16[576,256]{1,0:T(8,128)(2,1)S(1)}, u32[]{:S(2)}, u32[]{:S(2)}) collective-permute-start(bf16[576,256]{1,0:T(8,128)(2,1)S(1)} %pad_maximum_fusion.cache_ref), channel_id=1, source_target_pairs={{0,1},{1,0},{2,3},{3,2},{4,5},{5,4},{6,7},{7,6},{8,9},{9,8},{10,11... | collective-permute-start | bytes 884744 | tf_op jit(solution)/shard_map/ppermute | solution.py:315
  31.6 1.6 %copy-start.1 = (bf16[16,512,128]{2,1,0:T(8,128)(2,1)S(1)}, bf16[16,512,128]{2,1,0:T(8,128)(2,1)}, u32[]{:S(2)}) copy-start(bf16[16,512,128]{2,1,0:T(8,128)(2,1)} %value_ref.1) | copy-start | bytes 6291460
  31.6 1.6 %copy-start.2 = (bf16[2,256,128]{2,1,0:T(8,128)(2,1)S(1)}, bf16[2,256,128]{2,1,0:T(8,128)(2,1)}, u32[]{:S(2)}) copy-start(bf16[2,256,128]{2,1,0:T(8,128)(2,1)} %keys_ref.1) | copy-start | bytes 393220

commit v5 on v4

--- a/solution.py
+++ b/solution.py
@@ -47,8 +47,8 @@
 
 
 def prepare(
-    sources, place, blocks_hbm, lengths_hbm, slot_hbm, gate_hbm, cache_ref, slots_ref, residual_ref, gain_ref, igate_ref, down_ref,
-    keep_ref, send_ref, base_ref, weight_ref, live_ref, limit_ref, gain_out_ref, igate_out_ref, down_out_ref,
+    sources, place, blocks_hbm, lengths_hbm, slot_hbm, gate_hbm, cache_ref, slots_ref, residual_ref, gain_ref, igate_ref,
+    keep_ref, send_ref, base_ref, weight_ref, live_ref, limit_ref, gain_out_ref, igate_out_ref,
     blocks_ref, lengths_ref, slot_ref, gate_ref, cache, own, residual, scalar_sems, sems,
 ):
     this, group = place[0], place[3]
@@ -59,11 +59,11 @@
     for copy in fetched:
         copy.start()
     moved = (
-        (down_ref, down_out_ref), (cache_ref.at[this], cache), (slots_ref.at[group], own), (residual_ref, residual), (gain_ref, gain_out_ref),
+        (cache_ref.at[this], cache), (slots_ref.at[group], own), (residual_ref, residual), (gain_ref, gain_out_ref),
         (igate_ref, igate_out_ref),
     )
     moves = [pltpu.make_async_copy(source, target, sems.at[k]) for k, (source, target) in enumerate(moved)]
-    for move in (*moves[1:], moves[0]):
+    for move in moves:
         move.start()
     for copy in fetched:
         copy.wait()
@@ -98,7 +98,7 @@
                 weights.append(weight[:, :1])
             else:
                 weight_ref[step - 1, r] = weight
-    moves[1].wait()
+    moves[0].wait()
     lane = lax.broadcasted_iota(jnp.int32, (width, LANES), 1)
     for pair in range(count // 2):
         total = jnp.zeros((width, LANES), jnp.float32)
@@ -110,19 +110,16 @@
         out_ref = keep_ref if 4 * pair < count else send_ref
         begin = pair % (count // 4) * LANES
         out_ref[:, begin : begin + LANES] = total.astype(out_ref.dtype)
-    for move in moves[2:]:
+    for move in moves[1:]:
         move.wait()
     for r in range(rows):
         routed = jnp.sum(weights[r] * own[...].astype(jnp.float32), axis=0, keepdims=True)
         base_ref[r : r + 1, :] = residual[r : r + 1].astype(jnp.float32) + routed
-    moves[0].wait()
-
-
-def combine_down(
-    sources, place, base_ref, weight_ref, gain_ref, igate_ref, down_ref, *refs
-):
+
+
+def combine(sources, place, base_ref, weight_ref, gain_ref, igate_ref, *refs):
     received = refs[:sources]
-    hidden_ref, part_ref = refs[sources:]
+    hidden_ref, scaled_ref, side_ref = refs[sources:]
     rows = base_ref.shape[0]
     group = place[3]
     routed = [base_ref[r : r + 1, :] for r in range(rows)]
@@ -134,12 +131,11 @@
     hidden_ref[...] = hidden
     widened = hidden.astype(jnp.float32)
     scaled = (widened * gain_ref[...].reshape(1, -1)).astype(jnp.bfloat16)
-    qlora = down_ref.shape[1]
+    scaled_ref[...] = scaled
     squares = jnp.sum(widened * widened, axis=1, keepdims=True)
-    part_ref[:, qlora + LANES :] = jnp.broadcast_to(squares, (rows, LANES))
+    side_ref[:, LANES:] = jnp.broadcast_to(squares, (rows, LANES))
     gates = lax.dot_general(scaled, igate_ref[...], NT, preferred_element_type=jnp.float32)
-    part_ref[:, qlora : qlora + LANES] = jnp.concatenate([gates, gates], axis=1)
-    part_ref[:, :qlora] = jnp.dot(scaled, down_ref[...], preferred_element_type=jnp.float32)
+    side_ref[:, :LANES] = jnp.concatenate([gates, gates], axis=1)
 
 
 def attend_row(live, content, turn, cache):
@@ -160,10 +156,11 @@
 
 
 def finish(
-    pieces, place, live_ref, absorbed, rotary, first_ref, cache_ref, value_ref, limit_ref, gates_ref, keys_ref, *refs
+    pieces, place, live_ref, absorbed, rotary, first_ref, cache_ref, value_ref, limit_ref, gates_ref, keys_ref, held_ref, *refs
 ):
     gathered = refs[:pieces]
-    out_ref, scores_ref, queries = refs[pieces:]
+    out_ref, scores_ref, hidden_ref, queries = refs[pieces:]
+    hidden_ref[...] = held_ref[...]
     index_heads = gathered[0].shape[1]
     order = lax.broadcasted_iota(jnp.int32, (IHEADS, IHEADS), 0)
     head = order
@@ -232,7 +229,7 @@
     scalars = [h, c * (span // BLK), c % 2, d, (c * n_hp + h) * index_span, *sources]
     place = in_vmem(jnp.stack(scalars).astype(jnp.int32))
     half = pltpu.VMEM((width, selected // 2 * BLK), bf16)
-    mine, send, *ready, live, limit, gain, igate, down = pl.pallas_call(
+    mine, send, *ready, live, limit, gain, igate = pl.pallas_call(
         functools.partial(prepare, len(received)),
         out_shape=(
             half,
@@ -243,10 +240,9 @@
             pltpu.VMEM((rows, index_span), f32),
             pltpu.VMEM(attn_gain.shape, f32),
             pltpu.VMEM(index_gate.shape[::-1], bf16),
-            pltpu.VMEM(query_down.shape, bf16),
         ),
-        in_specs=[SMEM] + [HBM] * 10,
-        out_specs=(VMEM,) * 9,
+        in_specs=[SMEM] + [HBM] * 9,
+        out_specs=(VMEM,) * 8,
         scratch_shapes=[
             pltpu.SMEM(block_list.shape, jnp.int32),
             pltpu.SMEM(lengths.shape, jnp.int32),
@@ -256,37 +252,40 @@
             pltpu.VMEM(slots.shape[1:], bf16),
             pltpu.VMEM(residual.shape, bf16),
             pltpu.SemaphoreType.DMA((4,)),
-            pltpu.SemaphoreType.DMA((6,)),
+            pltpu.SemaphoreType.DMA((5,)),
         ],
         compiler_params=limits(6),
+        cost_estimate=pl.CostEstimate(flops=10000000000, bytes_accessed=0, transcendentals=0),
         name="prepare",
     )(
         place,
         *map(in_hbm, (block_list, lengths, combine_slot, combine_gate)),
-        *map(in_hbm, (jnp.swapaxes(latent_cache, 1, 2), slots, residual, attn_gain, index_gate.T, query_down)),
+        *map(in_hbm, (jnp.swapaxes(latent_cache, 1, 2), slots, residual, attn_gain, index_gate.T)),
     )
     upper, lower = (lax.ppermute(x, "ctx", swapped(n_ctx, 1)) for x in (send[: width // 2], send[width // 2 :]))
-    ready = [*ready, gain, igate, down]
+    ready = [*ready, gain, igate]
     received, ready = lax.optimization_barrier((received, ready))
 
-    hidden, part = pl.pallas_call(
-        functools.partial(combine_down, len(received)),
+    hidden, scaled, side = pl.pallas_call(
+        functools.partial(combine, len(received)),
         out_shape=(
-            jax.ShapeDtypeStruct((rows, features), bf16),
-            pltpu.VMEM((rows, qlora + 2 * LANES), f32),
+            pltpu.VMEM((rows, features), bf16),
+            pltpu.VMEM((rows, features), bf16),
+            pltpu.VMEM((rows, 2 * LANES), f32),
         ),
-        in_specs=[SMEM] + [VMEM] * (5 + len(received)),
-        out_specs=(VMEM, VMEM),
-        compiler_params=limits(8),
+        in_specs=[SMEM] + [VMEM] * (4 + len(received)),
+        out_specs=(VMEM, VMEM, VMEM),
+        compiler_params=limits(4),
         cost_estimate=pl.CostEstimate(flops=10000000000, bytes_accessed=0, transcendentals=0),
-        name="combine_down",
+        name="combine",
     )(place, *map(in_vmem, ready), *received)
+    part = jnp.concatenate([jnp.dot(scaled, query_down, preferred_element_type=f32), side], axis=1)
 
     mine, upper, lower, _ = lax.optimization_barrier((mine, upper, lower, part))
     mine = mine + jnp.concatenate([upper, lower], axis=0)
     crossed = [lax.ppermute(mine, "ctx", swapped(n_ctx, 2))]
 
-    parts = [part] + [lax.ppermute(part, "ctx", swapped(n_ctx, step)) for step in range(1, n_ctx)]
+    parts = [part] + [lax.ppermute(part, "ctx", swapped(n_ctx, step)) for step in range(n_ctx - 1, 0, -1)]
     total = functools.reduce(jnp.add, parts)
     scale = lax.rsqrt(total[:, qlora + LANES : qlora + LANES + 1] / D + epsilon)
     latent_sum = total[:, :qlora] * scale
@@ -296,6 +295,7 @@
 
     index_local = jnp.einsum("rq,qnd->nrd", latent, index_query, preferred_element_type=f32).astype(bf16)
     index_other = lax.ppermute(index_local, "hp", swapped(n_hp, 1))
+    index_local, latent = lax.optimization_barrier((index_local, latent))
     projected = jnp.einsum("rq,qnd->rnd", latent, query_up, preferred_element_type=f32).astype(bf16)
     absorbed = jnp.einsum("rnk,nkc->rnc", projected[:, :, :NOPE], key_absorb, preferred_element_type=f32).astype(bf16)
     rotary = projected[:, :, NOPE:]
@@ -323,20 +323,21 @@
         name="attend_first",
     )(place, *map(in_vmem, (live, absorbed, rotary, mine)))
     gathered, attended = lax.optimization_barrier((gathered, attended))
-    attn_out, index_scores = pl.pallas_call(
+    attn_out, index_scores, hidden = pl.pallas_call(
         functools.partial(finish, n_ctx),
         out_shape=(
             jax.ShapeDtypeStruct((rows, heads, value_up.shape[2]), bf16),
             jax.ShapeDtypeStruct((rows, index_span), f32),
+            jax.ShapeDtypeStruct((rows, features), bf16),
         ),
-        in_specs=[SMEM] + [VMEM] * (9 + n_ctx),
-        out_specs=(VMEM, VMEM),
+        in_specs=[SMEM] + [VMEM] * (10 + n_ctx),
+        out_specs=(VMEM, VMEM, VMEM),
         scratch_shapes=[pltpu.VMEM((rows, IHEADS, IDIM), f32)],
         compiler_params=limits(8),
         name="finish",
     )(
         place,
-        *map(in_vmem, (live, absorbed, rotary, attended, theirs, value_up, limit, head_gate, index_keys, *gathered)),
+        *map(in_vmem, (live, absorbed, rotary, attended, theirs, value_up, limit, head_gate, index_keys, hidden, *gathered)),
     )
     return (hidden, index_scores, attn_out)
 

time: 35.4 us -> 33.9 us (0.958)
  Pallas kernels: 8.05 us -> 6.12 us
  matrix products: 3.49 us -> 4.23 us
  starting transfers between devices: 18.7 us -> 18.3 us
    pallas_call x1, Pallas kernels: 3.52 us -> 2.27 us  [local(): pl.pallas_call(functools.partial(prepare, len(received)), out_shape=(half...]
    dot_general x0 -> x1, matrix products: none -> 0.81 us  [local(): jnp.dot(scaled, query_down, preferred_element_type=f32)]
    pallas_call x1, Pallas kernels: 1.52 us -> 0.84 us  [local(): pl.pallas_call(functools.partial(combine, len(received)), out_shape=(pltp...]
    ppermute x1, waiting for transfers between devices: 0.4 us -> 0.01 us  [local(): index_other = lax.ppermute(index_local, 'hp', swapped(n_hp, 1))]
    ppermute x1, starting transfers between devices: 1.5 us -> 1.13 us  [local(): theirs = lax.ppermute(mine, 'hp', swapped(n_hp, 1))]
    ppermute x1, waiting for transfers between devices: 1.37 us -> 1.74 us  [local(): other = lax.ppermute(mine, 'ctx', swapped(n_ctx, 1))]
  transfers between devices with their start and end apart: 13 -> 13, of which waited for: 4 -> 3; matrix products, arithmetic and copies ran while one was open for 12% -> 15% of each run, Pallas kernels for 17% -> 12%
where the time goes in v5:
time: 33.9 us; the launch traced here: 33.8 us
  starting transfers between devices  18.3 us (54%)
  Pallas kernels  6.12 us (18%)
  matrix products  4.23 us (12%)
  waiting for transfers between devices  2.95 us (9%)
  between operations  0.89 us (3%)
  other arithmetic  0.68 us (2%)
  local copies, waits for them, and re-layouts  0.58 us (2%)
    ppermute x1, starting transfers between devices, local(): index_other = lax.ppermute(index_local, 'hp', swapped(n_hp, 1))  4.08 us
    ppermute x3, starting transfers between devices, local(): lax.ppermute(part, 'ctx', swapped(n_ctx, step))  3.7 us
    ppermute x3, starting transfers between devices, local(): lax.ppermute(index_pair, 'ctx', swapped(n_ctx, step))  3.61 us
    dot_general x1, matrix products, local(): jnp.einsum('rq,qnd->rnd', latent, query_up, preferred_element_type=f32)  2.53 us
    pallas_call x1, Pallas kernels, local(): pl.pallas_call(functools.partial(prepare, len(received)), out_shape=(half...  2.27 us
    ppermute x1, starting transfers between devices, local(): lax.ppermute(slots, 'dp', shifted(n_dp, step))  2.11 us
    ppermute x1, starting transfers between devices, local(): crossed = [lax.ppermute(mine, 'ctx', swapped(n_ctx, 2))]  2.08 us
    pallas_call x1, Pallas kernels, local(): pl.pallas_call(functools.partial(finish, n_ctx), out_shape=(jax.ShapeDtyp...  2.04 us
  transfers between devices with their start and end apart: 13, of which 3 were waited for; matrix products, arithmetic and copies ran while one was open for 15% of the time, Pallas kernels for 12%

profile of v5, /device:TPU:1, one launch (start us, length us, event | category | flops | bytes accessed | tf_op | source)
XLA Modules:
  0.0 33.8 jit_solution(11162337994667324253)
XLA Ops:
  0.6 2.1 %collective-permute-start = (bf16[2,16,1792]{2,1,0:T(8,128)(2,1)}, bf16[2,16,1792]{2,1,0:T(8,128)(2,1)S(1)}, u32[]{:S(2)}, u32[]{:S(2)}) collective-permute-start(bf16[2,16,1792]{2,1,0:T(8,128)(2,1)} %bitcast.39), channel_id=1, source_target_pairs={{0,2},{2,0},{1,3},{3,1},{4,6},{6,4},{5,7},{7,5},{8,10},{10,8},{9,1... | collective-permute-start | bytes 344072 | tf_op jit(solution)/shard_map/ppermute | solution.py:225
  2.8 2.3 %prepare.1 = (bf16[576,128]{1,0:T(8,128)(2,1)S(1)}, bf16[576,128]{1,0:T(8,128)(2,1)S(1)}, f32[2,1792]{1,0:T(2,128)S(1)}, f32[1,2,16,128]{3,2,1,0:T(8,128)S(1)}, ...) custom-call(s32[9]{0:T(128)S(1)} %stack.48.place, ...), custom_call_target="tpu_custom_call" | custom-call | flops 10000000000 | tf_op jit(solution)/shard_map/prepare/pallas_call | solution.py:232
  5.2 1.3 %collective-permute-start.5 = (bf16[288,128]{1,0:T(8,128)(2,1)S(1)}, bf16[288,128]{1,0:T(8,128)(2,1)S(1)}, u32[]{:S(2)}, u32[]{:S(2)}) collective-permute-start(bf16[288,128]{1,0:T(8,128)(2,1)S(1)} %get-tuple-element.76), channel_id=1, source_target_pairs={{0,4},{4,0},{8,12},{12,8},{1,5},{5,1},{9,13},{13,9},{2,6},{6,2},{1... | collective-permute-start | bytes 221192 | tf_op jit(solution)/shard_map/ppermute | solution.py:265
  6.5 0.2 collective-permute-start.6
  6.7 0.8 %combine.1 = (bf16[2,1792]{1,0:T(2,128)(2,1)S(1)}, bf16[2,1792]{1,0:T(2,128)(2,1)S(1)}, f32[2,256]{1,0:T(2,128)S(1)}) custom-call(s32[9]{0:T(128)S(1)} %stack.48.place, f32[2,1792]{1,0:T(2,128)S(1)} %get-tuple-element.43.base_ref, f32[1,2,16,128]{3,2,1,0:T(8,128)S(1)} %get-tuple-element.44.weight_ref, f32[1792]{0:T(1024)S(1)} %get-tuple-element.45.gain_ref, ...), custom_call_target="tpu_custom_call" | custom-call | flops 10000000000 | tf_op jit(solution)/shard_map/combine/pallas_call | solution.py:269
  7.6 0.8 %fusion.18 = f32[2,1536]{1,0:T(2,128)S(1)} fusion(bf16[2,1792]{1,0:T(2,128)(2,1)S(1)} %get-tuple-element.48, bf16[1792,1536]{1,0:T(8,128)(2,1)S(1)} %bitcast.34), kind=kOutput, calls=%fused_computation.28 | convolution fusion | flops 11010048 | bytes 5524480 | tf_op jit(solution)/shard_map/dot_general | solution.py:282
  8.4 3.3 %collective-permute-start.1 = (f32[2,1792]{1,0:T(2,128)S(1)}, f32[2,1792]{1,0:T(2,128)S(1)}, u32[]{:S(2)}, u32[]{:S(2)}) collective-permute-start(f32[2,1792]{1,0:T(2,128)S(1)} %pad_maximum_fusion.1), channel_id=1, source_target_pairs={{0,12},{4,8},{8,4},{12,0},{1,13},{5,9},{9,5},{13,1},{2,14},{6,10},... | collective-permute-start | bytes 43016 | tf_op jit(solution)/shard_map/ppermute | solution.py:288
  11.8 0.4 %collective-permute-start.3 = (f32[2,1792]{1,0:T(2,128)S(1)}, f32[2,1792]{1,0:T(2,128)S(1)}, u32[]{:S(2)}, u32[]{:S(2)}) collective-permute-start(f32[2,1792]{1,0:T(2,128)S(1)} %pad_maximum_fusion.1), channel_id=1, source_target_pairs={{0,4},{4,0},{8,12},{12,8},{1,5},{5,1},{9,13},{13,9},{2,6},{6,2},{1... | collective-permute-start | bytes 43016 | tf_op jit(solution)/shard_map/ppermute | solution.py:288
  12.2 2.1 %collective-permute-start.7 = (bf16[576,128]{1,0:T(8,128)(2,1)S(1)}, bf16[576,128]{1,0:T(8,128)(2,1)S(1)}, u32[]{:S(2)}, u32[]{:S(2)}) collective-permute-start(bf16[576,128]{1,0:T(8,128)(2,1)S(1)} %maximum_add_fusion), channel_id=1, source_target_pairs={{0,8},{4,12},{8,0},{12,4},{1,9},{5,13},{9,1},{13,5},{2,10},{6,14},... | collective-permute-start | bytes 442376 | tf_op jit(solution)/shard_map/ppermute | solution.py:286
  14.3 1.0 %collective-permute-done.2 = f32[2,1792]{1,0:T(2,128)S(1)} collective-permute-done((f32[2,1792]{1,0:T(2,128)S(1)}, f32[2,1792]{1,0:T(2,128)S(1)}, u32[]{:S(2)}, u32[]{:S(2)}) %collective-permute-start.2) | collective-permute-done | bytes 14368 | tf_op jit(solution)/shard_map/ppermute | solution.py:288
  15.3 0.2 multiply_reduce_fusion.1
  15.4 0.2 multiply_reduce_fusion
  15.7 0.5 %fusion.5 = bf16[8,2,128]{2,1,0:T(2,128)(2,1)S(1)} fusion(bf16[1536,8,128]{2,1,0:T(8,128)(2,1)S(1)} %copy-done, bf16[2,1536]{1,0:T(2,128)(2,1)S(1)} %multiply_convert_fusion), kind=kOutput, calls=%fused_computation.3 | convolution fusion | flops 6293504 | bytes 3155968 | tf_op jit(solution)/shard_map/rq,qnd->nrd/dot_general | solution.py:296
  16.3 4.1 %collective-permute-start.4 = (bf16[8,2,128]{2,1,0:T(2,128)(2,1)S(1)}, bf16[8,2,128]{2,1,0:T(2,128)(2,1)S(1)}, u32[]{:S(2)}, u32[]{:S(2)}) collective-permute-start(bf16[8,2,128]{2,1,0:T(2,128)(2,1)S(1)} %fusion.5), channel_id=1, source_target_pairs={{0,1},{1,0},{2,3},{3,2},{4,5},{5,4},{6,7},{7,6},{8,9},{9,8},{10,11... | collective-permute-start | bytes 12296 | tf_op jit(solution)/shard_map/ppermute | solution.py:297
  20.4 2.5 %fusion.11 = bf16[2,16,192]{2,0,1:T(2,128)(2,1)S(1)} fusion(bf16[1536,16,192]{0,2,1:T(8,128)(2,1)S(1)} %bitcast.32, bf16[2,1536]{1,0:T(2,128)(2,1)S(1)} %multiply_convert_fusion), kind=kOutput, calls=%fused_computation.17 | convolution fusion | flops 18874368 | bytes 9455616 | tf_op jit(solution)/shard_map/rq,qnd->rnd/dot_general | solution.py:299
  22.9 0.4 %fusion.9 = bf16[16,2,512]{2,1,0:T(2,128)(2,1)S(1)} fusion(bf16[16,128,512]{2,1,0:T(8,128)(2,1)S(1)} %copy-done.3, bf16[2,16,128]{2,1,0:T(8,128)(2,1)S(1)} %copy.41), kind=kOutput, calls=%fused_computation.15 | convolution fusion | flops 4194304 | bytes 2138112 | tf_op jit(solution)/shard_map/rnk,nkc->rnc/dot_general | solution.py:300
  23.6 1.8 %collective-permute-start.10 = (bf16[2,8,2,128]{3,2,1,0:T(2,128)(2,1)S(1)}, bf16[2,8,2,128]{3,2,1,0:T(2,128)(2,1)S(1)}, u32[]{:S(2)}, u32[]{:S(2)}) collective-permute-start(bf16[2,8,2,128]{3,2,1,0:T(2,128)(2,1)S(1)} %pad_maximum_fusion.2.refs_0_), channel_id=1, source_target_pairs={{0,12},{4,8},{8,4},{12,0},{1,13},{5,9},{9,5},{13,1},{2,14},{6,10},... | collective-permute-start | bytes 24584 | tf_op jit(solution)/shard_map/ppermute | solution.py:306
  25.5 1.8 %collective-permute-start.9 = (bf16[2,8,2,128]{3,2,1,0:T(2,128)(2,1)S(1)}, bf16[2,8,2,128]{3,2,1,0:T(2,128)(2,1)S(1)}, u32[]{:S(2)}, u32[]{:S(2)}) collective-permute-start(bf16[2,8,2,128]{3,2,1,0:T(2,128)(2,1)S(1)} %pad_maximum_fusion.2.refs_0_), channel_id=1, source_target_pairs={{0,8},{4,12},{8,0},{12,4},{1,9},{5,13},{9,1},{13,5},{2,10},{6,14},... | collective-permute-start | bytes 24584 | tf_op jit(solution)/shard_map/ppermute | solution.py:306
  27.2 1.7 %collective-permute-done.11 = bf16[576,128]{1,0:T(8,128)(2,1)S(1)} collective-permute-done((bf16[576,128]{1,0:T(8,128)(2,1)S(1)}, bf16[576,128]{1,0:T(8,128)(2,1)S(1)}, u32[]{:S(2)}, u32[]{:S(2)}) %collective-permute-start.11) | collective-permute-done | bytes 147488 | tf_op jit(solution)/shard_map/ppermute | solution.py:313
  29.0 1.1 %collective-permute-start.12 = (bf16[576,256]{1,0:T(8,128)(2,1)S(1)}, bf16[576,256]{1,0:T(8,128)(2,1)S(1)}, u32[]{:S(2)}, u32[]{:S(2)}) collective-permute-start(bf16[576,256]{1,0:T(8,128)(2,1)S(1)} %pad_maximum_fusion.cache_ref), channel_id=1, source_target_pairs={{0,1},{1,0},{2,3},{3,2},{4,5},{5,4},{6,7},{7,6},{8,9},{9,8},{10,11... | collective-permute-start | bytes 884744 | tf_op jit(solution)/shard_map/ppermute | solution.py:315
  30.1 1.0 %attend_first.1.first_ref = f32[16,512]{1,0:T(8,128)S(1)} custom-call(s32[9]{0:T(128)S(1)} %stack.48.place, f32[2,256]{1,0:T(2,128)S(1)} %get-tuple-element.38.live_ref, bf16[2,16,512]{2,1,0:T(8,128)(2,1)S(1)} %bitcast.29, bf16[2,16,64]{2,1,0:T(8,128)(2,1)S(1)} %copy.42.rotary, bf16[576,256]{1,0:T(8,128)(2,1)S(1)} %pad_maximum_fusion.cache_ref), custom_call_target="tpu_custom_call" | custom-call | flops 20000000000 | tf_op jit(solution)/shard_map/attend_first/pallas_call | solution.py:316
  31.2 0.2 collective-permute-done.12.cache_ref
  31.3 0.4 %copy-done.1 = bf16[16,512,128]{2,1,0:T(8,128)(2,1)S(1)} copy-done((bf16[16,512,128]{2,1,0:T(8,128)(2,1)S(1)}, bf16[16,512,128]{2,1,0:T(8,128)(2,1)}, u32[]{:S(2)}) %copy-start.1) | copy-done | bytes 2097176
  31.7 2.0 %finish.1 = (bf16[2,16,128]{2,1,0:T(8,128)(2,1)}, f32[2,256]{1,0:T(2,128)}, bf16[2,1792]{1,0:T(2,128)(2,1)}) custom-call(s32[9]{0:T(128)S(1)} %stack.48.place, f32[2,256]{1,0:T(2,128)S(1)} %get-tuple-element.38.live_ref, bf16[2,16,512]{2,1,0:T(8,128)(2,1)S(1)} %bitcast.30, bf16[2,16,64]{2,1,0:T(8,128)(2,1)S(1)} %copy.42.rotary, ...), custom_call_target="tpu_custom_call" | custom-call | tf_op jit(solution)/shard_map/finish/pallas_call | solution.py:326
  (50 shorter events, 0.7 us)
Async XLA Ops:
  0.6 15.1 %copy-start = (bf16[1536,8,128]{2,1,0:T(8,128)(2,1)S(1)}, bf16[1536,8,128]{2,1,0:T(8,128)(2,1)}, u32[]{:S(2)}) copy-start(bf16[1536,8,128]{2,1,0:T(8,128)(2,1)} %param.26) | copy-start | bytes 9437188
  0.6 6.0 %collective-permute-start = (bf16[2,16,1792]{2,1,0:T(8,128)(2,1)}, bf16[2,16,1792]{2,1,0:T(8,128)(2,1)S(1)}, u32[]{:S(2)}, u32[]{:S(2)}) collective-permute-start(bf16[2,16,1792]{2,1,0:T(8,128)(2,1)} %bitcast.39), channel_id=1, source_target_pairs={{0,2},{2,0},{1,3},{3,1},{4,6},{6,4},{5,7},{7,5},{8,10},{10,8},{9,1... | collective-permute-start | bytes 344072 | tf_op jit(solution)/shard_map/ppermute | solution.py:225
  2.8 4.7 %slice-start.3 = ((s8[5505024]{0:T(1024)(128)(4,1)}), s8[4194304]{0:T(1024)(128)(4,1)S(1)}, s32[]{:S(2)}) async-start(s8[5505024]{0:T(1024)(128)(4,1)} %bitcast.33), calls=%async_computation.3 | async-start | bytes 8388608
  5.1 2.4 %slice-start.4 = ((s8[5505024]{0:T(1024)(128)(4,1)}), s8[1310720]{0:T(1024)(128)(4,1)S(1)}, s32[]{:S(2)}) async-start(s8[5505024]{0:T(1024)(128)(4,1)} %bitcast.33), calls=%async_computation.4 | async-start | bytes 2621440
  5.2 7.0 %collective-permute-start.5 = (bf16[288,128]{1,0:T(8,128)(2,1)S(1)}, bf16[288,128]{1,0:T(8,128)(2,1)S(1)}, u32[]{:S(2)}, u32[]{:S(2)}) collective-permute-start(bf16[288,128]{1,0:T(8,128)(2,1)S(1)} %get-tuple-element.76), channel_id=1, source_target_pairs={{0,4},{4,0},{8,12},{12,8},{1,5},{5,1},{9,13},{13,9},{2,6},{6,2},{1... | collective-permute-start | bytes 221192 | tf_op jit(solution)/shard_map/ppermute | solution.py:265
  6.5 5.7 %collective-permute-start.6 = (bf16[288,128]{1,0:T(8,128)(2,1)S(1)}, bf16[288,128]{1,0:T(8,128)(2,1)S(1)}, u32[]{:S(2)}, u32[]{:S(2)}) collective-permute-start(bf16[288,128]{1,0:T(8,128)(2,1)S(1)} %get-tuple-element.75), channel_id=1, source_target_pairs={{0,4},{4,0},{8,12},{12,8},{1,5},{5,1},{9,13},{13,9},{2,6},{6,2},{1... | collective-permute-start | bytes 221192 | tf_op jit(solution)/shard_map/ppermute | solution.py:265
  6.7 13.7 %slice-start = ((s8[9437184]{0:T(1024)(128)(4,1)}), s8[4194304]{0:T(1024)(128)(4,1)S(1)}, s32[]{:S(2)}) async-start(s8[9437184]{0:T(1024)(128)(4,1)} %bitcast.31), calls=%async_computation | async-start | bytes 8388608
  6.7 13.7 %slice-start.1 = ((s8[9437184]{0:T(1024)(128)(4,1)}), s8[4194304]{0:T(1024)(128)(4,1)S(1)}, s32[]{:S(2)}) async-start(s8[9437184]{0:T(1024)(128)(4,1)} %bitcast.31), calls=%async_computation.1 | async-start | bytes 8388608
  6.7 13.7 %slice-start.2 = ((s8[9437184]{0:T(1024)(128)(4,1)}), s8[1048576]{0:T(1024)(128)(4,1)S(1)}, s32[]{:S(2)}) async-start(s8[9437184]{0:T(1024)(128)(4,1)} %bitcast.31), calls=%async_computation.2 | async-start | bytes 2097152
  7.5 8.1 %copy-start.4 = (f32[1536]{0:T(1024)S(1)}, f32[1536]{0:T(1024)}, u32[]{:S(2)}) copy-start(f32[1536]{0:T(1024)} %param.23) | copy-start | bytes 18436
  8.4 5.8 %collective-permute-start.1 = (f32[2,1792]{1,0:T(2,128)S(1)}, f32[2,1792]{1,0:T(2,128)S(1)}, u32[]{:S(2)}, u32[]{:S(2)}) collective-permute-start(f32[2,1792]{1,0:T(2,128)S(1)} %pad_maximum_fusion.1), channel_id=1, source_target_pairs={{0,12},{4,8},{8,4},{12,0},{1,13},{5,9},{9,5},{13,1},{2,14},{6,10},... | collective-permute-start | bytes 43016 | tf_op jit(solution)/shard_map/ppermute | solution.py:288
  11.8 3.5 %collective-permute-start.2 = (f32[2,1792]{1,0:T(2,128)S(1)}, f32[2,1792]{1,0:T(2,128)S(1)}, u32[]{:S(2)}, u32[]{:S(2)}) collective-permute-start(f32[2,1792]{1,0:T(2,128)S(1)} %pad_maximum_fusion.1), channel_id=1, source_target_pairs={{0,8},{4,12},{8,0},{12,4},{1,9},{5,13},{9,1},{13,5},{2,10},{6,14},... | collective-permute-start | bytes 43016 | tf_op jit(solution)/shard_map/ppermute | solution.py:288
  11.8 3.5 %collective-permute-start.3 = (f32[2,1792]{1,0:T(2,128)S(1)}, f32[2,1792]{1,0:T(2,128)S(1)}, u32[]{:S(2)}, u32[]{:S(2)}) collective-permute-start(f32[2,1792]{1,0:T(2,128)S(1)} %pad_maximum_fusion.1), channel_id=1, source_target_pairs={{0,4},{4,0},{8,12},{12,8},{1,5},{5,1},{9,13},{13,9},{2,6},{6,2},{1... | collective-permute-start | bytes 43016 | tf_op jit(solution)/shard_map/ppermute | solution.py:288
  12.2 11.2 %collective-permute-start.7 = (bf16[576,128]{1,0:T(8,128)(2,1)S(1)}, bf16[576,128]{1,0:T(8,128)(2,1)S(1)}, u32[]{:S(2)}, u32[]{:S(2)}) collective-permute-start(bf16[576,128]{1,0:T(8,128)(2,1)S(1)} %maximum_add_fusion), channel_id=1, source_target_pairs={{0,8},{4,12},{8,0},{12,4},{1,9},{5,13},{9,1},{13,5},{2,10},{6,14},... | collective-permute-start | bytes 442376 | tf_op jit(solution)/shard_map/ppermute | solution.py:286
  16.3 6.7 %copy-start.3 = (bf16[16,128,512]{2,1,0:T(8,128)(2,1)S(1)}, bf16[16,128,512]{2,1,0:T(8,128)(2,1)}, u32[]{:S(2)}) copy-start(bf16[16,128,512]{2,1,0:T(8,128)(2,1)} %param.25) | copy-start | bytes 6291460
  16.3 7.1 %collective-permute-start.4 = (bf16[8,2,128]{2,1,0:T(2,128)(2,1)S(1)}, bf16[8,2,128]{2,1,0:T(2,128)(2,1)S(1)}, u32[]{:S(2)}, u32[]{:S(2)}) collective-permute-start(bf16[8,2,128]{2,1,0:T(2,128)(2,1)S(1)} %fusion.5), channel_id=1, source_target_pairs={{0,1},{1,0},{2,3},{3,2},{4,5},{5,4},{6,7},{7,6},{8,9},{9,8},{10,11... | collective-permute-start | bytes 12296 | tf_op jit(solution)/shard_map/ppermute | solution.py:297
  23.4 5.5 %collective-permute-start.11 = (bf16[576,128]{1,0:T(8,128)(2,1)S(1)}, bf16[576,128]{1,0:T(8,128)(2,1)S(1)}, u32[]{:S(2)}, u32[]{:S(2)}) collective-permute-start(bf16[576,128]{1,0:T(8,128)(2,1)S(1)} %add.41), channel_id=1, source_target_pairs={{0,4},{4,0},{8,12},{12,8},{1,5},{5,1},{9,13},{13,9},{2,6},{6,2},{1... | collective-permute-start | bytes 442376 | tf_op jit(solution)/shard_map/ppermute | solution.py:313
  23.6 7.5 %collective-permute-start.10 = (bf16[2,8,2,128]{3,2,1,0:T(2,128)(2,1)S(1)}, bf16[2,8,2,128]{3,2,1,0:T(2,128)(2,1)S(1)}, u32[]{:S(2)}, u32[]{:S(2)}) collective-permute-start(bf16[2,8,2,128]{3,2,1,0:T(2,128)(2,1)S(1)} %pad_maximum_fusion.2.refs_0_), channel_id=1, source_target_pairs={{0,12},{4,8},{8,4},{12,0},{1,13},{5,9},{9,5},{13,1},{2,14},{6,10},... | collective-permute-start | bytes 24584 | tf_op jit(solution)/shard_map/ppermute | solution.py:306
  25.4 5.7 %collective-permute-start.8 = (bf16[2,8,2,128]{3,2,1,0:T(2,128)(2,1)S(1)}, bf16[2,8,2,128]{3,2,1,0:T(2,128)(2,1)S(1)}, u32[]{:S(2)}, u32[]{:S(2)}) collective-permute-start(bf16[2,8,2,128]{3,2,1,0:T(2,128)(2,1)S(1)} %pad_maximum_fusion.2.refs_0_), channel_id=1, source_target_pairs={{0,4},{4,0},{8,12},{12,8},{1,5},{5,1},{9,13},{13,9},{2,6},{6,2},{1... | collective-permute-start | bytes 24584 | tf_op jit(solution)/shard_map/ppermute | solution.py:306
  25.5 5.7 %collective-permute-start.9 = (bf16[2,8,2,128]{3,2,1,0:T(2,128)(2,1)S(1)}, bf16[2,8,2,128]{3,2,1,0:T(2,128)(2,1)S(1)}, u32[]{:S(2)}, u32[]{:S(2)}) collective-permute-start(bf16[2,8,2,128]{3,2,1,0:T(2,128)(2,1)S(1)} %pad_maximum_fusion.2.refs_0_), channel_id=1, source_target_pairs={{0,8},{4,12},{8,0},{12,4},{1,9},{5,13},{9,1},{13,5},{2,10},{6,14},... | collective-permute-start | bytes 24584 | tf_op jit(solution)/shard_map/ppermute | solution.py:306
  29.0 2.3 %collective-permute-start.12 = (bf16[576,256]{1,0:T(8,128)(2,1)S(1)}, bf16[576,256]{1,0:T(8,128)(2,1)S(1)}, u32[]{:S(2)}, u32[]{:S(2)}) collective-permute-start(bf16[576,256]{1,0:T(8,128)(2,1)S(1)} %pad_maximum_fusion.cache_ref), channel_id=1, source_target_pairs={{0,1},{1,0},{2,3},{3,2},{4,5},{5,4},{6,7},{7,6},{8,9},{9,8},{10,11... | collective-permute-start | bytes 884744 | tf_op jit(solution)/shard_map/ppermute | solution.py:315
  30.1 1.6 %copy-start.1 = (bf16[16,512,128]{2,1,0:T(8,128)(2,1)S(1)}, bf16[16,512,128]{2,1,0:T(8,128)(2,1)}, u32[]{:S(2)}) copy-start(bf16[16,512,128]{2,1,0:T(8,128)(2,1)} %value_ref.1) | copy-start | bytes 6291460
  30.1 1.6 %copy-start.2 = (bf16[2,256,128]{2,1,0:T(8,128)(2,1)S(1)}, bf16[2,256,128]{2,1,0:T(8,128)(2,1)}, u32[]{:S(2)}) copy-start(bf16[2,256,128]{2,1,0:T(8,128)(2,1)} %keys_ref.1) | copy-start | bytes 393220

commit v6 on v5

--- a/solution.py
+++ b/solution.py
@@ -225,7 +225,7 @@
     received = [lax.ppermute(slots, "dp", shifted(n_dp, step)) for step in range(1, n_dp)]
 
     index_heads, index_span = index_query.shape[1], index_keys.shape[1]
-    sources = [jnp.bitwise_xor(c, step) * n_hp * index_heads for step in range(n_ctx)]
+    sources = [jnp.bitwise_xor(c, step) * n_hp * index_heads for step in (0, *range(n_ctx - 1, 0, -1))]
     scalars = [h, c * (span // BLK), c % 2, d, (c * n_hp + h) * index_span, *sources]
     place = in_vmem(jnp.stack(scalars).astype(jnp.int32))
     half = pltpu.VMEM((width, selected // 2 * BLK), bf16)
@@ -262,7 +262,7 @@
         *map(in_hbm, (block_list, lengths, combine_slot, combine_gate)),
         *map(in_hbm, (jnp.swapaxes(latent_cache, 1, 2), slots, residual, attn_gain, index_gate.T)),
     )
-    upper, lower = (lax.ppermute(x, "ctx", swapped(n_ctx, 1)) for x in (send[: width // 2], send[width // 2 :]))
+    neighbour = lax.ppermute(send, "ctx", swapped(n_ctx, 1))
     ready = [*ready, gain, igate]
     received, ready = lax.optimization_barrier((received, ready))
 
@@ -281,11 +281,13 @@
     )(place, *map(in_vmem, ready), *received)
     part = jnp.concatenate([jnp.dot(scaled, query_down, preferred_element_type=f32), side], axis=1)
 
-    mine, upper, lower, _ = lax.optimization_barrier((mine, upper, lower, part))
-    mine = mine + jnp.concatenate([upper, lower], axis=0)
+    mine, neighbour, _ = lax.optimization_barrier((mine, neighbour, part))
+    mine = mine + neighbour
+    mine, near = lax.optimization_barrier((mine, part))
     crossed = [lax.ppermute(mine, "ctx", swapped(n_ctx, 2))]
 
-    parts = [part] + [lax.ppermute(part, "ctx", swapped(n_ctx, step)) for step in range(n_ctx - 1, 0, -1)]
+    parts = [part] + [lax.ppermute(part, "ctx", swapped(n_ctx, step)) for step in range(n_ctx - 1, 1, -1)]
+    parts.append(lax.ppermute(near, "ctx", swapped(n_ctx, 1)))
     total = functools.reduce(jnp.add, parts)
     scale = lax.rsqrt(total[:, qlora + LANES : qlora + LANES + 1] / D + epsilon)
     latent_sum = total[:, :qlora] * scale
@@ -303,7 +305,7 @@
         (index_local, index_other, mine, crossed, absorbed, rotary)
     )
     index_pair = jnp.stack([index_local, index_other])
-    gathered = [index_pair] + [lax.ppermute(index_pair, "ctx", swapped(n_ctx, step)) for step in range(1, n_ctx)]
+    gathered = [index_pair] + [lax.ppermute(index_pair, "ctx", swapped(n_ctx, step)) for step in range(n_ctx - 1, 0, -1)]
 
     mine = functools.reduce(jnp.add, crossed, mine)
     bit = 4

time: 33.9 us -> 33.5 us (0.988)
  starting transfers between devices: 18.3 us -> 17.4 us
  local copies, waits for them, and re-layouts: 0.58 us -> 1.01 us
    ppermute x3 -> x2, starting transfers between devices: 3.7 us -> 2.72 us  [local(): lax.ppermute(part, 'ctx', swapped(n_ctx, step))]
    ppermute x2, starting transfers between devices: 1.53 us -> 2.28 us  [the longest x1 1.31 us: local(): neighbour = lax.ppermute(send, 'ctx', swapped(n_ctx, 1))]
    ppermute x1, starting transfers between devices: 2.08 us -> 1.54 us  [local(): crossed = [lax.ppermute(mine, 'ctx', swapped(n_ctx, 2))]]
    unnamed x21, local copies, waits for them, and re-layouts: 0.43 us -> 0.88 us
    ppermute x3 -> x2, waiting for transfers between devices: 0.97 us -> 1.15 us  [local(): lax.ppermute(part, 'ctx', swapped(n_ctx, step))]
  transfers between devices with their start and end apart: 13 -> 12, of which waited for: 3 -> 3; matrix products, arithmetic and copies ran while one was open for 15% -> 15% of each run, Pallas kernels for 12% -> 12%
where the time goes in v6:
time: 33.5 us; the launch traced here: 33.4 us
  starting transfers between devices  17.4 us (52%)
  Pallas kernels  6.12 us (18%)
  matrix products  4.23 us (13%)
  waiting for transfers between devices  3.12 us (9%)
  local copies, waits for them, and re-layouts  1.01 us (3%)
  between operations  0.83 us (2%)
  other arithmetic  0.68 us (2%)
    ppermute x1, starting transfers between devices, local(): index_other = lax.ppermute(index_local, 'hp', swapped(n_hp, 1))  3.93 us
    ppermute x3, starting transfers between devices, local(): lax.ppermute(index_pair, 'ctx', swapped(n_ctx, step))  3.61 us
    ppermute x2, starting transfers between devices, local(): lax.ppermute(part, 'ctx', swapped(n_ctx, step))  2.72 us
    dot_general x1, matrix products, local(): jnp.einsum('rq,qnd->rnd', latent, query_up, preferred_element_type=f32)  2.53 us
    pallas_call x1, Pallas kernels, local(): pl.pallas_call(functools.partial(prepare, len(received)), out_shape=(half...  2.27 us
    ppermute x1, starting transfers between devices, local(): lax.ppermute(slots, 'dp', shifted(n_dp, step))  2.11 us
    pallas_call x1, Pallas kernels, local(): pl.pallas_call(functools.partial(finish, n_ctx), out_shape=(jax.ShapeDtyp...  2.04 us
    ppermute x1, waiting for transfers between devices, local(): other = lax.ppermute(mine, 'ctx', swapped(n_ctx, 1))  1.74 us
  transfers between devices with their start and end apart: 12, of which 3 were waited for; matrix products, arithmetic and copies ran while one was open for 15% of the time, Pallas kernels for 12%

profile of v6, /device:TPU:1, one launch (start us, length us, event | category | flops | bytes accessed | tf_op | source)
XLA Modules:
  0.0 33.4 jit_solution(17797181319724058871)
XLA Ops:
  0.6 2.1 %collective-permute-start = (bf16[2,16,1792]{2,1,0:T(8,128)(2,1)}, bf16[2,16,1792]{2,1,0:T(8,128)(2,1)S(1)}, u32[]{:S(2)}, u32[]{:S(2)}) collective-permute-start(bf16[2,16,1792]{2,1,0:T(8,128)(2,1)} %bitcast.39), channel_id=1, source_target_pairs={{0,2},{2,0},{1,3},{3,1},{4,6},{6,4},{5,7},{7,5},{8,10},{10,8},{9,1... | collective-permute-start | bytes 344072 | tf_op jit(solution)/shard_map/ppermute | solution.py:225
  2.8 2.3 %prepare.1 = (bf16[576,128]{1,0:T(8,128)(2,1)S(1)}, bf16[576,128]{1,0:T(8,128)(2,1)S(1)}, f32[2,1792]{1,0:T(2,128)S(1)}, f32[1,2,16,128]{3,2,1,0:T(8,128)S(1)}, ...) custom-call(s32[9]{0:T(128)S(1)} %stack.48.place, ...), custom_call_target="tpu_custom_call" | custom-call | flops 10000000000 | tf_op jit(solution)/shard_map/prepare/pallas_call | solution.py:232
  5.1 1.3 %collective-permute-start.3 = (bf16[576,128]{1,0:T(8,128)(2,1)S(1)}, bf16[576,128]{1,0:T(8,128)(2,1)S(1)}, u32[]{:S(2)}, u32[]{:S(2)}) collective-permute-start(bf16[576,128]{1,0:T(8,128)(2,1)S(1)} %get-tuple-element.52), channel_id=1, source_target_pairs={{0,4},{4,0},{8,12},{12,8},{1,5},{5,1},{9,13},{13,9},{2,6},{6,2},{1... | collective-permute-start | bytes 442376 | tf_op jit(solution)/shard_map/ppermute | solution.py:265
  6.5 0.8 %combine.1 = (bf16[2,1792]{1,0:T(2,128)(2,1)S(1)}, bf16[2,1792]{1,0:T(2,128)(2,1)S(1)}, f32[2,256]{1,0:T(2,128)S(1)}) custom-call(s32[9]{0:T(128)S(1)} %stack.48.place, f32[2,1792]{1,0:T(2,128)S(1)} %get-tuple-element.44.base_ref, f32[1,2,16,128]{3,2,1,0:T(8,128)S(1)} %get-tuple-element.45.weight_ref, f32[1792]{0:T(1024)S(1)} %get-tuple-element.46.gain_ref, ...), custom_call_target="tpu_custom_call" | custom-call | flops 10000000000 | tf_op jit(solution)/shard_map/combine/pallas_call | solution.py:269
  7.3 0.5 %slice-done.4 = s8[1310720]{0:T(1024)(128)(4,1)S(1)} async-done(((s8[5505024]{0:T(1024)(128)(4,1)}), s8[1310720]{0:T(1024)(128)(4,1)S(1)}, s32[]{:S(2)}) %slice-start.4) | async-done | bytes 1310744
  7.8 0.8 %fusion.17 = f32[2,1536]{1,0:T(2,128)S(1)} fusion(bf16[2,1792]{1,0:T(2,128)(2,1)S(1)} %get-tuple-element.49, bf16[1792,1536]{1,0:T(8,128)(2,1)S(1)} %bitcast.34), kind=kOutput, calls=%fused_computation.26 | convolution fusion | flops 11010048 | bytes 5524480 | tf_op jit(solution)/shard_map/dot_general | solution.py:282
  8.6 2.7 %collective-permute-start.1 = (f32[2,1792]{1,0:T(2,128)S(1)}, f32[2,1792]{1,0:T(2,128)S(1)}, u32[]{:S(2)}, u32[]{:S(2)}) collective-permute-start(f32[2,1792]{1,0:T(2,128)S(1)} %pad_maximum_fusion.1), channel_id=1, source_target_pairs={{0,12},{4,8},{8,4},{12,0},{1,13},{5,9},{9,5},{13,1},{2,14},{6,10},... | collective-permute-start | bytes 43016 | tf_op jit(solution)/shard_map/ppermute | solution.py:289
  11.4 1.0 %collective-permute-start.4 = (f32[2,1792]{1,0:T(2,128)S(1)}, f32[2,1792]{1,0:T(2,128)S(1)}, u32[]{:S(2)}, u32[]{:S(2)}) collective-permute-start(f32[2,1792]{1,0:T(2,128)S(1)} %pad_maximum_fusion.1), channel_id=1, source_target_pairs={{0,4},{4,0},{8,12},{12,8},{1,5},{5,1},{9,13},{13,9},{2,6},{6,2},{1... | collective-permute-start | bytes 43016 | tf_op jit(solution)/shard_map/ppermute | solution.py:290
  12.3 1.5 %collective-permute-start.6 = (bf16[576,128]{1,0:T(8,128)(2,1)S(1)}, bf16[576,128]{1,0:T(8,128)(2,1)S(1)}, u32[]{:S(2)}, u32[]{:S(2)}) collective-permute-start(bf16[576,128]{1,0:T(8,128)(2,1)S(1)} %add.37), channel_id=1, source_target_pairs={{0,8},{4,12},{8,0},{12,4},{1,9},{5,13},{9,1},{13,5},{2,10},{6,14},... | collective-permute-start | bytes 442376 | tf_op jit(solution)/shard_map/ppermute | solution.py:287
  13.9 1.1 %collective-permute-done.2 = f32[2,1792]{1,0:T(2,128)S(1)} collective-permute-done((f32[2,1792]{1,0:T(2,128)S(1)}, f32[2,1792]{1,0:T(2,128)S(1)}, u32[]{:S(2)}, u32[]{:S(2)}) %collective-permute-start.2) | collective-permute-done | bytes 14368 | tf_op jit(solution)/shard_map/ppermute | solution.py:289
  15.2 0.2 multiply_reduce_fusion
  15.5 0.5 %fusion.5 = bf16[8,2,128]{2,1,0:T(2,128)(2,1)S(1)} fusion(bf16[1536,8,128]{2,1,0:T(8,128)(2,1)S(1)} %copy-done, bf16[2,1536]{1,0:T(2,128)(2,1)S(1)} %multiply_convert_fusion), kind=kOutput, calls=%fused_computation.3 | convolution fusion | flops 6293504 | bytes 3155968 | tf_op jit(solution)/shard_map/rq,qnd->nrd/dot_general | solution.py:298
  16.0 3.9 %collective-permute-start.5 = (bf16[8,2,128]{2,1,0:T(2,128)(2,1)S(1)}, bf16[8,2,128]{2,1,0:T(2,128)(2,1)S(1)}, u32[]{:S(2)}, u32[]{:S(2)}) collective-permute-start(bf16[8,2,128]{2,1,0:T(2,128)(2,1)S(1)} %fusion.5), channel_id=1, source_target_pairs={{0,1},{1,0},{2,3},{3,2},{4,5},{5,4},{6,7},{7,6},{8,9},{9,8},{10,11... | collective-permute-start | bytes 12296 | tf_op jit(solution)/shard_map/ppermute | solution.py:299
  20.0 2.5 %fusion.11 = bf16[2,16,192]{2,0,1:T(2,128)(2,1)S(1)} fusion(bf16[1536,16,192]{0,2,1:T(8,128)(2,1)S(1)} %bitcast.32, bf16[2,1536]{1,0:T(2,128)(2,1)S(1)} %multiply_convert_fusion), kind=kOutput, calls=%fused_computation.16 | convolution fusion | flops 18874368 | bytes 9455616 | tf_op jit(solution)/shard_map/rq,qnd->rnd/dot_general | solution.py:301
  22.5 0.4 %fusion.9 = bf16[16,2,512]{2,1,0:T(2,128)(2,1)S(1)} fusion(bf16[16,128,512]{2,1,0:T(8,128)(2,1)S(1)} %copy-done.3, bf16[2,16,128]{2,1,0:T(8,128)(2,1)S(1)} %copy.41), kind=kOutput, calls=%fused_computation.14 | convolution fusion | flops 4194304 | bytes 2138112 | tf_op jit(solution)/shard_map/rnk,nkc->rnc/dot_general | solution.py:302
  23.2 1.9 %collective-permute-start.7 = (bf16[2,8,2,128]{3,2,1,0:T(2,128)(2,1)S(1)}, bf16[2,8,2,128]{3,2,1,0:T(2,128)(2,1)S(1)}, u32[]{:S(2)}, u32[]{:S(2)}) collective-permute-start(bf16[2,8,2,128]{3,2,1,0:T(2,128)(2,1)S(1)} %pad_maximum_fusion.2.refs_0_), channel_id=1, source_target_pairs={{0,12},{4,8},{8,4},{12,0},{1,13},{5,9},{9,5},{13,1},{2,14},{6,10},... | collective-permute-start | bytes 24584 | tf_op jit(solution)/shard_map/ppermute | solution.py:308
  25.1 0.8 %collective-permute-start.8 = (bf16[2,8,2,128]{3,2,1,0:T(2,128)(2,1)S(1)}, bf16[2,8,2,128]{3,2,1,0:T(2,128)(2,1)S(1)}, u32[]{:S(2)}, u32[]{:S(2)}) collective-permute-start(bf16[2,8,2,128]{3,2,1,0:T(2,128)(2,1)S(1)} %pad_maximum_fusion.2.refs_0_), channel_id=1, source_target_pairs={{0,8},{4,12},{8,0},{12,4},{1,9},{5,13},{9,1},{13,5},{2,10},{6,14},... | collective-permute-start | bytes 24584 | tf_op jit(solution)/shard_map/ppermute | solution.py:308
  25.9 0.9 %collective-permute-start.9 = (bf16[2,8,2,128]{3,2,1,0:T(2,128)(2,1)S(1)}, bf16[2,8,2,128]{3,2,1,0:T(2,128)(2,1)S(1)}, u32[]{:S(2)}, u32[]{:S(2)}) collective-permute-start(bf16[2,8,2,128]{3,2,1,0:T(2,128)(2,1)S(1)} %pad_maximum_fusion.2.refs_0_), channel_id=1, source_target_pairs={{0,4},{4,0},{8,12},{12,8},{1,5},{5,1},{9,13},{13,9},{2,6},{6,2},{1... | collective-permute-start | bytes 24584 | tf_op jit(solution)/shard_map/ppermute | solution.py:308
  26.8 1.7 %collective-permute-done.10 = bf16[576,128]{1,0:T(8,128)(2,1)S(1)} collective-permute-done((bf16[576,128]{1,0:T(8,128)(2,1)S(1)}, bf16[576,128]{1,0:T(8,128)(2,1)S(1)}, u32[]{:S(2)}, u32[]{:S(2)}) %collective-permute-start.10) | collective-permute-done | bytes 147488 | tf_op jit(solution)/shard_map/ppermute | solution.py:315
  28.6 1.1 %collective-permute-start.11 = (bf16[576,256]{1,0:T(8,128)(2,1)S(1)}, bf16[576,256]{1,0:T(8,128)(2,1)S(1)}, u32[]{:S(2)}, u32[]{:S(2)}) collective-permute-start(bf16[576,256]{1,0:T(8,128)(2,1)S(1)} %pad_maximum_fusion.cache_ref), channel_id=1, source_target_pairs={{0,1},{1,0},{2,3},{3,2},{4,5},{5,4},{6,7},{7,6},{8,9},{9,8},{10,11... | collective-permute-start | bytes 884744 | tf_op jit(solution)/shard_map/ppermute | solution.py:317
  29.7 1.0 %attend_first.1.first_ref = f32[16,512]{1,0:T(8,128)S(1)} custom-call(s32[9]{0:T(128)S(1)} %stack.48.place, f32[2,256]{1,0:T(2,128)S(1)} %get-tuple-element.39.live_ref, bf16[2,16,512]{2,1,0:T(8,128)(2,1)S(1)} %bitcast.29, bf16[2,16,64]{2,1,0:T(8,128)(2,1)S(1)} %copy.42.rotary, bf16[576,256]{1,0:T(8,128)(2,1)S(1)} %pad_maximum_fusion.cache_ref), custom_call_target="tpu_custom_call" | custom-call | flops 20000000000 | tf_op jit(solution)/shard_map/attend_first/pallas_call | solution.py:318
  30.8 0.2 collective-permute-done.11.cache_ref
  31.0 0.4 %copy-done.1 = bf16[16,512,128]{2,1,0:T(8,128)(2,1)S(1)} copy-done((bf16[16,512,128]{2,1,0:T(8,128)(2,1)S(1)}, bf16[16,512,128]{2,1,0:T(8,128)(2,1)}, u32[]{:S(2)}) %copy-start.1) | copy-done | bytes 2097176
  31.3 2.0 %finish.1 = (bf16[2,16,128]{2,1,0:T(8,128)(2,1)}, f32[2,256]{1,0:T(2,128)}, bf16[2,1792]{1,0:T(2,128)(2,1)}) custom-call(s32[9]{0:T(128)S(1)} %stack.48.place, f32[2,256]{1,0:T(2,128)S(1)} %get-tuple-element.39.live_ref, bf16[2,16,512]{2,1,0:T(8,128)(2,1)S(1)} %bitcast.30, bf16[2,16,64]{2,1,0:T(8,128)(2,1)S(1)} %copy.42.rotary, ...), custom_call_target="tpu_custom_call" | custom-call | tf_op jit(solution)/shard_map/finish/pallas_call | solution.py:328
  (47 shorter events, 0.8 us)
Async XLA Ops:
  0.6 14.9 %copy-start = (bf16[1536,8,128]{2,1,0:T(8,128)(2,1)S(1)}, bf16[1536,8,128]{2,1,0:T(8,128)(2,1)}, u32[]{:S(2)}) copy-start(bf16[1536,8,128]{2,1,0:T(8,128)(2,1)} %param.26) | copy-start | bytes 9437188
  0.6 5.8 %collective-permute-start = (bf16[2,16,1792]{2,1,0:T(8,128)(2,1)}, bf16[2,16,1792]{2,1,0:T(8,128)(2,1)S(1)}, u32[]{:S(2)}, u32[]{:S(2)}) collective-permute-start(bf16[2,16,1792]{2,1,0:T(8,128)(2,1)} %bitcast.39), channel_id=1, source_target_pairs={{0,2},{2,0},{1,3},{3,1},{4,6},{6,4},{5,7},{7,5},{8,10},{10,8},{9,1... | collective-permute-start | bytes 344072 | tf_op jit(solution)/shard_map/ppermute | solution.py:225
  2.8 4.5 %slice-start.3 = ((s8[5505024]{0:T(1024)(128)(4,1)}), s8[4194304]{0:T(1024)(128)(4,1)S(1)}, s32[]{:S(2)}) async-start(s8[5505024]{0:T(1024)(128)(4,1)} %bitcast.33), calls=%async_computation.3 | async-start | bytes 8388608
  5.1 6.2 %collective-permute-start.3 = (bf16[576,128]{1,0:T(8,128)(2,1)S(1)}, bf16[576,128]{1,0:T(8,128)(2,1)S(1)}, u32[]{:S(2)}, u32[]{:S(2)}) collective-permute-start(bf16[576,128]{1,0:T(8,128)(2,1)S(1)} %get-tuple-element.52), channel_id=1, source_target_pairs={{0,4},{4,0},{8,12},{12,8},{1,5},{5,1},{9,13},{13,9},{2,6},{6,2},{1... | collective-permute-start | bytes 442376 | tf_op jit(solution)/shard_map/ppermute | solution.py:265
  6.4 1.3 %slice-start.4 = ((s8[5505024]{0:T(1024)(128)(4,1)}), s8[1310720]{0:T(1024)(128)(4,1)S(1)}, s32[]{:S(2)}) async-start(s8[5505024]{0:T(1024)(128)(4,1)} %bitcast.33), calls=%async_computation.4 | async-start | bytes 2621440
  6.4 13.5 %slice-start = ((s8[9437184]{0:T(1024)(128)(4,1)}), s8[4194304]{0:T(1024)(128)(4,1)S(1)}, s32[]{:S(2)}) async-start(s8[9437184]{0:T(1024)(128)(4,1)} %bitcast.31), calls=%async_computation | async-start | bytes 8388608
  6.4 13.5 %slice-start.1 = ((s8[9437184]{0:T(1024)(128)(4,1)}), s8[4194304]{0:T(1024)(128)(4,1)S(1)}, s32[]{:S(2)}) async-start(s8[9437184]{0:T(1024)(128)(4,1)} %bitcast.31), calls=%async_computation.1 | async-start | bytes 8388608
  6.4 13.5 %slice-start.2 = ((s8[9437184]{0:T(1024)(128)(4,1)}), s8[1048576]{0:T(1024)(128)(4,1)S(1)}, s32[]{:S(2)}) async-start(s8[9437184]{0:T(1024)(128)(4,1)} %bitcast.31), calls=%async_computation.2 | async-start | bytes 2097152
  7.3 8.1 %copy-start.4 = (f32[1536]{0:T(1024)S(1)}, f32[1536]{0:T(1024)}, u32[]{:S(2)}) copy-start(f32[1536]{0:T(1024)} %param.23) | copy-start | bytes 18436
  8.6 5.3 %collective-permute-start.1 = (f32[2,1792]{1,0:T(2,128)S(1)}, f32[2,1792]{1,0:T(2,128)S(1)}, u32[]{:S(2)}, u32[]{:S(2)}) collective-permute-start(f32[2,1792]{1,0:T(2,128)S(1)} %pad_maximum_fusion.1), channel_id=1, source_target_pairs={{0,12},{4,8},{8,4},{12,0},{1,13},{5,9},{9,5},{13,1},{2,14},{6,10},... | collective-permute-start | bytes 43016 | tf_op jit(solution)/shard_map/ppermute | solution.py:289
  11.3 3.7 %collective-permute-start.2 = (f32[2,1792]{1,0:T(2,128)S(1)}, f32[2,1792]{1,0:T(2,128)S(1)}, u32[]{:S(2)}, u32[]{:S(2)}) collective-permute-start(f32[2,1792]{1,0:T(2,128)S(1)} %pad_maximum_fusion.1), channel_id=1, source_target_pairs={{0,8},{4,12},{8,0},{12,4},{1,9},{5,13},{9,1},{13,5},{2,10},{6,14},... | collective-permute-start | bytes 43016 | tf_op jit(solution)/shard_map/ppermute | solution.py:289
  11.4 3.7 %collective-permute-start.4 = (f32[2,1792]{1,0:T(2,128)S(1)}, f32[2,1792]{1,0:T(2,128)S(1)}, u32[]{:S(2)}, u32[]{:S(2)}) collective-permute-start(f32[2,1792]{1,0:T(2,128)S(1)} %pad_maximum_fusion.1), channel_id=1, source_target_pairs={{0,4},{4,0},{8,12},{12,8},{1,5},{5,1},{9,13},{13,9},{2,6},{6,2},{1... | collective-permute-start | bytes 43016 | tf_op jit(solution)/shard_map/ppermute | solution.py:290
  12.3 10.7 %collective-permute-start.6 = (bf16[576,128]{1,0:T(8,128)(2,1)S(1)}, bf16[576,128]{1,0:T(8,128)(2,1)S(1)}, u32[]{:S(2)}, u32[]{:S(2)}) collective-permute-start(bf16[576,128]{1,0:T(8,128)(2,1)S(1)} %add.37), channel_id=1, source_target_pairs={{0,8},{4,12},{8,0},{12,4},{1,9},{5,13},{9,1},{13,5},{2,10},{6,14},... | collective-permute-start | bytes 442376 | tf_op jit(solution)/shard_map/ppermute | solution.py:287
  16.0 6.5 %copy-start.3 = (bf16[16,128,512]{2,1,0:T(8,128)(2,1)S(1)}, bf16[16,128,512]{2,1,0:T(8,128)(2,1)}, u32[]{:S(2)}) copy-start(bf16[16,128,512]{2,1,0:T(8,128)(2,1)} %param.25) | copy-start | bytes 6291460
  16.0 6.9 %collective-permute-start.5 = (bf16[8,2,128]{2,1,0:T(2,128)(2,1)S(1)}, bf16[8,2,128]{2,1,0:T(2,128)(2,1)S(1)}, u32[]{:S(2)}, u32[]{:S(2)}) collective-permute-start(bf16[8,2,128]{2,1,0:T(2,128)(2,1)S(1)} %fusion.5), channel_id=1, source_target_pairs={{0,1},{1,0},{2,3},{3,2},{4,5},{5,4},{6,7},{7,6},{8,9},{9,8},{10,11... | collective-permute-start | bytes 12296 | tf_op jit(solution)/shard_map/ppermute | solution.py:299
  23.0 5.5 %collective-permute-start.10 = (bf16[576,128]{1,0:T(8,128)(2,1)S(1)}, bf16[576,128]{1,0:T(8,128)(2,1)S(1)}, u32[]{:S(2)}, u32[]{:S(2)}) collective-permute-start(bf16[576,128]{1,0:T(8,128)(2,1)S(1)} %add.41), channel_id=1, source_target_pairs={{0,4},{4,0},{8,12},{12,8},{1,5},{5,1},{9,13},{13,9},{2,6},{6,2},{1... | collective-permute-start | bytes 442376 | tf_op jit(solution)/shard_map/ppermute | solution.py:315
  23.2 7.5 %collective-permute-start.7 = (bf16[2,8,2,128]{3,2,1,0:T(2,128)(2,1)S(1)}, bf16[2,8,2,128]{3,2,1,0:T(2,128)(2,1)S(1)}, u32[]{:S(2)}, u32[]{:S(2)}) collective-permute-start(bf16[2,8,2,128]{3,2,1,0:T(2,128)(2,1)S(1)} %pad_maximum_fusion.2.refs_0_), channel_id=1, source_target_pairs={{0,12},{4,8},{8,4},{12,0},{1,13},{5,9},{9,5},{13,1},{2,14},{6,10},... | collective-permute-start | bytes 24584 | tf_op jit(solution)/shard_map/ppermute | solution.py:308
  25.1 5.6 %collective-permute-start.8 = (bf16[2,8,2,128]{3,2,1,0:T(2,128)(2,1)S(1)}, bf16[2,8,2,128]{3,2,1,0:T(2,128)(2,1)S(1)}, u32[]{:S(2)}, u32[]{:S(2)}) collective-permute-start(bf16[2,8,2,128]{3,2,1,0:T(2,128)(2,1)S(1)} %pad_maximum_fusion.2.refs_0_), channel_id=1, source_target_pairs={{0,8},{4,12},{8,0},{12,4},{1,9},{5,13},{9,1},{13,5},{2,10},{6,14},... | collective-permute-start | bytes 24584 | tf_op jit(solution)/shard_map/ppermute | solution.py:308
  25.9 4.8 %collective-permute-start.9 = (bf16[2,8,2,128]{3,2,1,0:T(2,128)(2,1)S(1)}, bf16[2,8,2,128]{3,2,1,0:T(2,128)(2,1)S(1)}, u32[]{:S(2)}, u32[]{:S(2)}) collective-permute-start(bf16[2,8,2,128]{3,2,1,0:T(2,128)(2,1)S(1)} %pad_maximum_fusion.2.refs_0_), channel_id=1, source_target_pairs={{0,4},{4,0},{8,12},{12,8},{1,5},{5,1},{9,13},{13,9},{2,6},{6,2},{1... | collective-permute-start | bytes 24584 | tf_op jit(solution)/shard_map/ppermute | solution.py:308
  28.6 2.3 %collective-permute-start.11 = (bf16[576,256]{1,0:T(8,128)(2,1)S(1)}, bf16[576,256]{1,0:T(8,128)(2,1)S(1)}, u32[]{:S(2)}, u32[]{:S(2)}) collective-permute-start(bf16[576,256]{1,0:T(8,128)(2,1)S(1)} %pad_maximum_fusion.cache_ref), channel_id=1, source_target_pairs={{0,1},{1,0},{2,3},{3,2},{4,5},{5,4},{6,7},{7,6},{8,9},{9,8},{10,11... | collective-permute-start | bytes 884744 | tf_op jit(solution)/shard_map/ppermute | solution.py:317
  29.7 1.6 %copy-start.1 = (bf16[16,512,128]{2,1,0:T(8,128)(2,1)S(1)}, bf16[16,512,128]{2,1,0:T(8,128)(2,1)}, u32[]{:S(2)}) copy-start(bf16[16,512,128]{2,1,0:T(8,128)(2,1)} %value_ref.1) | copy-start | bytes 6291460
  29.7 1.6 %copy-start.2 = (bf16[2,256,128]{2,1,0:T(8,128)(2,1)S(1)}, bf16[2,256,128]{2,1,0:T(8,128)(2,1)}, u32[]{:S(2)}) copy-start(bf16[2,256,128]{2,1,0:T(8,128)(2,1)} %keys_ref.1) | copy-start | bytes 393220

commit v7 on v6

--- a/solution.py
+++ b/solution.py
@@ -286,7 +286,7 @@
     mine, near = lax.optimization_barrier((mine, part))
     crossed = [lax.ppermute(mine, "ctx", swapped(n_ctx, 2))]
 
-    parts = [part] + [lax.ppermute(part, "ctx", swapped(n_ctx, step)) for step in range(n_ctx - 1, 1, -1)]
+    parts = [part] + [lax.ppermute(part, "ctx", swapped(n_ctx, step)) for step in range(2, n_ctx)]
     parts.append(lax.ppermute(near, "ctx", swapped(n_ctx, 1)))
     total = functools.reduce(jnp.add, parts)
     scale = lax.rsqrt(total[:, qlora + LANES : qlora + LANES + 1] / D + epsilon)

time: 33.5 us -> 32.8 us (0.979)
  waiting for transfers between devices: 3.12 us -> 1.32 us
  starting transfers between devices: 17.4 us -> 18.5 us
    ppermute x1, starting transfers between devices: 1.54 us -> 2.92 us  [local(): crossed = [lax.ppermute(mine, 'ctx', swapped(n_ctx, 2))]]
    ppermute x1, waiting for transfers between devices: 1.74 us -> 0.39 us  [local(): other = lax.ppermute(mine, 'ctx', swapped(n_ctx, 1))]
    ppermute x1, starting transfers between devices: 3.93 us -> 2.9 us  [local(): index_other = lax.ppermute(index_local, 'hp', swapped(n_hp, 1))]
    ppermute x1, starting transfers between devices: 0.07 us -> 0.77 us  [local(): other = lax.ppermute(mine, 'ctx', swapped(n_ctx, 1))]
    ppermute x1, starting transfers between devices: 0.96 us -> 0.27 us  [local(): parts.append(lax.ppermute(near, 'ctx', swapped(n_ctx, 1)))]
    ppermute x1, starting transfers between devices: 1.13 us -> 1.8 us  [local(): theirs = lax.ppermute(mine, 'hp', swapped(n_hp, 1))]
    ppermute x2, waiting for transfers between devices: 1.15 us -> 0.7 us  [local(): lax.ppermute(part, 'ctx', swapped(n_ctx, step))]
where the time goes in v7:
time: 32.8 us; the launch traced here: 32.7 us
  starting transfers between devices  18.5 us (56%)
  Pallas kernels  6.12 us (19%)
  matrix products  4.23 us (13%)
  waiting for transfers between devices  1.32 us (4%)
  local copies, waits for them, and re-layouts  1.01 us (3%)
  between operations  0.82 us (2%)
  other arithmetic  0.68 us (2%)
    ppermute x3, starting transfers between devices, local(): lax.ppermute(index_pair, 'ctx', swapped(n_ctx, step))  3.61 us
    ppermute x1, starting transfers between devices, local(): crossed = [lax.ppermute(mine, 'ctx', swapped(n_ctx, 2))]  2.92 us
    ppermute x1, starting transfers between devices, local(): index_other = lax.ppermute(index_local, 'hp', swapped(n_hp, 1))  2.9 us
    ppermute x2, starting transfers between devices, local(): lax.ppermute(part, 'ctx', swapped(n_ctx, step))  2.79 us
    dot_general x1, matrix products, local(): jnp.einsum('rq,qnd->rnd', latent, query_up, preferred_element_type=f32)  2.53 us
    pallas_call x1, Pallas kernels, local(): pl.pallas_call(functools.partial(prepare, len(received)), out_shape=(half...  2.27 us
    ppermute x1, starting transfers between devices, local(): lax.ppermute(slots, 'dp', shifted(n_dp, step))  2.11 us
    pallas_call x1, Pallas kernels, local(): pl.pallas_call(functools.partial(finish, n_ctx), out_shape=(jax.ShapeDtyp...  2.04 us
  transfers between devices with their start and end apart: 12, of which 3 were waited for; matrix products, arithmetic and copies ran while one was open for 15% of the time, Pallas kernels for 12%

profile of v7, /device:TPU:1, one launch (start us, length us, event | category | flops | bytes accessed | tf_op | source)
XLA Modules:
  0.0 32.7 jit_solution(7314505737261289987)
XLA Ops:
  0.6 2.1 %collective-permute-start = (bf16[2,16,1792]{2,1,0:T(8,128)(2,1)}, bf16[2,16,1792]{2,1,0:T(8,128)(2,1)S(1)}, u32[]{:S(2)}, u32[]{:S(2)}) collective-permute-start(bf16[2,16,1792]{2,1,0:T(8,128)(2,1)} %bitcast.39), channel_id=1, source_target_pairs={{0,2},{2,0},{1,3},{3,1},{4,6},{6,4},{5,7},{7,5},{8,10},{10,8},{9,1... | collective-permute-start | bytes 344072 | tf_op jit(solution)/shard_map/ppermute | solution.py:225
  2.8 2.3 %prepare.1 = (bf16[576,128]{1,0:T(8,128)(2,1)S(1)}, bf16[576,128]{1,0:T(8,128)(2,1)S(1)}, f32[2,1792]{1,0:T(2,128)S(1)}, f32[1,2,16,128]{3,2,1,0:T(8,128)S(1)}, ...) custom-call(s32[9]{0:T(128)S(1)} %stack.48.place, ...), custom_call_target="tpu_custom_call" | custom-call | flops 10000000000 | tf_op jit(solution)/shard_map/prepare/pallas_call | solution.py:232
  5.1 1.3 %collective-permute-start.3 = (bf16[576,128]{1,0:T(8,128)(2,1)S(1)}, bf16[576,128]{1,0:T(8,128)(2,1)S(1)}, u32[]{:S(2)}, u32[]{:S(2)}) collective-permute-start(bf16[576,128]{1,0:T(8,128)(2,1)S(1)} %get-tuple-element.52), channel_id=1, source_target_pairs={{0,4},{4,0},{8,12},{12,8},{1,5},{5,1},{9,13},{13,9},{2,6},{6,2},{1... | collective-permute-start | bytes 442376 | tf_op jit(solution)/shard_map/ppermute | solution.py:265
  6.5 0.8 %combine.1 = (bf16[2,1792]{1,0:T(2,128)(2,1)S(1)}, bf16[2,1792]{1,0:T(2,128)(2,1)S(1)}, f32[2,256]{1,0:T(2,128)S(1)}) custom-call(s32[9]{0:T(128)S(1)} %stack.48.place, f32[2,1792]{1,0:T(2,128)S(1)} %get-tuple-element.44.base_ref, f32[1,2,16,128]{3,2,1,0:T(8,128)S(1)} %get-tuple-element.45.weight_ref, f32[1792]{0:T(1024)S(1)} %get-tuple-element.46.gain_ref, ...), custom_call_target="tpu_custom_call" | custom-call | flops 10000000000 | tf_op jit(solution)/shard_map/combine/pallas_call | solution.py:269
  7.3 0.5 %slice-done.4 = s8[1310720]{0:T(1024)(128)(4,1)S(1)} async-done(((s8[5505024]{0:T(1024)(128)(4,1)}), s8[1310720]{0:T(1024)(128)(4,1)S(1)}, s32[]{:S(2)}) %slice-start.4) | async-done | bytes 1310744
  7.8 0.8 %fusion.17 = f32[2,1536]{1,0:T(2,128)S(1)} fusion(bf16[2,1792]{1,0:T(2,128)(2,1)S(1)} %get-tuple-element.49, bf16[1792,1536]{1,0:T(8,128)(2,1)S(1)} %bitcast.34), kind=kOutput, calls=%fused_computation.26 | convolution fusion | flops 11010048 | bytes 5524480 | tf_op jit(solution)/shard_map/dot_general | solution.py:282
  8.6 2.4 %collective-permute-start.1 = (f32[2,1792]{1,0:T(2,128)S(1)}, f32[2,1792]{1,0:T(2,128)S(1)}, u32[]{:S(2)}, u32[]{:S(2)}) collective-permute-start(f32[2,1792]{1,0:T(2,128)S(1)} %pad_maximum_fusion.1), channel_id=1, source_target_pairs={{0,8},{4,12},{8,0},{12,4},{1,9},{5,13},{9,1},{13,5},{2,10},{6,14},... | collective-permute-start | bytes 43016 | tf_op jit(solution)/shard_map/ppermute | solution.py:289
  11.0 0.4 %collective-permute-start.2 = (f32[2,1792]{1,0:T(2,128)S(1)}, f32[2,1792]{1,0:T(2,128)S(1)}, u32[]{:S(2)}, u32[]{:S(2)}) collective-permute-start(f32[2,1792]{1,0:T(2,128)S(1)} %pad_maximum_fusion.1), channel_id=1, source_target_pairs={{0,12},{4,8},{8,4},{12,0},{1,13},{5,9},{9,5},{13,1},{2,14},{6,10},... | collective-permute-start | bytes 43016 | tf_op jit(solution)/shard_map/ppermute | solution.py:289
  11.4 0.3 collective-permute-start.4
  11.7 2.9 %collective-permute-start.6 = (bf16[576,128]{1,0:T(8,128)(2,1)S(1)}, bf16[576,128]{1,0:T(8,128)(2,1)S(1)}, u32[]{:S(2)}, u32[]{:S(2)}) collective-permute-start(bf16[576,128]{1,0:T(8,128)(2,1)S(1)} %add.37), channel_id=1, source_target_pairs={{0,8},{4,12},{8,0},{12,4},{1,9},{5,13},{9,1},{13,5},{2,10},{6,14},... | collective-permute-start | bytes 442376 | tf_op jit(solution)/shard_map/ppermute | solution.py:287
  14.6 0.7 %collective-permute-done.2 = f32[2,1792]{1,0:T(2,128)S(1)} collective-permute-done((f32[2,1792]{1,0:T(2,128)S(1)}, f32[2,1792]{1,0:T(2,128)S(1)}, u32[]{:S(2)}, u32[]{:S(2)}) %collective-permute-start.2) | collective-permute-done | bytes 14368 | tf_op jit(solution)/shard_map/ppermute | solution.py:289
  15.8 0.5 %fusion.5 = bf16[8,2,128]{2,1,0:T(2,128)(2,1)S(1)} fusion(bf16[1536,8,128]{2,1,0:T(8,128)(2,1)S(1)} %copy-done, bf16[2,1536]{1,0:T(2,128)(2,1)S(1)} %multiply_convert_fusion), kind=kOutput, calls=%fused_computation.3 | convolution fusion | flops 6293504 | bytes 3155968 | tf_op jit(solution)/shard_map/rq,qnd->nrd/dot_general | solution.py:298
  16.3 2.9 %collective-permute-start.5 = (bf16[8,2,128]{2,1,0:T(2,128)(2,1)S(1)}, bf16[8,2,128]{2,1,0:T(2,128)(2,1)S(1)}, u32[]{:S(2)}, u32[]{:S(2)}) collective-permute-start(bf16[8,2,128]{2,1,0:T(2,128)(2,1)S(1)} %fusion.5), channel_id=1, source_target_pairs={{0,1},{1,0},{2,3},{3,2},{4,5},{5,4},{6,7},{7,6},{8,9},{9,8},{10,11... | collective-permute-start | bytes 12296 | tf_op jit(solution)/shard_map/ppermute | solution.py:299
  19.3 2.5 %fusion.11 = bf16[2,16,192]{2,0,1:T(2,128)(2,1)S(1)} fusion(bf16[1536,16,192]{0,2,1:T(8,128)(2,1)S(1)} %bitcast.32, bf16[2,1536]{1,0:T(2,128)(2,1)S(1)} %multiply_convert_fusion), kind=kOutput, calls=%fused_computation.16 | convolution fusion | flops 18874368 | bytes 9455616 | tf_op jit(solution)/shard_map/rq,qnd->rnd/dot_general | solution.py:301
  21.8 0.4 %fusion.9 = bf16[16,2,512]{2,1,0:T(2,128)(2,1)S(1)} fusion(bf16[16,128,512]{2,1,0:T(8,128)(2,1)S(1)} %copy-done.3, bf16[2,16,128]{2,1,0:T(8,128)(2,1)S(1)} %copy.41), kind=kOutput, calls=%fused_computation.14 | convolution fusion | flops 4194304 | bytes 2138112 | tf_op jit(solution)/shard_map/rnk,nkc->rnc/dot_general | solution.py:302
  22.3 0.8 %collective-permute-start.10 = (bf16[576,128]{1,0:T(8,128)(2,1)S(1)}, bf16[576,128]{1,0:T(8,128)(2,1)S(1)}, u32[]{:S(2)}, u32[]{:S(2)}) collective-permute-start(bf16[576,128]{1,0:T(8,128)(2,1)S(1)} %add.41), channel_id=1, source_target_pairs={{0,4},{4,0},{8,12},{12,8},{1,5},{5,1},{9,13},{13,9},{2,6},{6,2},{1... | collective-permute-start | bytes 442376 | tf_op jit(solution)/shard_map/ppermute | solution.py:315
  23.2 1.2 %collective-permute-start.7 = (bf16[2,8,2,128]{3,2,1,0:T(2,128)(2,1)S(1)}, bf16[2,8,2,128]{3,2,1,0:T(2,128)(2,1)S(1)}, u32[]{:S(2)}, u32[]{:S(2)}) collective-permute-start(bf16[2,8,2,128]{3,2,1,0:T(2,128)(2,1)S(1)} %pad_maximum_fusion.2.refs_0_), channel_id=1, source_target_pairs={{0,12},{4,8},{8,4},{12,0},{1,13},{5,9},{9,5},{13,1},{2,14},{6,10},... | collective-permute-start | bytes 24584 | tf_op jit(solution)/shard_map/ppermute | solution.py:308
  24.4 0.8 %collective-permute-start.8 = (bf16[2,8,2,128]{3,2,1,0:T(2,128)(2,1)S(1)}, bf16[2,8,2,128]{3,2,1,0:T(2,128)(2,1)S(1)}, u32[]{:S(2)}, u32[]{:S(2)}) collective-permute-start(bf16[2,8,2,128]{3,2,1,0:T(2,128)(2,1)S(1)} %pad_maximum_fusion.2.refs_0_), channel_id=1, source_target_pairs={{0,8},{4,12},{8,0},{12,4},{1,9},{5,13},{9,1},{13,5},{2,10},{6,14},... | collective-permute-start | bytes 24584 | tf_op jit(solution)/shard_map/ppermute | solution.py:308
  25.2 1.6 %collective-permute-start.9 = (bf16[2,8,2,128]{3,2,1,0:T(2,128)(2,1)S(1)}, bf16[2,8,2,128]{3,2,1,0:T(2,128)(2,1)S(1)}, u32[]{:S(2)}, u32[]{:S(2)}) collective-permute-start(bf16[2,8,2,128]{3,2,1,0:T(2,128)(2,1)S(1)} %pad_maximum_fusion.2.refs_0_), channel_id=1, source_target_pairs={{0,4},{4,0},{8,12},{12,8},{1,5},{5,1},{9,13},{13,9},{2,6},{6,2},{1... | collective-permute-start | bytes 24584 | tf_op jit(solution)/shard_map/ppermute | solution.py:308
  26.8 0.4 %collective-permute-done.10 = bf16[576,128]{1,0:T(8,128)(2,1)S(1)} collective-permute-done((bf16[576,128]{1,0:T(8,128)(2,1)S(1)}, bf16[576,128]{1,0:T(8,128)(2,1)S(1)}, u32[]{:S(2)}, u32[]{:S(2)}) %collective-permute-start.10) | collective-permute-done | bytes 147488 | tf_op jit(solution)/shard_map/ppermute | solution.py:315
  27.2 1.8 %collective-permute-start.11 = (bf16[576,256]{1,0:T(8,128)(2,1)S(1)}, bf16[576,256]{1,0:T(8,128)(2,1)S(1)}, u32[]{:S(2)}, u32[]{:S(2)}) collective-permute-start(bf16[576,256]{1,0:T(8,128)(2,1)S(1)} %pad_maximum_fusion.cache_ref), channel_id=1, source_target_pairs={{0,1},{1,0},{2,3},{3,2},{4,5},{5,4},{6,7},{7,6},{8,9},{9,8},{10,11... | collective-permute-start | bytes 884744 | tf_op jit(solution)/shard_map/ppermute | solution.py:317
  29.0 1.0 %attend_first.1.first_ref = f32[16,512]{1,0:T(8,128)S(1)} custom-call(s32[9]{0:T(128)S(1)} %stack.48.place, f32[2,256]{1,0:T(2,128)S(1)} %get-tuple-element.39.live_ref, bf16[2,16,512]{2,1,0:T(8,128)(2,1)S(1)} %bitcast.29, bf16[2,16,64]{2,1,0:T(8,128)(2,1)S(1)} %copy.42.rotary, bf16[576,256]{1,0:T(8,128)(2,1)S(1)} %pad_maximum_fusion.cache_ref), custom_call_target="tpu_custom_call" | custom-call | flops 20000000000 | tf_op jit(solution)/shard_map/attend_first/pallas_call | solution.py:318
  30.2 0.4 %copy-done.1 = bf16[16,512,128]{2,1,0:T(8,128)(2,1)S(1)} copy-done((bf16[16,512,128]{2,1,0:T(8,128)(2,1)S(1)}, bf16[16,512,128]{2,1,0:T(8,128)(2,1)}, u32[]{:S(2)}) %copy-start.1) | copy-done | bytes 2097176
  30.6 2.0 %finish.1 = (bf16[2,16,128]{2,1,0:T(8,128)(2,1)}, f32[2,256]{1,0:T(2,128)}, bf16[2,1792]{1,0:T(2,128)(2,1)}) custom-call(s32[9]{0:T(128)S(1)} %stack.48.place, f32[2,256]{1,0:T(2,128)S(1)} %get-tuple-element.39.live_ref, bf16[2,16,512]{2,1,0:T(8,128)(2,1)S(1)} %bitcast.30, bf16[2,16,64]{2,1,0:T(8,128)(2,1)S(1)} %copy.42.rotary, ...), custom_call_target="tpu_custom_call" | custom-call | tf_op jit(solution)/shard_map/finish/pallas_call | solution.py:328
  (47 shorter events, 1.1 us)
Async XLA Ops:
  0.6 15.2 %copy-start = (bf16[1536,8,128]{2,1,0:T(8,128)(2,1)S(1)}, bf16[1536,8,128]{2,1,0:T(8,128)(2,1)}, u32[]{:S(2)}) copy-start(bf16[1536,8,128]{2,1,0:T(8,128)(2,1)} %param.26) | copy-start | bytes 9437188
  0.6 5.8 %collective-permute-start = (bf16[2,16,1792]{2,1,0:T(8,128)(2,1)}, bf16[2,16,1792]{2,1,0:T(8,128)(2,1)S(1)}, u32[]{:S(2)}, u32[]{:S(2)}) collective-permute-start(bf16[2,16,1792]{2,1,0:T(8,128)(2,1)} %bitcast.39), channel_id=1, source_target_pairs={{0,2},{2,0},{1,3},{3,1},{4,6},{6,4},{5,7},{7,5},{8,10},{10,8},{9,1... | collective-permute-start | bytes 344072 | tf_op jit(solution)/shard_map/ppermute | solution.py:225
  2.8 4.5 %slice-start.3 = ((s8[5505024]{0:T(1024)(128)(4,1)}), s8[4194304]{0:T(1024)(128)(4,1)S(1)}, s32[]{:S(2)}) async-start(s8[5505024]{0:T(1024)(128)(4,1)} %bitcast.33), calls=%async_computation.3 | async-start | bytes 8388608
  5.1 6.3 %collective-permute-start.3 = (bf16[576,128]{1,0:T(8,128)(2,1)S(1)}, bf16[576,128]{1,0:T(8,128)(2,1)S(1)}, u32[]{:S(2)}, u32[]{:S(2)}) collective-permute-start(bf16[576,128]{1,0:T(8,128)(2,1)S(1)} %get-tuple-element.52), channel_id=1, source_target_pairs={{0,4},{4,0},{8,12},{12,8},{1,5},{5,1},{9,13},{13,9},{2,6},{6,2},{1... | collective-permute-start | bytes 442376 | tf_op jit(solution)/shard_map/ppermute | solution.py:265
  6.4 1.3 %slice-start.4 = ((s8[5505024]{0:T(1024)(128)(4,1)}), s8[1310720]{0:T(1024)(128)(4,1)S(1)}, s32[]{:S(2)}) async-start(s8[5505024]{0:T(1024)(128)(4,1)} %bitcast.33), calls=%async_computation.4 | async-start | bytes 2621440
  6.4 12.8 %slice-start = ((s8[9437184]{0:T(1024)(128)(4,1)}), s8[4194304]{0:T(1024)(128)(4,1)S(1)}, s32[]{:S(2)}) async-start(s8[9437184]{0:T(1024)(128)(4,1)} %bitcast.31), calls=%async_computation | async-start | bytes 8388608
  6.4 12.8 %slice-start.1 = ((s8[9437184]{0:T(1024)(128)(4,1)}), s8[4194304]{0:T(1024)(128)(4,1)S(1)}, s32[]{:S(2)}) async-start(s8[9437184]{0:T(1024)(128)(4,1)} %bitcast.31), calls=%async_computation.1 | async-start | bytes 8388608
  6.4 12.8 %slice-start.2 = ((s8[9437184]{0:T(1024)(128)(4,1)}), s8[1048576]{0:T(1024)(128)(4,1)S(1)}, s32[]{:S(2)}) async-start(s8[9437184]{0:T(1024)(128)(4,1)} %bitcast.31), calls=%async_computation.2 | async-start | bytes 2097152
  7.3 8.4 %copy-start.4 = (f32[1536]{0:T(1024)S(1)}, f32[1536]{0:T(1024)}, u32[]{:S(2)}) copy-start(f32[1536]{0:T(1024)} %param.23) | copy-start | bytes 18436
  8.6 6.0 %collective-permute-start.1 = (f32[2,1792]{1,0:T(2,128)S(1)}, f32[2,1792]{1,0:T(2,128)S(1)}, u32[]{:S(2)}, u32[]{:S(2)}) collective-permute-start(f32[2,1792]{1,0:T(2,128)S(1)} %pad_maximum_fusion.1), channel_id=1, source_target_pairs={{0,8},{4,12},{8,0},{12,4},{1,9},{5,13},{9,1},{13,5},{2,10},{6,14},... | collective-permute-start | bytes 43016 | tf_op jit(solution)/shard_map/ppermute | solution.py:289
  11.0 4.4 %collective-permute-start.2 = (f32[2,1792]{1,0:T(2,128)S(1)}, f32[2,1792]{1,0:T(2,128)S(1)}, u32[]{:S(2)}, u32[]{:S(2)}) collective-permute-start(f32[2,1792]{1,0:T(2,128)S(1)} %pad_maximum_fusion.1), channel_id=1, source_target_pairs={{0,12},{4,8},{8,4},{12,0},{1,13},{5,9},{9,5},{13,1},{2,14},{6,10},... | collective-permute-start | bytes 43016 | tf_op jit(solution)/shard_map/ppermute | solution.py:289
  11.4 3.9 %collective-permute-start.4 = (f32[2,1792]{1,0:T(2,128)S(1)}, f32[2,1792]{1,0:T(2,128)S(1)}, u32[]{:S(2)}, u32[]{:S(2)}) collective-permute-start(f32[2,1792]{1,0:T(2,128)S(1)} %pad_maximum_fusion.1), channel_id=1, source_target_pairs={{0,4},{4,0},{8,12},{12,8},{1,5},{5,1},{9,13},{13,9},{2,6},{6,2},{1... | collective-permute-start | bytes 43016 | tf_op jit(solution)/shard_map/ppermute | solution.py:290
  11.7 10.6 %collective-permute-start.6 = (bf16[576,128]{1,0:T(8,128)(2,1)S(1)}, bf16[576,128]{1,0:T(8,128)(2,1)S(1)}, u32[]{:S(2)}, u32[]{:S(2)}) collective-permute-start(bf16[576,128]{1,0:T(8,128)(2,1)S(1)} %add.37), channel_id=1, source_target_pairs={{0,8},{4,12},{8,0},{12,4},{1,9},{5,13},{9,1},{13,5},{2,10},{6,14},... | collective-permute-start | bytes 442376 | tf_op jit(solution)/shard_map/ppermute | solution.py:287
  16.3 5.5 %copy-start.3 = (bf16[16,128,512]{2,1,0:T(8,128)(2,1)S(1)}, bf16[16,128,512]{2,1,0:T(8,128)(2,1)}, u32[]{:S(2)}) copy-start(bf16[16,128,512]{2,1,0:T(8,128)(2,1)} %param.25) | copy-start | bytes 6291460
  16.3 5.9 %collective-permute-start.5 = (bf16[8,2,128]{2,1,0:T(2,128)(2,1)S(1)}, bf16[8,2,128]{2,1,0:T(2,128)(2,1)S(1)}, u32[]{:S(2)}, u32[]{:S(2)}) collective-permute-start(bf16[8,2,128]{2,1,0:T(2,128)(2,1)S(1)} %fusion.5), channel_id=1, source_target_pairs={{0,1},{1,0},{2,3},{3,2},{4,5},{5,4},{6,7},{7,6},{8,9},{9,8},{10,11... | collective-permute-start | bytes 12296 | tf_op jit(solution)/shard_map/ppermute | solution.py:299
  22.3 4.9 %collective-permute-start.10 = (bf16[576,128]{1,0:T(8,128)(2,1)S(1)}, bf16[576,128]{1,0:T(8,128)(2,1)S(1)}, u32[]{:S(2)}, u32[]{:S(2)}) collective-permute-start(bf16[576,128]{1,0:T(8,128)(2,1)S(1)} %add.41), channel_id=1, source_target_pairs={{0,4},{4,0},{8,12},{12,8},{1,5},{5,1},{9,13},{13,9},{2,6},{6,2},{1... | collective-permute-start | bytes 442376 | tf_op jit(solution)/shard_map/ppermute | solution.py:315
  23.2 6.8 %collective-permute-start.7 = (bf16[2,8,2,128]{3,2,1,0:T(2,128)(2,1)S(1)}, bf16[2,8,2,128]{3,2,1,0:T(2,128)(2,1)S(1)}, u32[]{:S(2)}, u32[]{:S(2)}) collective-permute-start(bf16[2,8,2,128]{3,2,1,0:T(2,128)(2,1)S(1)} %pad_maximum_fusion.2.refs_0_), channel_id=1, source_target_pairs={{0,12},{4,8},{8,4},{12,0},{1,13},{5,9},{9,5},{13,1},{2,14},{6,10},... | collective-permute-start | bytes 24584 | tf_op jit(solution)/shard_map/ppermute | solution.py:308
  24.4 5.6 %collective-permute-start.8 = (bf16[2,8,2,128]{3,2,1,0:T(2,128)(2,1)S(1)}, bf16[2,8,2,128]{3,2,1,0:T(2,128)(2,1)S(1)}, u32[]{:S(2)}, u32[]{:S(2)}) collective-permute-start(bf16[2,8,2,128]{3,2,1,0:T(2,128)(2,1)S(1)} %pad_maximum_fusion.2.refs_0_), channel_id=1, source_target_pairs={{0,8},{4,12},{8,0},{12,4},{1,9},{5,13},{9,1},{13,5},{2,10},{6,14},... | collective-permute-start | bytes 24584 | tf_op jit(solution)/shard_map/ppermute | solution.py:308
  25.2 4.8 %collective-permute-start.9 = (bf16[2,8,2,128]{3,2,1,0:T(2,128)(2,1)S(1)}, bf16[2,8,2,128]{3,2,1,0:T(2,128)(2,1)S(1)}, u32[]{:S(2)}, u32[]{:S(2)}) collective-permute-start(bf16[2,8,2,128]{3,2,1,0:T(2,128)(2,1)S(1)} %pad_maximum_fusion.2.refs_0_), channel_id=1, source_target_pairs={{0,4},{4,0},{8,12},{12,8},{1,5},{5,1},{9,13},{13,9},{2,6},{6,2},{1... | collective-permute-start | bytes 24584 | tf_op jit(solution)/shard_map/ppermute | solution.py:308
  27.2 3.0 %collective-permute-start.11 = (bf16[576,256]{1,0:T(8,128)(2,1)S(1)}, bf16[576,256]{1,0:T(8,128)(2,1)S(1)}, u32[]{:S(2)}, u32[]{:S(2)}) collective-permute-start(bf16[576,256]{1,0:T(8,128)(2,1)S(1)} %pad_maximum_fusion.cache_ref), channel_id=1, source_target_pairs={{0,1},{1,0},{2,3},{3,2},{4,5},{5,4},{6,7},{7,6},{8,9},{9,8},{10,11... | collective-permute-start | bytes 884744 | tf_op jit(solution)/shard_map/ppermute | solution.py:317
  29.0 1.6 %copy-start.1 = (bf16[16,512,128]{2,1,0:T(8,128)(2,1)S(1)}, bf16[16,512,128]{2,1,0:T(8,128)(2,1)}, u32[]{:S(2)}) copy-start(bf16[16,512,128]{2,1,0:T(8,128)(2,1)} %value_ref.1) | copy-start | bytes 6291460
  29.0 1.6 %copy-start.2 = (bf16[2,256,128]{2,1,0:T(8,128)(2,1)S(1)}, bf16[2,256,128]{2,1,0:T(8,128)(2,1)}, u32[]{:S(2)}) copy-start(bf16[2,256,128]{2,1,0:T(8,128)(2,1)} %keys_ref.1) | copy-start | bytes 393220

commit v8 on v7

--- a/solution.py
+++ b/solution.py
@@ -149,10 +149,21 @@
     return merged / total
 
 
-def attend_first(place, live_ref, absorbed, rotary, cache_ref, out_ref):
+def attend_first(place, live_ref, projected_ref, absorb_ref, cache_ref, out_ref, absorbed, rotary):
+    heads, rows = projected_ref.shape[:2]
+    for n in range(heads):
+        projected = projected_ref[n]
+        query = jnp.dot(projected[:, :NOPE], absorb_ref[n], preferred_element_type=jnp.float32)
+        query = query.astype(jnp.bfloat16).astype(jnp.float32)
+        turn = projected[:, NOPE:].astype(jnp.float32)
+        for r in range(rows):
+            absorbed[r, n : n + 1, :] = query[r : r + 1]
+            rotary[r, n : n + 1, :] = turn[r : r + 1]
     row = place[0]
     live = live_ref[:1, :] > 0.0
-    out_ref[...] = attend_row(live, absorbed[pl.ds(row, 1)][0], rotary[pl.ds(row, 1)][0], cache_ref[...])
+    content = absorbed[pl.ds(row, 1)][0].astype(jnp.bfloat16)
+    turn = rotary[pl.ds(row, 1)][0].astype(jnp.bfloat16)
+    out_ref[...] = attend_row(live, content, turn, cache_ref[...])
 
 
 def finish(
@@ -183,7 +194,9 @@
     this = place[0]
     row = 1 - this
     live = live_ref[1:, :] > 0.0
-    second = attend_row(live, absorbed[pl.ds(row, 1)][0], rotary[pl.ds(row, 1)][0], cache_ref[...])
+    content = absorbed[pl.ds(row, 1)][0].astype(jnp.bfloat16)
+    turn = rotary[pl.ds(row, 1)][0].astype(jnp.bfloat16)
+    second = attend_row(live, content, turn, cache_ref[...])
     attended = jnp.concatenate([first_ref[...], second], axis=0).astype(jnp.bfloat16)
     head = lax.broadcasted_iota(jnp.int32, (2 * heads, value_ref.shape[2]), 0) % heads
     result = jnp.zeros(head.shape, jnp.float32)
@@ -299,10 +312,8 @@
     index_other = lax.ppermute(index_local, "hp", swapped(n_hp, 1))
     index_local, latent = lax.optimization_barrier((index_local, latent))
     projected = jnp.einsum("rq,qnd->rnd", latent, query_up, preferred_element_type=f32).astype(bf16)
-    absorbed = jnp.einsum("rnk,nkc->rnc", projected[:, :, :NOPE], key_absorb, preferred_element_type=f32).astype(bf16)
-    rotary = projected[:, :, NOPE:]
-    index_local, index_other, mine, crossed, absorbed, rotary = lax.optimization_barrier(
-        (index_local, index_other, mine, crossed, absorbed, rotary)
+    index_local, index_other, mine, crossed, projected = lax.optimization_barrier(
+        (index_local, index_other, mine, crossed, projected)
     )
     index_pair = jnp.stack([index_local, index_other])
     gathered = [index_pair] + [lax.ppermute(index_pair, "ctx", swapped(n_ctx, step)) for step in range(n_ctx - 1, 0, -1)]
@@ -315,15 +326,19 @@
     other = lax.ppermute(mine, "ctx", swapped(n_ctx, 1))
     mine = jnp.concatenate([mine, other], axis=1)
     theirs = lax.ppermute(mine, "hp", swapped(n_hp, 1))
-    attended = pl.pallas_call(
+    attended, absorbed, rotary = pl.pallas_call(
         attend_first,
-        out_shape=pltpu.VMEM((heads, KVLORA), f32),
+        out_shape=(
+            pltpu.VMEM((heads, KVLORA), f32),
+            pltpu.VMEM((rows, heads, KVLORA), f32),
+            pltpu.VMEM((rows, heads, ROPE), f32),
+        ),
         in_specs=[SMEM] + [VMEM] * 4,
-        out_specs=VMEM,
+        out_specs=(VMEM, VMEM, VMEM),
         compiler_params=limits(4),
         cost_estimate=pl.CostEstimate(flops=20000000000, bytes_accessed=0, transcendentals=0),
         name="attend_first",
-    )(place, *map(in_vmem, (live, absorbed, rotary, mine)))
+    )(place, *map(in_vmem, (live, jnp.transpose(projected, (1, 0, 2)), key_absorb, mine)))
     gathered, attended = lax.optimization_barrier((gathered, attended))
     attn_out, index_scores, hidden = pl.pallas_call(
         functools.partial(finish, n_ctx),

time: 32.8 us -> 35.6 us (1.085)
  waiting for transfers between devices: 1.32 us -> 2.72 us
  starting transfers between devices: 18.5 us -> 19.5 us
  Pallas kernels: 6.12 us -> 6.53 us
  matrix products: 4.23 us -> 3.85 us
    ppermute x1, starting transfers between devices: 2.9 us -> 5.58 us  [local(): index_other = lax.ppermute(index_local, 'hp', swapped(n_hp, 1))]
    ppermute x1, waiting for transfers between devices: 0.39 us -> 1.76 us  [local(): other = lax.ppermute(mine, 'ctx', swapped(n_ctx, 1))]
    ppermute x1, starting transfers between devices: 2.92 us -> 2.08 us  [local(): crossed = [lax.ppermute(mine, 'ctx', swapped(n_ctx, 2))]]
    ppermute x1, starting transfers between devices: 1.8 us -> 0.96 us  [local(): theirs = lax.ppermute(mine, 'hp', swapped(n_hp, 1))]
    ppermute x1, starting transfers between devices: 0.77 us -> 0.07 us  [local(): other = lax.ppermute(mine, 'ctx', swapped(n_ctx, 1))]
    ppermute x2, starting transfers between devices: 2.79 us -> 3.32 us  [local(): lax.ppermute(part, 'ctx', swapped(n_ctx, step))]
    pallas_call x1, Pallas kernels: 0.97 us -> 1.36 us  [local(): pl.pallas_call(attend_first, out_shape=(pltpu.VMEM((heads, KVLORA), f32),...]
    dot_general x1 -> x0, matrix products: 0.38 us -> none  [local(): jnp.einsum('rnk,nkc->rnc', projected[:, :, :NOPE], key_absorb, preferred_...]
  transfers between devices with their start and end apart: 12 -> 12, of which waited for: 3 -> 2; matrix products, arithmetic and copies ran while one was open for 15% -> 13% of each run, Pallas kernels for 12% -> 13%
where the time goes in v8:
time: 35.6 us; the launch traced here: 35.4 us
  starting transfers between devices  19.5 us (55%)
  Pallas kernels  6.53 us (18%)
  matrix products  3.85 us (11%)
  waiting for transfers between devices  2.72 us (8%)
  local copies, waits for them, and re-layouts  1.3 us (4%)
  between operations  0.79 us (2%)
  other arithmetic  0.68 us (2%)
    ppermute x1, starting transfers between devices, local(): index_other = lax.ppermute(index_local, 'hp', swapped(n_hp, 1))  5.58 us
    ppermute x3, starting transfers between devices, local(): lax.ppermute(index_pair, 'ctx', swapped(n_ctx, step))  3.68 us
    ppermute x2, starting transfers between devices, local(): lax.ppermute(part, 'ctx', swapped(n_ctx, step))  3.32 us
    dot_general x1, matrix products, local(): jnp.einsum('rq,qnd->rnd', latent, query_up, preferred_element_type=f32)  2.53 us
    pallas_call x1, Pallas kernels, local(): pl.pallas_call(functools.partial(prepare, len(received)), out_shape=(half...  2.3 us
    ppermute x1, starting transfers between devices, local(): lax.ppermute(slots, 'dp', shifted(n_dp, step))  2.11 us
    ppermute x1, starting transfers between devices, local(): crossed = [lax.ppermute(mine, 'ctx', swapped(n_ctx, 2))]  2.08 us
    pallas_call x1, Pallas kernels, local(): pl.pallas_call(functools.partial(finish, n_ctx), out_shape=(jax.ShapeDtyp...  2.04 us
  transfers between devices with their start and end apart: 12, of which 2 were waited for; matrix products, arithmetic and copies ran while one was open for 13% of the time, Pallas kernels for 13%

profile of v8, /device:TPU:1, one launch (start us, length us, event | category | flops | bytes accessed | tf_op | source)
XLA Modules:
  0.0 35.4 jit_solution(1647112233897647136)
XLA Ops:
  0.6 2.1 %collective-permute-start = (bf16[2,16,1792]{2,1,0:T(8,128)(2,1)}, bf16[2,16,1792]{2,1,0:T(8,128)(2,1)S(1)}, u32[]{:S(2)}, u32[]{:S(2)}) collective-permute-start(bf16[2,16,1792]{2,1,0:T(8,128)(2,1)} %bitcast.35), channel_id=1, source_target_pairs={{0,2},{2,0},{1,3},{3,1},{4,6},{6,4},{5,7},{7,5},{8,10},{10,8},{9,1... | collective-permute-start | bytes 344072 | tf_op jit(solution)/shard_map/ppermute | solution.py:238
  2.8 0.1 stack.48.place
  2.9 2.3 %prepare.1 = (bf16[576,128]{1,0:T(8,128)(2,1)S(1)}, bf16[576,128]{1,0:T(8,128)(2,1)S(1)}, f32[2,1792]{1,0:T(2,128)S(1)}, f32[1,2,16,128]{3,2,1,0:T(8,128)S(1)}, ...) custom-call(s32[9]{0:T(128)S(1)} %stack.48.place, ...), custom_call_target="tpu_custom_call" | custom-call | flops 10000000000 | tf_op jit(solution)/shard_map/prepare/pallas_call | solution.py:245
  5.2 1.3 %collective-permute-start.3 = (bf16[576,128]{1,0:T(8,128)(2,1)S(1)}, bf16[576,128]{1,0:T(8,128)(2,1)S(1)}, u32[]{:S(2)}, u32[]{:S(2)}) collective-permute-start(bf16[576,128]{1,0:T(8,128)(2,1)S(1)} %get-tuple-element.54), channel_id=1, source_target_pairs={{0,4},{4,0},{8,12},{12,8},{1,5},{5,1},{9,13},{13,9},{2,6},{6,2},{1... | collective-permute-start | bytes 442376 | tf_op jit(solution)/shard_map/ppermute | solution.py:278
  6.5 0.8 %combine.1 = (bf16[2,1792]{1,0:T(2,128)(2,1)S(1)}, bf16[2,1792]{1,0:T(2,128)(2,1)S(1)}, f32[2,256]{1,0:T(2,128)S(1)}) custom-call(s32[9]{0:T(128)S(1)} %stack.48.place, f32[2,1792]{1,0:T(2,128)S(1)} %get-tuple-element.46.base_ref, f32[1,2,16,128]{3,2,1,0:T(8,128)S(1)} %get-tuple-element.47.weight_ref, f32[1792]{0:T(1024)S(1)} %get-tuple-element.48.gain_ref, ...), custom_call_target="tpu_custom_call" | custom-call | flops 10000000000 | tf_op jit(solution)/shard_map/combine/pallas_call | solution.py:282
  7.3 1.0 %slice-done.4 = s8[1310720]{0:T(1024)(128)(4,1)S(1)} async-done(((s8[5505024]{0:T(1024)(128)(4,1)}), s8[1310720]{0:T(1024)(128)(4,1)S(1)}, s32[]{:S(2)}) %slice-start.4) | async-done | bytes 1310744
  8.3 0.8 %fusion.13 = f32[2,1536]{1,0:T(2,128)S(1)} fusion(bf16[2,1792]{1,0:T(2,128)(2,1)S(1)} %get-tuple-element.51, bf16[1792,1536]{1,0:T(8,128)(2,1)S(1)} %bitcast.30), kind=kOutput, calls=%fused_computation.21 | convolution fusion | flops 11010048 | bytes 5524480 | tf_op jit(solution)/shard_map/dot_general | solution.py:295
  9.2 3.3 %collective-permute-start.2 = (f32[2,1792]{1,0:T(2,128)S(1)}, f32[2,1792]{1,0:T(2,128)S(1)}, u32[]{:S(2)}, u32[]{:S(2)}) collective-permute-start(f32[2,1792]{1,0:T(2,128)S(1)} %pad_maximum_fusion.1), channel_id=1, source_target_pairs={{0,12},{4,8},{8,4},{12,0},{1,13},{5,9},{9,5},{13,1},{2,14},{6,10},... | collective-permute-start | bytes 43016 | tf_op jit(solution)/shard_map/ppermute | solution.py:302
  12.5 0.4 %collective-permute-start.4 = (f32[2,1792]{1,0:T(2,128)S(1)}, f32[2,1792]{1,0:T(2,128)S(1)}, u32[]{:S(2)}, u32[]{:S(2)}) collective-permute-start(f32[2,1792]{1,0:T(2,128)S(1)} %pad_maximum_fusion.1), channel_id=1, source_target_pairs={{0,4},{4,0},{8,12},{12,8},{1,5},{5,1},{9,13},{13,9},{2,6},{6,2},{1... | collective-permute-start | bytes 43016 | tf_op jit(solution)/shard_map/ppermute | solution.py:303
  13.0 2.1 %collective-permute-start.6 = (bf16[576,128]{1,0:T(8,128)(2,1)S(1)}, bf16[576,128]{1,0:T(8,128)(2,1)S(1)}, u32[]{:S(2)}, u32[]{:S(2)}) collective-permute-start(bf16[576,128]{1,0:T(8,128)(2,1)S(1)} %add.37), channel_id=1, source_target_pairs={{0,8},{4,12},{8,0},{12,4},{1,9},{5,13},{9,1},{13,5},{2,10},{6,14},... | collective-permute-start | bytes 442376 | tf_op jit(solution)/shard_map/ppermute | solution.py:300
  15.1 0.9 %collective-permute-done.1 = f32[2,1792]{1,0:T(2,128)S(1)} collective-permute-done((f32[2,1792]{1,0:T(2,128)S(1)}, f32[2,1792]{1,0:T(2,128)S(1)}, u32[]{:S(2)}, u32[]{:S(2)}) %collective-permute-start.1) | collective-permute-done | bytes 14368 | tf_op jit(solution)/shard_map/ppermute | solution.py:302
  16.0 0.2 multiply_reduce_fusion.1
  16.1 0.2 multiply_reduce_fusion
  16.4 0.1 multiply_convert_fusion
  16.5 0.5 %fusion.5 = bf16[8,2,128]{2,1,0:T(2,128)(2,1)S(1)} fusion(bf16[1536,8,128]{2,1,0:T(8,128)(2,1)S(1)} %copy-done, bf16[2,1536]{1,0:T(2,128)(2,1)S(1)} %multiply_convert_fusion), kind=kOutput, calls=%fused_computation.4 | convolution fusion | flops 6293504 | bytes 3155968 | tf_op jit(solution)/shard_map/rq,qnd->nrd/dot_general | solution.py:311
  17.0 5.6 %collective-permute-start.5 = (bf16[8,2,128]{2,1,0:T(2,128)(2,1)S(1)}, bf16[8,2,128]{2,1,0:T(2,128)(2,1)S(1)}, u32[]{:S(2)}, u32[]{:S(2)}) collective-permute-start(bf16[8,2,128]{2,1,0:T(2,128)(2,1)S(1)} %fusion.5), channel_id=1, source_target_pairs={{0,1},{1,0},{2,3},{3,2},{4,5},{5,4},{6,7},{7,6},{8,9},{9,8},{10,11... | collective-permute-start | bytes 12296 | tf_op jit(solution)/shard_map/ppermute | solution.py:312
  22.6 2.5 %convolution_convert_fusion = bf16[2,16,192]{2,0,1:T(2,128)(2,1)S(1)} fusion(bf16[1536,16,192]{0,2,1:T(8,128)(2,1)S(1)} %bitcast.28, bf16[2,1536]{1,0:T(2,128)(2,1)S(1)} %multiply_convert_fusion), kind=kOutput, calls=%fused_computation.2 | convolution fusion | flops 18880512 | bytes 9455616 | tf_op jit(solution)/shard_map/rq,qnd->rnd/dot_general | solution.py:314
  25.3 1.5 %collective-permute-start.10 = (bf16[2,8,2,128]{3,2,1,0:T(2,128)(2,1)S(1)}, bf16[2,8,2,128]{3,2,1,0:T(2,128)(2,1)S(1)}, u32[]{:S(2)}, u32[]{:S(2)}) collective-permute-start(bf16[2,8,2,128]{3,2,1,0:T(2,128)(2,1)S(1)} %pad_maximum_fusion.2.refs_0_), channel_id=1, source_target_pairs={{0,4},{4,0},{8,12},{12,8},{1,5},{5,1},{9,13},{13,9},{2,6},{6,2},{1... | collective-permute-start | bytes 24584 | tf_op jit(solution)/shard_map/ppermute | solution.py:319
  26.9 2.2 %collective-permute-start.8 = (bf16[2,8,2,128]{3,2,1,0:T(2,128)(2,1)S(1)}, bf16[2,8,2,128]{3,2,1,0:T(2,128)(2,1)S(1)}, u32[]{:S(2)}, u32[]{:S(2)}) collective-permute-start(bf16[2,8,2,128]{3,2,1,0:T(2,128)(2,1)S(1)} %pad_maximum_fusion.2.refs_0_), channel_id=1, source_target_pairs={{0,12},{4,8},{8,4},{12,0},{1,13},{5,9},{9,5},{13,1},{2,14},{6,10},... | collective-permute-start | bytes 24584 | tf_op jit(solution)/shard_map/ppermute | solution.py:319
  29.0 1.8 %collective-permute-done.7 = bf16[576,128]{1,0:T(8,128)(2,1)S(1)} collective-permute-done((bf16[576,128]{1,0:T(8,128)(2,1)S(1)}, bf16[576,128]{1,0:T(8,128)(2,1)S(1)}, u32[]{:S(2)}, u32[]{:S(2)}) %collective-permute-start.7) | collective-permute-done | bytes 147488 | tf_op jit(solution)/shard_map/ppermute | solution.py:326
  30.8 1.0 %collective-permute-start.11 = (bf16[576,256]{1,0:T(8,128)(2,1)S(1)}, bf16[576,256]{1,0:T(8,128)(2,1)S(1)}, u32[]{:S(2)}, u32[]{:S(2)}) collective-permute-start(bf16[576,256]{1,0:T(8,128)(2,1)S(1)} %pad_maximum_fusion.cache_ref), channel_id=1, source_target_pairs={{0,1},{1,0},{2,3},{3,2},{4,5},{5,4},{6,7},{7,6},{8,9},{9,8},{10,11... | collective-permute-start | bytes 884744 | tf_op jit(solution)/shard_map/ppermute | solution.py:328
  31.8 1.4 %attend_first.1 = (f32[16,512]{1,0:T(8,128)S(1)}, f32[2,16,512]{2,1,0:T(8,128)S(1)}, f32[2,16,64]{2,1,0:T(8,128)S(1)}) custom-call(s32[9]{0:T(128)S(1)} %stack.48.place, f32[2,256]{1,0:T(2,128)S(1)} %get-tuple-element.41.live_ref, bf16[16,2,192]{2,1,0:T(2,128)(2,1)S(1)} %bitcast.26, bf16[16,128,512]{2,1,0:T(8,128)(2,1)S(1)} %copy-done.3, ...), custom_call_target="tpu_custom_call" | custom-call | flops 20000000000 | tf_op jit(solution)/shard_map/attend_first/pallas_call | solution.py:329
  33.2 0.2 copy-done.1
  33.4 2.0 %finish.1 = (bf16[2,16,128]{2,1,0:T(8,128)(2,1)}, f32[2,256]{1,0:T(2,128)}, bf16[2,1792]{1,0:T(2,128)(2,1)}) custom-call(s32[9]{0:T(128)S(1)} %stack.48.place, f32[2,256]{1,0:T(2,128)S(1)} %get-tuple-element.41.live_ref, f32[2,16,512]{2,1,0:T(8,128)S(1)} %get-tuple-element.64.absorbed, f32[2,16,64]{2,1,0:T(8,128)S(1)} %get-tuple-element.65.rotary, ...), custom_call_target="tpu_custom_call" | custom-call | tf_op jit(solution)/shard_map/finish/pallas_call | solution.py:343
  (41 shorter events, 0.4 us)
Async XLA Ops:
  0.6 15.8 %copy-start = (bf16[1536,8,128]{2,1,0:T(8,128)(2,1)S(1)}, bf16[1536,8,128]{2,1,0:T(8,128)(2,1)}, u32[]{:S(2)}) copy-start(bf16[1536,8,128]{2,1,0:T(8,128)(2,1)} %param.26) | copy-start | bytes 9437188
  0.6 5.8 %collective-permute-start = (bf16[2,16,1792]{2,1,0:T(8,128)(2,1)}, bf16[2,16,1792]{2,1,0:T(8,128)(2,1)S(1)}, u32[]{:S(2)}, u32[]{:S(2)}) collective-permute-start(bf16[2,16,1792]{2,1,0:T(8,128)(2,1)} %bitcast.35), channel_id=1, source_target_pairs={{0,2},{2,0},{1,3},{3,1},{4,6},{6,4},{5,7},{7,5},{8,10},{10,8},{9,1... | collective-permute-start | bytes 344072 | tf_op jit(solution)/shard_map/ppermute | solution.py:238
  2.8 4.5 %slice-start.3 = ((s8[5505024]{0:T(1024)(128)(4,1)}), s8[4194304]{0:T(1024)(128)(4,1)S(1)}, s32[]{:S(2)}) async-start(s8[5505024]{0:T(1024)(128)(4,1)} %bitcast.29), calls=%async_computation.3 | async-start | bytes 8388608
  2.8 19.7 %slice-start = ((s8[9437184]{0:T(1024)(128)(4,1)}), s8[4194304]{0:T(1024)(128)(4,1)S(1)}, s32[]{:S(2)}) async-start(s8[9437184]{0:T(1024)(128)(4,1)} %bitcast.27), calls=%async_computation | async-start | bytes 8388608
  2.8 19.7 %slice-start.1 = ((s8[9437184]{0:T(1024)(128)(4,1)}), s8[4194304]{0:T(1024)(128)(4,1)S(1)}, s32[]{:S(2)}) async-start(s8[9437184]{0:T(1024)(128)(4,1)} %bitcast.27), calls=%async_computation.1 | async-start | bytes 8388608
  5.2 7.3 %collective-permute-start.3 = (bf16[576,128]{1,0:T(8,128)(2,1)S(1)}, bf16[576,128]{1,0:T(8,128)(2,1)S(1)}, u32[]{:S(2)}, u32[]{:S(2)}) collective-permute-start(bf16[576,128]{1,0:T(8,128)(2,1)S(1)} %get-tuple-element.54), channel_id=1, source_target_pairs={{0,4},{4,0},{8,12},{12,8},{1,5},{5,1},{9,13},{13,9},{2,6},{6,2},{1... | collective-permute-start | bytes 442376 | tf_op jit(solution)/shard_map/ppermute | solution.py:278
  6.5 1.9 %slice-start.4 = ((s8[5505024]{0:T(1024)(128)(4,1)}), s8[1310720]{0:T(1024)(128)(4,1)S(1)}, s32[]{:S(2)}) async-start(s8[5505024]{0:T(1024)(128)(4,1)} %bitcast.29), calls=%async_computation.4 | async-start | bytes 2621440
  6.5 16.1 %slice-start.2 = ((s8[9437184]{0:T(1024)(128)(4,1)}), s8[1048576]{0:T(1024)(128)(4,1)S(1)}, s32[]{:S(2)}) async-start(s8[9437184]{0:T(1024)(128)(4,1)} %bitcast.27), calls=%async_computation.2 | async-start | bytes 2097152
  7.3 9.0 %copy-start.4 = (f32[1536]{0:T(1024)S(1)}, f32[1536]{0:T(1024)}, u32[]{:S(2)}) copy-start(f32[1536]{0:T(1024)} %param.23) | copy-start | bytes 18436
  9.2 5.9 %collective-permute-start.2 = (f32[2,1792]{1,0:T(2,128)S(1)}, f32[2,1792]{1,0:T(2,128)S(1)}, u32[]{:S(2)}, u32[]{:S(2)}) collective-permute-start(f32[2,1792]{1,0:T(2,128)S(1)} %pad_maximum_fusion.1), channel_id=1, source_target_pairs={{0,12},{4,8},{8,4},{12,0},{1,13},{5,9},{9,5},{13,1},{2,14},{6,10},... | collective-permute-start | bytes 43016 | tf_op jit(solution)/shard_map/ppermute | solution.py:302
  12.5 3.5 %collective-permute-start.1 = (f32[2,1792]{1,0:T(2,128)S(1)}, f32[2,1792]{1,0:T(2,128)S(1)}, u32[]{:S(2)}, u32[]{:S(2)}) collective-permute-start(f32[2,1792]{1,0:T(2,128)S(1)} %pad_maximum_fusion.1), channel_id=1, source_target_pairs={{0,8},{4,12},{8,0},{12,4},{1,9},{5,13},{9,1},{13,5},{2,10},{6,14},... | collective-permute-start | bytes 43016 | tf_op jit(solution)/shard_map/ppermute | solution.py:302
  12.5 3.4 %collective-permute-start.4 = (f32[2,1792]{1,0:T(2,128)S(1)}, f32[2,1792]{1,0:T(2,128)S(1)}, u32[]{:S(2)}, u32[]{:S(2)}) collective-permute-start(f32[2,1792]{1,0:T(2,128)S(1)} %pad_maximum_fusion.1), channel_id=1, source_target_pairs={{0,4},{4,0},{8,12},{12,8},{1,5},{5,1},{9,13},{13,9},{2,6},{6,2},{1... | collective-permute-start | bytes 43016 | tf_op jit(solution)/shard_map/ppermute | solution.py:303
  13.0 12.1 %collective-permute-start.6 = (bf16[576,128]{1,0:T(8,128)(2,1)S(1)}, bf16[576,128]{1,0:T(8,128)(2,1)S(1)}, u32[]{:S(2)}, u32[]{:S(2)}) collective-permute-start(bf16[576,128]{1,0:T(8,128)(2,1)S(1)} %add.37), channel_id=1, source_target_pairs={{0,8},{4,12},{8,0},{12,4},{1,9},{5,13},{9,1},{13,5},{2,10},{6,14},... | collective-permute-start | bytes 442376 | tf_op jit(solution)/shard_map/ppermute | solution.py:300
  17.0 14.8 %copy-start.3 = (bf16[16,128,512]{2,1,0:T(8,128)(2,1)S(1)}, bf16[16,128,512]{2,1,0:T(8,128)(2,1)}, u32[]{:S(2)}) copy-start(bf16[16,128,512]{2,1,0:T(8,128)(2,1)} %absorb_ref.1) | copy-start | bytes 6291460
  17.0 8.1 %collective-permute-start.5 = (bf16[8,2,128]{2,1,0:T(2,128)(2,1)S(1)}, bf16[8,2,128]{2,1,0:T(2,128)(2,1)S(1)}, u32[]{:S(2)}, u32[]{:S(2)}) collective-permute-start(bf16[8,2,128]{2,1,0:T(2,128)(2,1)S(1)} %fusion.5), channel_id=1, source_target_pairs={{0,1},{1,0},{2,3},{3,2},{4,5},{5,4},{6,7},{7,6},{8,9},{9,8},{10,11... | collective-permute-start | bytes 12296 | tf_op jit(solution)/shard_map/ppermute | solution.py:312
  25.2 5.6 %collective-permute-start.7 = (bf16[576,128]{1,0:T(8,128)(2,1)S(1)}, bf16[576,128]{1,0:T(8,128)(2,1)S(1)}, u32[]{:S(2)}, u32[]{:S(2)}) collective-permute-start(bf16[576,128]{1,0:T(8,128)(2,1)S(1)} %add.41), channel_id=1, source_target_pairs={{0,4},{4,0},{8,12},{12,8},{1,5},{5,1},{9,13},{13,9},{2,6},{6,2},{1... | collective-permute-start | bytes 442376 | tf_op jit(solution)/shard_map/ppermute | solution.py:326
  25.3 7.8 %collective-permute-start.10 = (bf16[2,8,2,128]{3,2,1,0:T(2,128)(2,1)S(1)}, bf16[2,8,2,128]{3,2,1,0:T(2,128)(2,1)S(1)}, u32[]{:S(2)}, u32[]{:S(2)}) collective-permute-start(bf16[2,8,2,128]{3,2,1,0:T(2,128)(2,1)S(1)} %pad_maximum_fusion.2.refs_0_), channel_id=1, source_target_pairs={{0,4},{4,0},{8,12},{12,8},{1,5},{5,1},{9,13},{13,9},{2,6},{6,2},{1... | collective-permute-start | bytes 24584 | tf_op jit(solution)/shard_map/ppermute | solution.py:319
  26.9 6.3 %collective-permute-start.9 = (bf16[2,8,2,128]{3,2,1,0:T(2,128)(2,1)S(1)}, bf16[2,8,2,128]{3,2,1,0:T(2,128)(2,1)S(1)}, u32[]{:S(2)}, u32[]{:S(2)}) collective-permute-start(bf16[2,8,2,128]{3,2,1,0:T(2,128)(2,1)S(1)} %pad_maximum_fusion.2.refs_0_), channel_id=1, source_target_pairs={{0,8},{4,12},{8,0},{12,4},{1,9},{5,13},{9,1},{13,5},{2,10},{6,14},... | collective-permute-start | bytes 24584 | tf_op jit(solution)/shard_map/ppermute | solution.py:319
  26.9 6.3 %collective-permute-start.8 = (bf16[2,8,2,128]{3,2,1,0:T(2,128)(2,1)S(1)}, bf16[2,8,2,128]{3,2,1,0:T(2,128)(2,1)S(1)}, u32[]{:S(2)}, u32[]{:S(2)}) collective-permute-start(bf16[2,8,2,128]{3,2,1,0:T(2,128)(2,1)S(1)} %pad_maximum_fusion.2.refs_0_), channel_id=1, source_target_pairs={{0,12},{4,8},{8,4},{12,0},{1,13},{5,9},{9,5},{13,1},{2,14},{6,10},... | collective-permute-start | bytes 24584 | tf_op jit(solution)/shard_map/ppermute | solution.py:319
  30.8 2.4 %collective-permute-start.11 = (bf16[576,256]{1,0:T(8,128)(2,1)S(1)}, bf16[576,256]{1,0:T(8,128)(2,1)S(1)}, u32[]{:S(2)}, u32[]{:S(2)}) collective-permute-start(bf16[576,256]{1,0:T(8,128)(2,1)S(1)} %pad_maximum_fusion.cache_ref), channel_id=1, source_target_pairs={{0,1},{1,0},{2,3},{3,2},{4,5},{5,4},{6,7},{7,6},{8,9},{9,8},{10,11... | collective-permute-start | bytes 884744 | tf_op jit(solution)/shard_map/ppermute | solution.py:328
  31.8 1.6 %copy-start.1 = (bf16[16,512,128]{2,1,0:T(8,128)(2,1)S(1)}, bf16[16,512,128]{2,1,0:T(8,128)(2,1)}, u32[]{:S(2)}) copy-start(bf16[16,512,128]{2,1,0:T(8,128)(2,1)} %value_ref.1) | copy-start | bytes 6291460
  31.8 1.6 %copy-start.2 = (bf16[2,256,128]{2,1,0:T(8,128)(2,1)S(1)}, bf16[2,256,128]{2,1,0:T(8,128)(2,1)}, u32[]{:S(2)}) copy-start(bf16[2,256,128]{2,1,0:T(8,128)(2,1)} %keys_ref.1) | copy-start | bytes 393220
